TPU v7x, 32 devices: a whole 2x2x4 slice. The times are simulated.
32 devices in a mesh: dp: 4 (over z), mp: 8 (over y, x, core).
Axes of the slice: x: 2, y: 2, z: 4, core: 2. Of those that a mesh axis runs over, the one named last changes fastest.
Arguments:
- patches: bfloat16 [32, 256, 1152], P('dp'), may hold values from -6 to 6
- condition: bfloat16 [32, 1152], P('dp'), may hold values from -6 to 6
- lengths: int32 [32], P('dp'), may hold values from 144 to 192, as said below
- keep_order: int32 [32, 256], P('dp'), may hold values from 0 to 255, each once within a row
- cotangent: bfloat16 [32, 192, 1152], P('dp'), may hold values from -6 to 6
- projection_weight: bfloat16 [3, 1152, 1152], P(None, None, 'mp'), may hold values from -0.1875 to 0.1875
- query_value_bias: bfloat16 [2, 1152], P(None, 'mp'), may hold values from -3 to 3
- merge_weight: bfloat16 [1152, 1152], P('mp'), may hold values from -0.75 to 0.75
- merge_output_bias: bfloat16 [1152], replicated, may hold values from -3 to 3
- up_weight: bfloat16 [1152, 4608], P(None, 'mp'), may hold values from -0.1875 to 0.1875
- up_projection_bias: bfloat16 [4608], P('mp'), may hold values from -3 to 3
- down_weight: bfloat16 [4608, 1152], P('mp'), may hold values from -0.09375 to 0.09375
- down_projection_bias: bfloat16 [1152], replicated, may hold values from -3 to 3
- w_modulate: bfloat16 [1152, 6912], P(None, 'mp'), may hold values from -0.1875 to 0.1875
- bias_modulate: bfloat16 [6912], P('mp'), may hold values from -3 to 3
- bias_table: bfloat16 [16, 961], P('mp'), may hold values from -5 to 5
Outputs:
- block_out: bfloat16 [32, 192, 1152], P('dp')
- patch_grad: float32 [32, 256, 1152], P('dp')
- project_grad: float32 [3, 1152, 1152], P(None, None, 'mp')
- project_bias_grad: float32 [2, 1152], P(None, 'mp')
- merge_grad: float32 [1152, 1152], P('mp')
- merge_bias_grad: float32 [1152], replicated
- up_grad: float32 [1152, 4608], P(None, 'mp')
- up_bias_grad: float32 [4608], P('mp')
- down_grad: float32 [4608, 1152], P('mp')
- down_bias_grad: float32 [1152], replicated
- modulate_grad: float32 [1152, 6912], P(None, 'mp')
- modulate_bias_grad: float32 [6912], P('mp')
- table_grad: float32 [16, 961], P('mp')
Inputs may be any that keep to these rules, and one draw needn't show every extreme that they name: `lengths`: some sample keeps exactly 192 tokens. Each row holds every patch position once; slot j of sample b holds patch keep_order[b, j] when j < lengths[b].
All inputs are finite; a program needn't handle non-finite values.
Results may differ from a plain program's by a relative error of at most 0.02.
The roundings to bfloat16 on the way count: a program that leaves them out, or rounds other values in their place, can miss the bound.
Values may be sent and summed in bfloat16 or wider, within the bound.
A program may use at most 256 MiB of HBM per device.

v0:
```python
import math

import jax
import jax.numpy as jnp
from jax import lax
from jax.sharding import PartitionSpec as P

EXACT_PRECISION = lax.Precision.HIGHEST
EPSILON = 1e-06
MASKED = -1000000000.0


def layer_stats(values):
    centre = jnp.mean(values, axis=-1, keepdims=True)
    shifted = values - centre
    spread = jnp.mean(shifted * shifted, axis=-1, keepdims=True)
    inv_std = lax.rsqrt(spread + EPSILON)
    return (shifted * inv_std, inv_std)


def layer_back(gradient, normed, inv_std):
    mean_grad = jnp.mean(gradient, axis=-1, keepdims=True)
    mean_mix = jnp.mean(gradient * normed, axis=-1, keepdims=True)
    return inv_std * (gradient - mean_grad - normed * mean_mix)


def times_transposed(left_side, right_side):
    return lax.dot_general(
        left_side, right_side, (((1,), (1,)), ((), ())), preferred_element_type=jnp.float32
    )


def transposed_times(left_side, right_side):
    return lax.dot_general(
        left_side, right_side, (((0,), (0,)), ((), ())), preferred_element_type=jnp.float32
    )


def shift_onehot(grid_side):
    offsets = jnp.arange(grid_side, dtype=jnp.int32)
    targets = jnp.arange(2 * grid_side - 1, dtype=jnp.int32)
    return (
        offsets[:, None, None] - offsets[None, :, None] + grid_side - 1 == targets[None, None, :]
    ).astype(jnp.float32)


def body(
    patches,
    condition,
    lengths,
    keep_order,
    cotangent,
    projection_weight,
    query_value_bias,
    merge_weight,
    merge_output_bias,
    up_weight,
    up_projection_bias,
    down_weight,
    down_projection_bias,
    w_modulate,
    bias_modulate,
    bias_table,
):
    samples, patch_count, model_width = patches.shape
    keep_slots = cotangent.shape[1]
    grid_side = math.isqrt(patch_count)
    bucket_span = 2 * grid_side - 1
    heads_here = bias_table.shape[0]
    local_width = projection_weight.shape[2]
    head_size = local_width // heads_here
    row_count = samples * keep_slots
    factor = head_size ** (-0.5)
    head_shape = (samples, keep_slots, heads_here, head_size)
    slot_ids = jnp.arange(keep_slots, dtype=jnp.int32)
    live_slots = (slot_ids[None, :] < lengths[:, None]).astype(jnp.float32)
    live_rows = live_slots.reshape(row_count, 1)
    positions = keep_order[:, :keep_slots]
    row_picker = (
        positions[:, :, None] == jnp.arange(patch_count, dtype=jnp.int32)[None, None, :]
    ).astype(jnp.float32) * live_slots[:, :, None]
    signal = jax.nn.silu(condition.astype(jnp.float32)).astype(jnp.bfloat16)
    local_mod = jnp.dot(
        signal, w_modulate, preferred_element_type=jnp.float32
    ) + bias_modulate.astype(jnp.float32)
    modulation = lax.all_gather(local_mod, "mp", axis=1, tiled=True)
    row_mod = jnp.broadcast_to(
        modulation[:, None, :], (samples, keep_slots, modulation.shape[1])
    ).reshape(row_count, modulation.shape[1])
    shift_one, scale_one, gate_one, shift_two, scale_two, gate_two = [
        row_mod[:, column * model_width : (column + 1) * model_width] for column in range(6)
    ]
    taken = jnp.take_along_axis(patches, positions[:, :, None], axis=1).astype(jnp.float32)
    retained_rows = (taken * live_slots[:, :, None]).reshape(row_count, model_width)
    normed_one, inv_one = layer_stats(retained_rows)
    attention_entry = (normed_one * (1.0 + scale_one) + shift_one).astype(jnp.bfloat16)
    projected = jnp.einsum(
        "rd,cde->cre", attention_entry, projection_weight, preferred_element_type=jnp.float32
    )
    bias_float = query_value_bias.astype(jnp.float32)
    query_heads = (projected[0] + bias_float[0]).astype(jnp.bfloat16).reshape(head_shape)
    key_heads = projected[1].astype(jnp.bfloat16).reshape(head_shape)
    value_heads = (projected[2] + bias_float[1]).astype(jnp.bfloat16).reshape(head_shape)
    spread_table = shift_onehot(grid_side)
    table_grid = bias_table.astype(jnp.float32).reshape(heads_here, bucket_span, bucket_span)
    grid_bias = jnp.einsum(
        "rsa,cdb,hab->hrcsd", spread_table, spread_table, table_grid, precision=EXACT_PRECISION
    ).reshape(heads_here, patch_count, patch_count)
    left_bias = jnp.einsum("sql,hlm->shqm", row_picker, grid_bias, precision=EXACT_PRECISION)
    pair_bias = jnp.einsum("shqm,skm->shqk", left_bias, row_picker, precision=EXACT_PRECISION)

    def attention_scores(query_part, key_part):
        logits = (
            jnp.einsum("sqhe,skhe->shqk", query_part, key_part, preferred_element_type=jnp.float32)
            * factor
        )
        return jnp.where(live_slots[:, None, None, :] > 0.5, logits + pair_bias, MASKED)

    scores = attention_scores(query_heads, key_heads)
    row_max = jnp.max(scores, axis=-1, keepdims=True)
    exponent = jnp.exp(scores - row_max)
    row_sum = jnp.sum(exponent, axis=-1, keepdims=True)
    log_total = row_max + jnp.log(row_sum)
    attended_values = jnp.einsum(
        "shqk,skhe->sqhe",
        (exponent / row_sum).astype(jnp.bfloat16),
        value_heads,
        preferred_element_type=jnp.float32,
    )
    attended_values = attended_values.reshape(row_count, local_width).astype(jnp.bfloat16)
    attn_sum = lax.psum(
        jnp.dot(attended_values, merge_weight, preferred_element_type=jnp.float32).astype(
            jnp.bfloat16
        ),
        "mp",
    ).astype(jnp.float32)
    attention_result = attn_sum + merge_output_bias.astype(jnp.float32)
    hidden_one = retained_rows + gate_one * attention_result
    normed_two, inv_two = layer_stats(hidden_one)
    mlp_own = (normed_two * (1.0 + scale_two) + shift_two).astype(jnp.bfloat16)
    preactivation_hidden = jnp.dot(
        mlp_own, up_weight, preferred_element_type=jnp.float32
    ) + up_projection_bias.astype(jnp.float32)
    activated_hidden = jax.nn.gelu(preactivation_hidden, approximate=True).astype(jnp.bfloat16)
    mlp_sum = lax.psum(
        jnp.dot(activated_hidden, down_weight, preferred_element_type=jnp.float32).astype(
            jnp.bfloat16
        ),
        "mp",
    ).astype(jnp.float32)
    feedforward_result = mlp_sum + down_projection_bias.astype(jnp.float32)
    out_own = ((hidden_one + gate_two * feedforward_result) * live_rows).astype(jnp.bfloat16)
    block_out = out_own.reshape(samples, keep_slots, model_width)
    d_out = cotangent.reshape(row_count, model_width).astype(jnp.float32) * live_rows
    d_mlp = (gate_two * d_out).astype(jnp.bfloat16)
    down_grad = transposed_times(activated_hidden, d_mlp)
    down_bias_grad = jnp.sum(d_mlp.astype(jnp.float32), axis=0)
    d_act = times_transposed(d_mlp, down_weight)
    gelu_pull = jax.vjp(
        lambda pre_value: jax.nn.gelu(pre_value, approximate=True), preactivation_hidden
    )[1]
    d_pre = gelu_pull(d_act)[0].astype(jnp.bfloat16)
    up_grad = transposed_times(mlp_own, d_pre)
    up_bias_grad = jnp.sum(d_pre.astype(jnp.float32), axis=0)
    d_mlp_in = lax.psum(times_transposed(d_pre, up_weight).astype(jnp.bfloat16), "mp").astype(
        jnp.float32
    )
    d_hidden_one = d_out + layer_back(d_mlp_in * (1.0 + scale_two), normed_two, inv_two)
    d_attn_own = (gate_one * d_hidden_one).astype(jnp.bfloat16)
    merge_grad = transposed_times(attended_values, d_attn_own)
    merge_bias_grad = jnp.sum(d_attn_own.astype(jnp.float32), axis=0)
    d_attended = times_transposed(d_attn_own, merge_weight).astype(jnp.bfloat16).reshape(head_shape)
    probs_back = jnp.exp(attention_scores(query_heads, key_heads) - log_total)
    d_probs = jnp.einsum(
        "sqhe,skhe->shqk", d_attended, value_heads, preferred_element_type=jnp.float32
    )
    d_values = jnp.einsum(
        "shqk,sqhe->skhe",
        probs_back.astype(jnp.bfloat16),
        d_attended,
        preferred_element_type=jnp.float32,
    ).astype(jnp.bfloat16)
    d_scores = probs_back * (d_probs - jnp.sum(probs_back * d_probs, axis=-1, keepdims=True))
    d_logits = d_scores.astype(jnp.bfloat16)
    d_queries = (
        jnp.einsum("shqk,skhe->sqhe", d_logits, key_heads, preferred_element_type=jnp.float32)
        * factor
    ).astype(jnp.bfloat16)
    d_keys = (
        jnp.einsum("shqk,sqhe->skhe", d_logits, query_heads, preferred_element_type=jnp.float32)
        * factor
    ).astype(jnp.bfloat16)
    left_grad = jnp.einsum("sqm,shqk->shmk", row_picker, d_scores, precision=EXACT_PRECISION)
    grid_grad = jnp.einsum("shmk,skn->hmn", left_grad, row_picker, precision=EXACT_PRECISION)
    grid_grad = grid_grad.reshape(heads_here, grid_side, grid_side, grid_side, grid_side)
    table_grad = jnp.einsum(
        "rsa,cdb,hrcsd->hab", spread_table, spread_table, grid_grad, precision=EXACT_PRECISION
    ).reshape(heads_here, bucket_span * bucket_span)
    d_projected = jnp.stack(
        [
            d_queries.reshape(row_count, local_width),
            d_keys.reshape(row_count, local_width),
            d_values.reshape(row_count, local_width),
        ]
    )
    project_grad = jnp.einsum(
        "rd,cre->cde", attention_entry, d_projected, preferred_element_type=jnp.float32
    )
    project_bias_grad = jnp.stack(
        [
            jnp.sum(d_projected[0].astype(jnp.float32), axis=0),
            jnp.sum(d_projected[2].astype(jnp.float32), axis=0),
        ]
    )
    d_attn_in = lax.psum(
        jnp.einsum(
            "cre,cde->rd", d_projected, projection_weight, preferred_element_type=jnp.float32
        ).astype(jnp.bfloat16),
        "mp",
    ).astype(jnp.float32)
    d_kept_own = d_hidden_one + layer_back(d_attn_in * (1.0 + scale_one), normed_one, inv_one)
    mod_rows = jnp.concatenate(
        [
            d_attn_in,
            d_attn_in * normed_one,
            d_hidden_one * attention_result,
            d_mlp_in,
            d_mlp_in * normed_two,
            feedforward_result * d_out,
        ],
        axis=1,
    )
    d_modulation = jnp.sum(mod_rows.reshape(samples, keep_slots, mod_rows.shape[1]), axis=1)
    live_grad = d_kept_own.reshape(samples, keep_slots, model_width) * live_slots[:, :, None]
    sample_ids = jnp.arange(samples, dtype=jnp.int32)[:, None]
    patch_grad = (
        jnp.zeros((samples, patch_count, model_width), jnp.float32)
        .at[sample_ids, positions]
        .add(live_grad)
    )
    modulate_cols = w_modulate.shape[1]
    own_modulation = lax.dynamic_slice_in_dim(
        d_modulation, lax.axis_index("mp") * modulate_cols, modulate_cols, 1
    )
    modulate_grad = jnp.dot(signal.astype(jnp.float32).T, own_modulation, precision=EXACT_PRECISION)
    modulate_bias_grad = jnp.sum(own_modulation, axis=0)
    (
        project_grad,
        project_bias_grad,
        merge_grad,
        merge_bias_grad,
        up_grad,
        up_bias_grad,
        down_grad,
        down_bias_grad,
        modulate_grad,
        modulate_bias_grad,
        table_grad,
    ) = (
        lax.psum(project_grad.astype(jnp.bfloat16), "dp").astype(jnp.float32),
        lax.psum(project_bias_grad.astype(jnp.bfloat16), "dp").astype(jnp.float32),
        lax.psum(merge_grad.astype(jnp.bfloat16), "dp").astype(jnp.float32),
        lax.psum(merge_bias_grad.astype(jnp.bfloat16), "dp").astype(jnp.float32),
        lax.psum(up_grad.astype(jnp.bfloat16), "dp").astype(jnp.float32),
        lax.psum(up_bias_grad.astype(jnp.bfloat16), "dp").astype(jnp.float32),
        lax.psum(down_grad.astype(jnp.bfloat16), "dp").astype(jnp.float32),
        lax.psum(down_bias_grad.astype(jnp.bfloat16), "dp").astype(jnp.float32),
        lax.psum(modulate_grad.astype(jnp.bfloat16), "dp").astype(jnp.float32),
        lax.psum(modulate_bias_grad.astype(jnp.bfloat16), "dp").astype(jnp.float32),
        lax.psum(table_grad.astype(jnp.bfloat16), "dp").astype(jnp.float32),
    )
    return (
        block_out,
        patch_grad,
        project_grad,
        project_bias_grad,
        merge_grad,
        merge_bias_grad,
        up_grad,
        up_bias_grad,
        down_grad,
        down_bias_grad,
        modulate_grad,
        modulate_bias_grad,
        table_grad,
    )


def solution(mesh):
    placed = (
        P("dp", None, None),
        P("dp", None),
        P("dp"),
        P("dp", None),
        P("dp", None, None),
        P(None, None, "mp"),
        P(None, "mp"),
        P("mp", None),
        P(),
        P(None, "mp"),
        P("mp"),
        P("mp", None),
        P(),
        P(None, "mp"),
        P("mp"),
        P("mp", None),
    )
    return jax.shard_map(
        body,
        mesh=mesh,
        in_specs=placed,
        out_specs=(
            P("dp", None, None),
            P("dp", None, None),
            P(None, None, "mp"),
            P(None, "mp"),
            P("mp", None),
            P(),
            P(None, "mp"),
            P("mp"),
            P("mp", None),
            P(),
            P(None, "mp"),
            P("mp"),
            P("mp", None),
        ),
        check_vma=False,
    )
```

profile of v0, /device:TPU:0, one launch (start us, length us, event | category | flops | bytes accessed | tf_op | source)
XLA Modules:
  0.0 739.8 jit_solution(1977281370888989965)
XLA Ops:
  10.4 32.2 %gather_fusion = bf16[1536,1152]{1,0:T(8,128)(2,1)} fusion(bf16[8,256,1152]{2,1,0:T(8,128)(2,1)} %param.16, s32[1536]{0:T(1024)S(1)} %reshape.282), kind=kCustom, calls=%fused_computation | custom fusion | bytes 7090176 | tf_op jit(solution)/shard_map/jit(take_along_axis)/gather | solution.py:93
  48.2 10.8 %all-gather = f32[8,864,8]{1,2,0:T(8,128)S(1)} all-gather(f32[1,864,8]{1,2,0:T(8,128)S(1)} %fusion.58), channel_id=1, replica_groups=mesh['dp'=4,'mp'=8] {'mp'}, dimensions={0}, use_global_device_ids=true | all-gather | bytes 248832 | tf_op jit(solution)/shard_map/all_gather | solution.py:86
  59.3 14.1 %broadcast_in_dim.39 = f32[8,192,6912]{2,1,0:T(8,128)} broadcast(f32[8,6912]{1,0:T(8,128)S(1)} %bitcast.184), dimensions={0,2} | broadcast | bytes 42688512 | tf_op jit(solution)/shard_map/broadcast_in_dim | solution.py:87
  73.3 6.7 fusion.4
  121.4 62.6 %all-reduce.8.cloned.1.call-done = bf16[1536,1152]{1,0:T(8,128)(2,1)} async-done(((bf16[1536,1152]{1,0:T(8,128)(2,1)}), bf16[1536,1152]{1,0:T(8,128)(2,1)}) %all-reduce.8.cloned.1.call-update) | async-done | bytes 3538960 | tf_op jit(solution)/shard_map/psum | solution.py:131
  184.0 6.5 fusion.117
  193.5 6.1 fusion.3
  200.0 5.5 fusion.113
  211.7 7.6 %convolution_convert_fusion.2 = bf16[1536,1152]{1,0:T(8,128)(2,1)} fusion(bf16[576,1152]{1,0:T(8,128)(2,1)} %param.27, f32[1536,576]{0,1:T(8,128)} %get-tuple-element.52), kind=kOutput, calls=%fused_computation.12 | convolution fusion | flops 2048163840 | bytes 8404992 | tf_op jit(solution)/shard_map/dot_general | solution.py:146
  219.3 66.1 %all-reduce.10.cloned.1.call-done = bf16[1536,1152]{1,0:T(8,128)(2,1)} async-done(((bf16[1536,1152]{1,0:T(8,128)(2,1)}), bf16[1536,1152]{1,0:T(8,128)(2,1)}) %all-reduce.10.cloned.1.call-update) | async-done | bytes 3538960 | tf_op jit(solution)/shard_map/psum | solution.py:165
  285.4 7.5 %fusion.60 = (f32[1536]{0:T(1024)S(1)}, f32[1536]{0:T(1024)S(1)}) fusion(f32[1536,6912]{1,0:T(8,128)} %bitcast.168, bf16[1536,1152]{1,0:T(8,128)(2,1)} %all-reduce.10.cloned.1.call-done, f32[1536]{0:T(1024)S(1)} %add_rsqrt_fusion, f32[1536,1152]{1,0:T(8,128)} %copy-done.2, f32[1536]{0:T(1024)S(1)} %broadcast_multiply_fusion.5), kind=kLoop, calls=%fused_computation.111 | loop fusion | flops 14152704 | bytes 17719296 | tf_op jit(solution)/shard_map/reduce_sum | solution.py:22
  293.6 12.1 %fusion.115 = (bf16[1152]{0:T(1024)(128)(2,1)S(1)}, bf16[1536,1152]{1,0:T(8,128)(2,1)S(1)}, f32[1536,1152]{1,0:T(8,128)}) fusion(f32[1536,6912]{1,0:T(8,128)} %bitcast.169, f32[1536]{0:T(1024)S(1)} %broadcast_multiply_fusion.3, f32[1536,1152]{1,0:T(8,128)} %copy-done.2, f32[1536]{0:T(1024)S(1)} %broadcast_multiply_fusion.5, ...), kind=kLoop, calls=%fused_computation.184 | loop fusion | flops 26540928 | bytes 38961408 | tf_op jit(solution)/shard_map/reduce_sum | solution.py:171
  328.5 5.7 convolution_convert_fusion.4
  343.4 96.8 %all-reduce.12.cloned.1.call-done = (bf16[1536,1152]{1,0:T(8,128)(2,1)}, bf16[1536,1152]{1,0:T(8,128)(2,1)}) async-done(((bf16[1536,1152]{1,0:T(8,128)(2,1)}, bf16[1536,1152]{1,0:T(8,128)(2,1)}), (bf16[1536,1152]{1,0:T(8,128)(2,1)}, bf16[1536,1152]{1,0:T(8,128)(2,1)})) %all-reduce.12.cloned.1.call-update) | async-done | bytes 7077904 | tf_op jit(solution)/shard_map/psum | solution.py:145
  440.3 7.8 %fusion.61 = (f32[1536]{0:T(1024)S(1)}, f32[1536]{0:T(1024)S(1)}) fusion(f32[1536,6912]{1,0:T(8,128)} %bitcast.170, bf16[1536,1152]{1,0:T(8,128)(2,1)} %get-tuple-element.20, f32[1536]{0:T(1024)S(1)} %rsqrt.20, f32[1536]{0:T(1024)S(1)} %div.40, f32[1536]{0:T(1024)S(1)} %reshape.280, bf16[1536,1152]{1,0:T(8,128)(2,1)} %gather_fusion, ...), kind=kLoop, calls=%fused_computation.112 | loop fusion | flops 19461120 | bytes 14188032 | tf_op jit(solution)/shard_map/reduce_sum | solution.py:22
  451.7 17.0 %multiply_add_fusion = (f32[1536,1152]{1,0:T(8,128)}, bf16[1536,1152]{1,0:T(8,128)(2,1)}, f32[1536,6912]{1,0:T(8,128)}) fusion(f32[1536,1152]{1,0:T(8,128)} %get-tuple-element.38, f32[1536]{0:T(1024)S(1)} %broadcast_multiply_fusion.1, f32[1536]{0:T(1024)S(1)} %broadcast_multiply_fusion.2, f32[1536]{0:T(1024)S(1)} %rsqrt.20, f32[1536]{0:T(1024)S(1)} %div.40, ...), kind=kLoop, calls=%fused_computation.28 | loop fusion | flops 35389440 | bytes 56659968 | tf_op jit(solution)/shard_map/add | solution.py:221
  468.7 7.7 %multiply_dynamic-update-slice_fusion = f32[1536,6912]{1,0:T(8,128)} fusion(f32[1536,6912]{1,0:T(8,128)} %get-tuple-element.43, f32[1536,1152]{1,0:T(8,128)} %get-tuple-element.38, bf16[1536,1152]{1,0:T(8,128)(2,1)} %all-reduce.8.cloned.1.call-done, f32[1152]{0:T(1024)S(1)} %convert_element_type.251), kind=kLoop, calls=%fused_computation.27 | loop fusion | flops 5308416 | bytes 17699328
  489.4 14.7 %reduce_sum.177 = f32[8,6912]{1,0:T(8,128)S(1)} reduce(f32[8,192,6912]{2,1,0:T(8,128)} %bitcast.176, f32[]{:T(128)} %constant.29.clone.1), dimensions={1}, to_apply=%region_29.30 | reduce | flops 10561536 | bytes 42688516 | tf_op jit(solution)/shard_map/reduce_sum | solution.py:233
  513.1 5.6 fusion.53
  521.3 5.6 convolution_bitcast_fusion.2
  527.6 25.1 %all-reduce.1 = (bf16[2,144]{1,0:T(2,128)(2,1)S(1)}, bf16[1152]{0:T(1024)(128)(2,1)S(1)}, bf16[576]{0:T(1024)(128)(2,1)S(1)}, bf16[1152]{0:T(1024)(128)(2,1)S(1)...) all-reduce(bf16[2,144]{1,0:T(2,128)(2,1)S(1)} %pad_maximum_fusion, ...), channel_id=1, replica_groups=mesh['dp'=4,'mp'=8] {'dp'}, use_global_device_ids=true, to_apply=%region_19.20 | all-reduce | flops 5954 | bytes 23816 | tf_op jit(solution)/shard_map/psum | solution.py:261
  556.3 6.5 broadcast_multiply_fusion
  562.7 19.8 %scatter_custom_fusion = f32[2048,1152]{1,0:T(8,128)} fusion(s32[1536]{0:T(1024)S(1)} %reshape.288, f32[1536,1152]{1,0:T(8,128)} %bitcast.180, f32[]{:T(128)} %constant.29.clone.1), kind=kCustom, calls=%fused_computation.45 | custom fusion | flops 1769472 | bytes 9437696
  582.6 140.2 %all-reduce.14.cloned.1.call-done = (bf16[3,1152,144]{1,2,0:T(8,128)(2,1)}, bf16[144,1152]{1,0:T(8,128)(2,1)}, bf16[1152,576]{0,1:T(8,128)(2,1)}, bf16[576,1152]{1,0:T(8,128)(2,1)}, bf16[1152,864]{0,1:T(8,128)(2,1)}) async-done(((bf16[3,1152,144]{1,2,0:T(8,128)(2,1)}, bf16[144,1152]{1,0:T(8,128)(2,1)}, bf16[1152,576]{0,1:T(8,128)(2,1)}, bf16[576,1152]{1,0:T(8,128)(2,1)}, bf16[1152,864]{0,1:T(8,128)(2,1)}), ...) | async-done | bytes 5971984 | tf_op jit(solution)/shard_map/psum | solution.py:260
  (227 shorter events, 134.5 us)
Async XLA Ops:
  7.2 40.4 %copy-start = (bf16[1152,864]{0,1:T(8,128)(2,1)S(1)}, bf16[1152,864]{0,1:T(8,128)(2,1)}, u32[]{:S(2)}) copy-start(bf16[1152,864]{0,1:T(8,128)(2,1)} %param.29) | copy-start | bytes 5971972
  7.2 176.8 %all-reduce.8.cloned.1.call-start = ((), (), s32[]{:S(2)}) async-start(), calls=%async_computation | async-start | bytes 7077888 | tf_op jit(solution)/shard_map/psum | solution.py:131
  7.3 76.4 %copy-start.31 = (s32[16,16]{1,0:T(8,128)}, s32[16,16]{1,0:T(8,128)S(1)}, u32[]{:S(2)}) copy-start(s32[16,16]{1,0:T(8,128)S(1)} %subtract_add_fusion) | copy-start | bytes 3076
  9.4 84.5 %copy-start.35 = (s32[8,192]{1,0:T(8,128)}, s32[8,192]{1,0:T(8,128)S(1)}, u32[]{:S(2)}) copy-start(s32[8,192]{1,0:T(8,128)S(1)} %get-tuple-element.47) | copy-start | bytes 18436
  10.3 83.7 %copy-start.28 = (f32[8,192]{1,0:T(8,128)}, f32[8,192]{1,0:T(8,128)S(1)}, u32[]{:S(2)}) copy-start(f32[8,192]{1,0:T(8,128)S(1)} %get-tuple-element.49) | copy-start | bytes 18436
  59.3 14.1 %copy-start.4 = (bf16[1536,1152]{1,0:T(8,128)(2,1)S(1)}, bf16[1536,1152]{1,0:T(8,128)(2,1)}, u32[]{:S(2)}) copy-start(bf16[1536,1152]{1,0:T(8,128)(2,1)} %gather_fusion) | copy-start | bytes 10616836
  73.3 6.8 copy-start.51
  99.2 5.7 copy-start.17
  109.8 175.6 %all-reduce.10.cloned.1.call-start = ((), (), s32[]{:S(2)}) async-start(), calls=%async_computation.1 | async-start | bytes 7077888 | tf_op jit(solution)/shard_map/psum | solution.py:165
  109.9 7.2 copy-start.50
  193.5 6.1 copy-start.49
  193.5 6.5 copy-start.52
  211.4 228.9 %all-reduce.12.cloned.1.call-start = ((), (), s32[]{:S(2)}) async-start(), calls=%async_computation.2 | async-start | bytes 14155776 | tf_op jit(solution)/shard_map/psum | solution.py:145
  285.4 7.6 %copy-start.8 = (bf16[1536,1152]{1,0:T(8,128)(2,1)S(1)}, bf16[1536,1152]{1,0:T(8,128)(2,1)}, u32[]{:S(2)}) copy-start(bf16[1536,1152]{1,0:T(8,128)(2,1)} %all-reduce.10.cloned.1.call-done) | copy-start | bytes 10616836
  285.4 8.2 %copy-start.11 = (bf16[8,192,1152]{2,1,0:T(8,128)(2,1)S(1)}, bf16[8,192,1152]{2,1,0:T(8,128)(2,1)}, u32[]{:S(2)}) copy-start(bf16[8,192,1152]{2,1,0:T(8,128)(2,1)} %param.20) | copy-start | bytes 10616836
  327.0 395.7 %all-reduce.14.cloned.1.call-start = ((), (), s32[]{:S(2)}) async-start(), calls=%async_computation.3 | async-start | bytes 11943936 | tf_op jit(solution)/shard_map/psum | solution.py:260
  334.1 5.7 copy-start.34
  440.3 11.3 %slice-start = ((s8[7077888]{0:T(1024)(128)(4,1)}), s8[4194304]{0:T(1024)(128)(4,1)S(1)}, s32[]{:S(2)}) async-start(s8[7077888]{0:T(1024)(128)(4,1)} %bitcast.172), calls=%async_computation.4 | async-start | bytes 8388608
  440.3 7.9 %copy-start.13 = (bf16[1536,1152]{1,0:T(8,128)(2,1)S(1)}, bf16[1536,1152]{1,0:T(8,128)(2,1)}, u32[]{:S(2)}) copy-start(bf16[1536,1152]{1,0:T(8,128)(2,1)} %get-tuple-element.20) | copy-start | bytes 10616836
  440.3 11.3 %slice-start.1 = ((s8[7077888]{0:T(1024)(128)(4,1)}), s8[2883584]{0:T(1024)(128)(4,1)S(1)}, s32[]{:S(2)}) async-start(s8[7077888]{0:T(1024)(128)(4,1)} %bitcast.172), calls=%async_computation.5 | async-start | bytes 5767168
  468.6 7.7 %copy-start.9 = (bf16[1536,1152]{1,0:T(8,128)(2,1)S(1)}, bf16[1536,1152]{1,0:T(8,128)(2,1)}, u32[]{:S(2)}) copy-start(bf16[1536,1152]{1,0:T(8,128)(2,1)} %all-reduce.10.cloned.1.call-done) | copy-start | bytes 10616836
  489.4 14.7 %copy-start.39 = (bf16[8,1152]{1,0:T(8,128)(2,1)S(1)}, bf16[8,1152]{1,0:T(8,128)(2,1)}, u32[]{:S(2)}) copy-start(bf16[8,1152]{1,0:T(8,128)(2,1)} %param.17) | copy-start | bytes 55300
  513.1 8.3 %copy-start.32 = (s32[16,16]{1,0:T(8,128)S(1)}, s32[16,16]{1,0:T(8,128)}, u32[]{:S(2)}) copy-start(s32[16,16]{1,0:T(8,128)} %copy-done.31) | copy-start | bytes 3076
  521.3 6.3 copy-start.40
  (38 other events, 111.9 us)
Sparse Core Ops, SparseCore 0:
  109.9 74.0 all-reduce.7
  211.5 73.8 all-reduce.9
  327.1 113.1 all-reduce.11
  507.4 215.2 all-reduce.13
where the time goes:
time: 744 us; the launch traced here: 740 us
  waiting for transfers between devices  366 us (49%)
  other arithmetic  157 us (21%)
  matrix products  91.1 us (12%)
  local copies, waits for them, and re-layouts  74.6 us (10%)
  blocking collectives  35.8 us (5%)
  between operations  14.7 us (2%)
    psum x1, waiting for transfers between devices, body(): lax.psum(project_grad.astype(jnp.bfloat16), 'dp').astype(jnp.float32)  140 us
    psum x1, waiting for transfers between devices, body(): lax.psum(jnp.dot(activated_hidden, down_weight, preferred_element_type=jn...  96.8 us
    psum x1, waiting for transfers between devices, body(): lax.psum(times_transposed(d_pre, up_weight).astype(jnp.bfloat16), 'mp')  66.1 us
    psum x1, waiting for transfers between devices, body(): lax.psum(jnp.dot(attended_values, merge_weight, preferred_element_type=jn...  62.6 us
    unnamed x9, other arithmetic  38.7 us
    gather x3, local copies, waits for them, and re-layouts, body(): jnp.take_along_axis(patches, positions[:, :, None], axis=1)  32.3 us
    psum x1, blocking collectives, body(): lax.psum(project_bias_grad.astype(jnp.bfloat16), 'dp').astype(jnp.float32)  25.1 us
    add x1, other arithmetic, body(): d_hidden_one + layer_back(d_attn_in * (1.0 + scale_one), normed_one, inv_...  17 us
  transfers between devices with their start and end apart: 4, of which 4 were waited for; matrix products, arithmetic and copies ran while one was open for 11% of the time, Pallas kernels for 0%

commit v1 on v0

v1 whole, which is shorter than its diff:
```python
import functools
import math

import jax
import jax.numpy as jnp
import numpy as np
from jax import lax
from jax.experimental import pallas as pl
from jax.experimental.pallas import tpu as pltpu
from jax.sharding import PartitionSpec as P

MESH = pl.DeviceIdType.MESH
F32 = jnp.float32
BF16 = jnp.bfloat16
EPSILON = 1e-06
MASKED = -1000000000.0
GELU_C = math.sqrt(2.0 / math.pi)
GELU_A = 0.044715
VMEM = pl.BlockSpec(memory_space=pltpu.VMEM)
HEAD_PAD = 128


def dot(a, b, ca=1, cb=0):
    return lax.dot_general(a, b, (((ca,), (cb,)), ((), ())), preferred_element_type=F32)


def bit_of(value, k):
    return lax.rem(value // (1 << k), 2)


def flip(value, mask):
    out = value
    k = 0
    while (1 << k) <= mask:
        if mask & (1 << k):
            out = out + (1 << k) * (1 - 2 * bit_of(value, k))
        k += 1
    return out


def xor(a, b, bits):
    out = 0
    for k in range(bits):
        out = out + (1 << k) * lax.rem(bit_of(a, k) + bit_of(b, k), 2)
    return out


class Sizes:
    def __init__(self, mp, samples, slots, width):
        self.mp, self.samples, self.slots, self.width = mp, samples, slots, width
        self.bits = mp.bit_length() - 1
        self.rows = samples * slots
        self.block = self.rows // mp
        self.half = self.block // 2
        self.per = self.block and slots // self.block
        rest = [1 << k for k in range(1, self.bits)]
        self.orders = (rest, rest[::-1])
        self.sends = {}
        count = 0
        for h in range(2):
            live = list(range(0, mp, 2))
            for t, bit in enumerate(self.orders[h]):
                moved = [d for d in live if d & bit]
                live = [d for d in live if not d & bit]
                self.sends[h, t] = [(d, bit, count + i) for i, d in enumerate(moved)]
                count += len(moved)
        self.steps = len(rest)
        self.far = count
        self.near = mp // 2


def my_index():
    return lax.axis_index("dp"), lax.axis_index("mp")


def enter(sz):
    dp, me = my_index()
    barrier = pltpu.get_barrier_semaphore()
    for d in range(1, sz.mp):
        pl.semaphore_signal(barrier, inc=1, device_id=(dp, flip(me, d)), device_id_type=MESH)
    pl.semaphore_wait(barrier, sz.mp - 1)


def rows_of(ref, start, size):
    return ref.at[pl.ds(start, size)]


class Reduce:
    def __init__(self, sz, part, near_buf, far_buf, sems):
        self.sz, self.part, self.near_buf, self.far_buf = sz, part, near_buf, far_buf
        self.near_send, self.near_recv, self.far_send, self.far_recv = sems
        self.dp, self.me = my_index()

    def near_copy(self, pair):
        b = self.sz.block
        return pltpu.make_async_remote_copy(
            src_ref=rows_of(self.part, (2 * pair + 1) * b, b),
            dst_ref=rows_of(self.near_buf, pair * b, b),
            send_sem=self.near_send.at[pair],
            recv_sem=self.near_recv.at[pair],
            device_id=(self.dp, flip(self.me, 1)),
            device_id_type=MESH,
        )

    def far_copy(self, h, d, bit, i):
        b, hb = self.sz.block, self.sz.half
        return pltpu.make_async_remote_copy(
            src_ref=rows_of(self.part, d * b + h * hb, hb),
            dst_ref=rows_of(self.far_buf, i * hb, hb),
            send_sem=self.far_send.at[i],
            recv_sem=self.far_recv.at[i],
            device_id=(self.dp, flip(self.me, bit)),
            device_id_type=MESH,
        )

    def add(self, start, buf, at, size):
        a = self.part[pl.ds(start, size), :].astype(F32) + buf[pl.ds(at, size), :].astype(F32)
        self.part[pl.ds(start, size), :] = a.astype(BF16)

    def near_finish(self):
        b = self.sz.block

        def one(i, carry):
            pair = self.sz.near - 1 - i
            self.near_copy(pair).wait()
            self.add(2 * pair * b, self.near_buf, pair * b, b)
            return carry

        lax.fori_loop(0, self.sz.near, one, 0)

    def far_start(self, t):
        for h in range(2):
            for d, bit, i in self.sz.sends[h, t]:
                self.far_copy(h, d, bit, i).start()

    def far_finish(self, t):
        b, hb = self.sz.block, self.sz.half
        for h in range(2):
            for d, bit, i in self.sz.sends[h, t]:
                self.far_copy(h, d, bit, i).wait()
                if t < self.sz.steps - 1:
                    self.add((d - bit) * b + h * hb, self.far_buf, i * hb, hb)

    def own_sum(self):
        hb = self.sz.half
        out = []
        for h in range(2):
            (_, _, i), = self.sz.sends[h, self.sz.steps - 1]
            out.append(self.part[h * hb : (h + 1) * hb, :].astype(F32) + self.far_buf[i * hb : (i + 1) * hb, :].astype(F32))
        return jnp.concatenate(out, axis=0)


class Gather:
    def __init__(self, sz, out, sems):
        self.sz, self.out = sz, out
        self.near_send, self.near_recv, self.far_send, self.far_recv = sems
        self.dp, self.me = my_index()
        self.plan = {}
        count = 0
        for h in range(2):
            have = [0]
            for t, bit in enumerate(sz.orders[h][::-1]):
                self.plan[h, t] = [(d, bit, count + i) for i, d in enumerate(have)]
                count += len(have)
                have = have + [d | bit for d in have]

    def near_copy(self, d, h):
        b, hb = self.sz.block, self.sz.half
        return pltpu.make_async_remote_copy(
            src_ref=rows_of(self.out, d * b + h * hb, hb),
            dst_ref=rows_of(self.out, (d + 1) * b + h * hb, hb),
            send_sem=self.near_send.at[d + h],
            recv_sem=self.near_recv.at[d + h],
            device_id=(self.dp, flip(self.me, 1)),
            device_id_type=MESH,
        )

    def far_copy(self, h, d, bit, i):
        b, hb = self.sz.block, self.sz.half
        return pltpu.make_async_remote_copy(
            src_ref=rows_of(self.out, d * b + h * hb, hb),
            dst_ref=rows_of(self.out, (d + bit) * b + h * hb, hb),
            send_sem=self.far_send.at[i],
            recv_sem=self.far_recv.at[i],
            device_id=(self.dp, flip(self.me, bit)),
            device_id_type=MESH,
        )

    def start(self):
        for h in range(2):
            for d, bit, i in self.plan[h, 0]:
                self.far_copy(h, d, bit, i).start()
        for h in range(2):
            self.near_copy(0, h).start()

    def step(self, t):
        for h in range(2):
            for d, bit, i in self.plan[h, t]:
                self.far_copy(h, d, bit, i).wait()
            if t + 1 < self.sz.steps:
                for d, bit, i in self.plan[h, t + 1]:
                    self.far_copy(h, d, bit, i).start()
            for d, bit, i in self.plan[h, t]:
                self.near_copy(d + bit, h).start()

    def finish(self):
        for d in range(0, self.sz.mp, 2):
            for h in range(2):
                self.near_copy(d, h).wait()


def reduce_scratch(sz):
    return [
        pltpu.VMEM((sz.near * sz.block, sz.width), BF16),
        pltpu.VMEM((sz.far * sz.half, sz.width), BF16),
        pltpu.SemaphoreType.DMA((sz.near,)),
        pltpu.SemaphoreType.DMA((sz.near,)),
        pltpu.SemaphoreType.DMA((sz.far,)),
        pltpu.SemaphoreType.DMA((sz.far,)),
    ]


def gather_scratch(sz):
    return [
        pltpu.SemaphoreType.DMA((sz.mp,)),
        pltpu.SemaphoreType.DMA((sz.mp,)),
        pltpu.SemaphoreType.DMA((sz.far,)),
        pltpu.SemaphoreType.DMA((sz.far,)),
    ]


def sample_loops(sz, body, send, middle=None):
    if sz.per == 1:
        n = sz.samples // 2

        def odd(i, carry):
            body(2 * i + 1)
            send(i)
            return carry

        def even(i, carry):
            body(2 * (n - 1 - i))
            return carry

        lax.fori_loop(0, n, odd, 0)
        if middle is not None:
            middle()
        lax.fori_loop(0, n, even, 0)
    else:
        pairs = sz.per // 2

        def one(i, carry):
            slot = sz.samples - 1 - i
            body(slot)
            for p in range(pairs):
                send(slot * pairs + p)
            return carry

        lax.fori_loop(0, sz.samples, one, 0)
        if middle is not None:
            middle()


def layer_stats(values):
    centre = jnp.mean(values, axis=-1, keepdims=True)
    shifted = values - centre
    spread = jnp.mean(shifted * shifted, axis=-1, keepdims=True)
    inv_std = lax.rsqrt(spread + EPSILON)
    return shifted * inv_std, inv_std


def layer_back(gradient, normed, inv_std):
    mean_grad = jnp.mean(gradient, axis=-1, keepdims=True)
    mean_mix = jnp.mean(gradient * normed, axis=-1, keepdims=True)
    return inv_std * (gradient - mean_grad - normed * mean_mix)


def picker(pos_ref, s, slots, patches):
    ids = lax.broadcasted_iota(jnp.int32, (slots, patches), 1)
    return (pos_ref[s] == ids).astype(F32).astype(BF16)


def attention_forward_kernel(
    sz, heads, head_size, grid_side, cols,
    patches, condition, w_mod, b_mod, pos_col, pos_row, w_qkv, b_qkv, band, w_merge, b_merge,
    modv, attn_in, qkv, probs, att, normed1_own, inv1_own, res_own, hidden_own, normed2_own, inv2_own, mlp,
    mod_buf, mod_wide, normed, kept_own, bias_full, part, mod_send, mod_recv, *rest,
):
    dp, me = my_index()
    mine = me // sz.per
    sbits = sz.samples.bit_length() - 1
    D, n, L = sz.width, sz.slots, patches.shape[1]
    lanes = heads * HEAD_PAD
    red = Reduce(sz, part, rest[0], rest[1], rest[2:6])
    gat = Gather(sz, mlp, rest[6:10])
    wide = mod_buf.shape[2]

    cond = condition[...].astype(F32)
    signal = (cond / (1.0 + jnp.exp(-cond))).astype(BF16)
    local = dot(signal, w_mod[...]) + b_mod[...]
    mod_buf[me] = jnp.zeros((sz.samples, wide), F32)
    mod_buf[me, :, 0:cols] = local
    enter(sz)

    def mod_copy(d):
        return pltpu.make_async_remote_copy(
            src_ref=mod_buf.at[me],
            dst_ref=mod_buf.at[me],
            send_sem=mod_send.at[d],
            recv_sem=mod_recv.at[d],
            device_id=(dp, flip(me, d)),
            device_id_type=MESH,
        )

    def mod_arrival(d):
        return pltpu.make_async_remote_copy(
            src_ref=mod_buf.at[flip(me, d)],
            dst_ref=mod_buf.at[flip(me, d)],
            send_sem=mod_send.at[d],
            recv_sem=mod_recv.at[d],
            device_id=(dp, flip(me, d)),
            device_id_type=MESH,
        )

    for d in range(1, sz.mp):
        mod_copy(d).start()

    span = band.shape[2]
    for h in range(heads):
        strip = band[h]
        for r in range(grid_side):
            shift = (grid_side - 1 - r) * grid_side
            rolled = pltpu.roll(strip, (span - shift) % span, 1) if shift else strip
            bias_full[h, r * grid_side : (r + 1) * grid_side, :] = rolled[:, :L].astype(BF16)

    def norm_one(slot, carry):
        s = xor(mine, slot, sbits)
        kept = dot(picker(pos_col, s, n, L), patches[s])
        value, inv = layer_stats(kept)
        normed[pl.ds(slot * n, n), :] = value

        @pl.when(slot == 0)
        def _():
            kept_own[...] = kept[: sz.block]
            normed1_own[...] = value[: sz.block]
            inv1_own[...] = inv[: sz.block]

        return carry

    lax.fori_loop(0, sz.samples, norm_one, 0)

    for d in range(1, sz.mp):
        mod_copy(d).wait_send()
        mod_arrival(d).wait_recv()
    mod_wide[...] = jnp.zeros_like(mod_wide)
    for m in range(sz.mp):
        base = m * cols // 128 * 128
        phase = m * cols - base
        piece = mod_buf[m]
        if phase:
            piece = pltpu.roll(piece, phase, 1)
        mod_wide[:, base : base + wide] += piece
    modv[...] = mod_wide[:, : 6 * D]

    factor = head_size ** (-0.5)

    def body(slot):
        s = xor(mine, slot, sbits)
        at = pl.ds(slot * n, n)
        shift = modv[pl.ds(s, 1), 0:D]
        scale = modv[pl.ds(s, 1), D : 2 * D]
        entry = (normed[at, :] * (1.0 + scale) + shift).astype(BF16)
        attn_in[at, :] = entry
        proj = (dot(entry, w_qkv[...]) + b_qkv[...]).astype(BF16)
        qkv[at, :] = proj
        sel = picker(pos_col, s, n, L)
        live = pos_row[s] >= 0
        outs = []
        for h in range(heads):
            q = proj[:, h * HEAD_PAD : (h + 1) * HEAD_PAD]
            k = proj[:, lanes + h * HEAD_PAD : lanes + (h + 1) * HEAD_PAD]
            v = proj[:, 2 * lanes + h * HEAD_PAD : 2 * lanes + (h + 1) * HEAD_PAD]
            bias = dot(dot(sel, bias_full[h]).astype(BF16), sel, 1, 1)
            scores = jnp.where(live, dot(q, k, 1, 1) * factor + bias, MASKED)
            top = jnp.max(scores, axis=-1, keepdims=True)
            e = jnp.exp(scores - top)
            p = e / jnp.sum(e, axis=-1, keepdims=True)
            probs[slot, h] = p
            outs.append(dot(p.astype(BF16), v).astype(BF16))
        joined = jnp.concatenate(outs, axis=1) if heads > 1 else outs[0]
        att[at, :] = joined
        part[at, :] = dot(joined, w_merge[...]).astype(BF16)

    sample_loops(sz, body, lambda pair: red.near_copy(pair).start())
    red.near_finish()
    for t in range(sz.steps):
        red.far_start(t)
        red.far_finish(t)
    result = red.own_sum() + b_merge[...]
    res_own[...] = result
    gate = modv[pl.ds(mine, 1), 2 * D : 3 * D]
    hidden = kept_own[...] + gate * result
    hidden_own[...] = hidden
    value, inv = layer_stats(hidden)
    normed2_own[...] = value
    inv2_own[...] = inv
    shift = modv[pl.ds(mine, 1), 3 * D : 4 * D]
    scale = modv[pl.ds(mine, 1), 4 * D : 5 * D]
    mlp[: sz.block, :] = (value * (1.0 + scale) + shift).astype(BF16)
    gat.start()
    for t in range(sz.steps):
        gat.step(t)
    gat.finish()


def mlp_kernel(
    sz,
    mlp, w_up, b_up, w_down, b_down, cot, pos_col, modv, res_own, hidden_own, normed2_own, inv2_own,
    up_g, down_g, up_bg, down_bg, d_attn, out, dh_own, dmod,
    slope, act, d_mlp, d_pre, part_f, part_b, *rest,
):
    dp, me = my_index()
    mine = me // sz.per
    sbits = sz.samples.bit_length() - 1
    D, n = sz.width, sz.slots
    fwd = Reduce(sz, part_f, rest[0], rest[1], rest[2:6])
    bwd = Reduce(sz, part_b, rest[6], rest[7], rest[8:12])
    gat_d = Gather(sz, d_attn, rest[12:16])
    gat_o = Gather(sz, out, rest[16:20])
    enter(sz)

    def forward(slot):
        at = pl.ds(slot * n, n)
        v = dot(mlp[at, :], w_up[...]) + b_up[...]
        square = v * v
        t = jnp.tanh(GELU_C * (v + GELU_A * v * square))
        active = (0.5 * v * (1.0 + t)).astype(BF16)
        act[at, :] = active
        slope[at, :] = 0.5 * (1.0 + t) + 0.5 * v * (1.0 - t * t) * (GELU_C * (1.0 + 3.0 * GELU_A * square))
        part_f[at, :] = dot(active, w_down[...]).astype(BF16)

    sample_loops(sz, forward, lambda pair: fwd.near_copy(pair).start())
    fwd.near_finish()
    fwd.far_start(0)

    up_bg[...] = jnp.zeros_like(up_bg)
    down_bg[...] = jnp.zeros_like(down_bg)

    def d_out_of(s, rows):
        live = (pos_col[s, 0:rows, :] >= 0).astype(F32)
        return cot[pl.ds(s * n, rows), :].astype(F32) * live

    def backward(slot):
        s = xor(mine, slot, sbits)
        at = pl.ds(slot * n, n)
        gate = modv[pl.ds(s, 1), 5 * D : 6 * D]
        dm = (gate * d_out_of(s, n)).astype(BF16)
        d_mlp[at, :] = dm
        down_bg[...] += jnp.sum(dm.astype(F32), axis=0, keepdims=True)
        dpre = (dot(dm, w_down[...], 1, 1) * slope[at, :]).astype(BF16)
        d_pre[at, :] = dpre
        up_bg[...] += jnp.sum(dpre.astype(F32), axis=0, keepdims=True)
        part_b[at, :] = dot(dpre, w_up[...], 1, 1).astype(BF16)

    def middle():
        for t in range(sz.steps):
            fwd.far_finish(t)
            if t + 1 < sz.steps:
                fwd.far_start(t + 1)

    sample_loops(sz, backward, lambda pair: bwd.near_copy(pair).start(), middle)
    bwd.near_finish()
    bwd.far_start(0)

    tile = D // 3

    def down_tile(i, carry):
        cols = pl.ds(pl.multiple_of(i * tile, 128), tile)
        down_g[:, cols] = dot(act[...], d_mlp[:, cols], 0, 0).astype(BF16)
        return carry

    lax.fori_loop(0, 3, down_tile, 0)
    for t in range(sz.steps):
        bwd.far_finish(t)
        if t + 1 < sz.steps:
            bwd.far_start(t + 1)

    mrow = pl.ds(mine, 1)
    d_out = d_out_of(mine, sz.block)
    d_mlp_in = bwd.own_sum()
    normed2 = normed2_own[...]
    g = d_mlp_in * (1.0 + modv[mrow, 4 * D : 5 * D])
    dh = d_out + layer_back(g, normed2, inv2_own[...])
    dh_own[...] = dh
    d_attn[: sz.block, :] = (modv[mrow, 2 * D : 3 * D] * dh).astype(BF16)
    gat_d.start()

    dmod[0:2, :] = jnp.zeros((2, D), F32)
    dmod[2:3, :] = jnp.sum(dh * res_own[...], axis=0, keepdims=True)
    dmod[3:4, :] = jnp.sum(d_mlp_in, axis=0, keepdims=True)
    dmod[4:5, :] = jnp.sum(d_mlp_in * normed2, axis=0, keepdims=True)
    mlp_out = fwd.own_sum() + b_down[...]
    dmod[5:6, :] = jnp.sum(mlp_out * d_out, axis=0, keepdims=True)
    dmod[6:8, :] = jnp.zeros((2, D), F32)
    live = (pos_col[mine, 0 : sz.block, :] >= 0).astype(F32)
    out[: sz.block, :] = ((hidden_own[...] + modv[mrow, 5 * D : 6 * D] * mlp_out) * live).astype(BF16)

    def up_tile(i, carry):
        cols = pl.ds(pl.multiple_of(i * tile, 128), tile)
        up_g[cols, :] = dot(mlp[:, cols], d_pre[...], 0, 0).astype(BF16)
        return carry

    gat_d.step(0)
    gat_o.start()
    lax.fori_loop(0, 3, up_tile, 0)
    for t in range(1, sz.steps):
        gat_d.step(t)
    for t in range(sz.steps):
        gat_o.step(t)
    gat_d.finish()
    gat_o.finish()


def attention_backward_kernel(
    sz, heads, head_size, grid_side,
    d_attn, attn_in, qkv, probs, att, w_qkv, w_merge, pos_col, modv, normed1_own, inv1_own, dh_own, dmod_in,
    proj_g, proj_bg, merge_g, merge_bg, band_g, d_kept, dmod_all,
    dqkv, part, grid_g, dm_send, dm_recv, *rest,
):
    dp, me = my_index()
    mine = me // sz.per
    sbits = sz.samples.bit_length() - 1
    D, n, L = sz.width, sz.slots, grid_side * grid_side
    lanes = heads * HEAD_PAD
    red = Reduce(sz, part, rest[0], rest[1], rest[2:6])
    gat = Gather(sz, d_kept, rest[6:10])
    factor = head_size ** (-0.5)
    enter(sz)
    merge_bg[...] = jnp.zeros_like(merge_bg)
    proj_bg[...] = jnp.zeros_like(proj_bg)
    grid_g[...] = jnp.zeros_like(grid_g)

    def body(slot):
        s = xor(mine, slot, sbits)
        at = pl.ds(slot * n, n)
        da = d_attn[at, :]
        merge_bg[...] += jnp.sum(da.astype(F32), axis=0, keepdims=True)
        d_att = dot(da, w_merge[...], 1, 1).astype(BF16)
        sel = picker(pos_col, s, n, L)
        dq, dk, dv = [], [], []
        for h in range(heads):
            q = qkv[at, h * HEAD_PAD : (h + 1) * HEAD_PAD]
            k = qkv[at, lanes + h * HEAD_PAD : lanes + (h + 1) * HEAD_PAD]
            v = qkv[at, 2 * lanes + h * HEAD_PAD : 2 * lanes + (h + 1) * HEAD_PAD]
            dh = d_att[:, h * HEAD_PAD : (h + 1) * HEAD_PAD]
            p = probs[slot, h]
            dp_ = dot(dh, v, 1, 1)
            dv.append(dot(p.astype(BF16), dh, 0, 0).astype(BF16))
            ds = p * (dp_ - jnp.sum(p * dp_, axis=-1, keepdims=True))
            dl = ds.astype(BF16)
            dq.append((dot(dl, k) * factor).astype(BF16))
            dk.append((dot(dl, q, 0, 0) * factor).astype(BF16))
            grid_g[h] += dot(sel, dot(dl, sel).astype(BF16), 0, 0)
        joined = jnp.concatenate(dq + dk + dv, axis=1)
        dqkv[at, :] = joined
        proj_bg[...] += jnp.sum(joined.astype(F32), axis=0, keepdims=True)
        part[at, :] = dot(joined, w_qkv[...], 1, 1).astype(BF16)

    sample_loops(sz, body, lambda pair: red.near_copy(pair).start())
    red.near_finish()
    red.far_start(0)

    tile = D // 3

    def proj_tile(i, carry):
        cols = pl.ds(pl.multiple_of(i * tile, 128), tile)
        full = dot(attn_in[:, cols], dqkv[...], 0, 0)
        for c in range(3):
            piece = full[:, c * lanes : c * lanes + HEAD_PAD]
            if heads > 1:
                zero = jnp.zeros((tile, (heads - 1) * HEAD_PAD), F32)
                piece = jnp.concatenate([piece, zero], axis=1)
                for h in range(1, heads):
                    other = full[:, c * lanes + h * HEAD_PAD : c * lanes + (h + 1) * HEAD_PAD]
                    piece = piece + pltpu.roll(jnp.concatenate([other, zero], axis=1), h * head_size, 1)
            proj_g[c, cols, :] = piece[:, : heads * head_size].astype(BF16)
        return carry

    def merge_tile(i, carry):
        cols = pl.ds(pl.multiple_of(i * tile, 128), tile)
        merge_g[:, cols] = dot(att[...], d_attn[:, cols], 0, 0).astype(BF16)
        return carry

    lax.fori_loop(0, 3, proj_tile, 0)
    for t in range(sz.steps):
        red.far_finish(t)
        if t + 1 < sz.steps:
            red.far_start(t + 1)
    d_in = red.own_sum()
    normed1 = normed1_own[...]
    g = d_in * (1.0 + modv[pl.ds(mine, 1), D : 2 * D])
    d_kept[: sz.block, :] = (dh_own[...] + layer_back(g, normed1, inv1_own[...])).astype(BF16)
    gat.start()
    dmod_all[me] = dmod_in[...]
    dmod_all[me, 0:1, :] = jnp.sum(d_in, axis=0, keepdims=True)
    dmod_all[me, 1:2, :] = jnp.sum(d_in * normed1, axis=0, keepdims=True)

    def dm_copy(d, slot):
        return pltpu.make_async_remote_copy(
            src_ref=dmod_all.at[slot],
            dst_ref=dmod_all.at[slot],
            send_sem=dm_send.at[d],
            recv_sem=dm_recv.at[d],
            device_id=(dp, flip(me, d)),
            device_id_type=MESH,
        )

    for d in range(1, sz.mp):
        dm_copy(d, me).start()
    lax.fori_loop(0, 3, merge_tile, 0)
    span = band_g.shape[2]
    for h in range(heads):
        strip = jnp.zeros((grid_side, span), F32)
        for r in range(grid_side):
            shift = (grid_side - 1 - r) * grid_side
            piece = jnp.concatenate(
                [grid_g[h, r * grid_side : (r + 1) * grid_side, :], jnp.zeros((grid_side, span - L), F32)], axis=1
            )
            strip = strip + (pltpu.roll(piece, shift, 1) if shift else piece)
        band_g[h] = strip
    for t in range(sz.steps):
        gat.step(t)
    gat.finish()
    for d in range(1, sz.mp):
        dm_copy(d, me).wait_send()
        dm_copy(d, flip(me, d)).wait_recv()


def scatter_kernel(slot_ref, pos_row, d_kept, out_in, patch_grad, block_out):
    ids = lax.broadcasted_iota(jnp.int32, (patch_grad.shape[1], pos_row.shape[2]), 0)
    sel = (ids == pos_row[0]).astype(F32).astype(BF16)
    patch_grad[0] = dot(sel, d_kept[0])
    block_out[...] = out_in[...]


def body(
    patches,
    condition,
    lengths,
    keep_order,
    cotangent,
    projection_weight,
    query_value_bias,
    merge_weight,
    merge_output_bias,
    up_weight,
    up_projection_bias,
    down_weight,
    down_projection_bias,
    w_modulate,
    bias_modulate,
    bias_table,
):
    samples, L, D = patches.shape
    n = cotangent.shape[1]
    grid_side = math.isqrt(L)
    offsets = 2 * grid_side - 1
    heads = bias_table.shape[0]
    local = projection_weight.shape[2]
    hd = local // heads
    lanes = heads * HEAD_PAD
    F = up_weight.shape[1]
    cols = w_modulate.shape[1]
    mp = lax.axis_size("mp")
    me = lax.axis_index("mp")
    sz = Sizes(mp, samples, n, D)
    rows, block = sz.rows, sz.block

    ids = jnp.arange(n, dtype=jnp.int32)
    pos = jnp.where(ids[None, :] < lengths[:, None], keep_order[:, :n], -1)
    cot = cotangent
    if sz.per > 1:
        part_at = lax.rem(me, sz.per)
        order = (ids // block) ^ part_at
        order = order * block + ids % block
        pos = jnp.take(pos, order, axis=1)
        cot = jnp.take(cot, order, axis=1)
    pos_col = pos[:, :, None]
    pos_row = pos[:, None, :]
    cot = cot.reshape(rows, D)

    def pad_heads(a, axis):
        shape = a.shape[:axis] + (heads, hd) + a.shape[axis + 1 :]
        pads = [(0, 0)] * len(shape)
        pads[axis + 1] = (0, HEAD_PAD - hd)
        return jnp.pad(a.reshape(shape), pads).reshape(a.shape[:axis] + (lanes,) + a.shape[axis + 1 :])

    w_qkv = jnp.concatenate([pad_heads(projection_weight[c], 1) for c in range(3)], axis=1)
    qv = query_value_bias.astype(F32)
    b_qkv = jnp.concatenate([pad_heads(qv[0], 0), jnp.zeros((lanes,), F32), pad_heads(qv[1], 0)])[None, :]
    w_merge = pad_heads(merge_weight, 0)

    table = bias_table.reshape(heads, offsets, offsets)[:, ::-1, :]
    shift = np.arange(grid_side)
    pick = (np.arange(offsets)[:, None, None] == shift[None, :, None] - shift[None, None, :] + grid_side - 1)
    pick = jnp.asarray(pick, dtype=BF16)
    band = jnp.einsum("hab,bxy->hxay", table, pick, preferred_element_type=F32)
    band = band.reshape(heads, grid_side, offsets * grid_side)
    span = -(-offsets * grid_side // 128) * 128
    band = jnp.pad(band, ((0, 0), (0, 0), (0, span - offsets * grid_side)))

    def shape(*dims, dtype=F32):
        return jax.ShapeDtypeStruct(dims, dtype)

    def call(kernel, name, cid, outs, scratch, *args):
        return pl.pallas_call(
            kernel,
            out_shape=outs,
            in_specs=[VMEM] * len(args),
            out_specs=[VMEM] * len(outs),
            scratch_shapes=scratch,
            name=name,
            compiler_params=pltpu.CompilerParams(
                collective_id=cid, has_side_effects=True, vmem_limit_bytes=62 << 20
            ),
        )(*args)

    wide = -(-cols // 128) * 128 + 128
    modw = max(m * cols // 128 * 128 + wide for m in range(mp))
    act_like = functools.partial(shape, dtype=BF16)
    (modv, attn_in, qkv, probs, att, normed1, inv1, res, hidden, normed2, inv2, mlp) = call(
        functools.partial(attention_forward_kernel, sz, heads, hd, grid_side, cols),
        "attention_forward",
        0,
        [
            shape(samples, 6 * D),
            act_like(rows, D),
            act_like(rows, 3 * lanes),
            shape(samples, heads, n, n),
            act_like(rows, lanes),
            shape(block, D),
            shape(block, 1),
            shape(block, D),
            shape(block, D),
            shape(block, D),
            shape(block, 1),
            act_like(rows, D),
        ],
        [
            pltpu.VMEM((mp, samples, wide), F32),
            pltpu.VMEM((samples, modw), F32),
            pltpu.VMEM((rows, D), F32),
            pltpu.VMEM((block, D), F32),
            pltpu.VMEM((heads, L, L), BF16),
            pltpu.VMEM((rows, D), BF16),
            pltpu.SemaphoreType.DMA((mp,)),
            pltpu.SemaphoreType.DMA((mp,)),
        ]
        + reduce_scratch(sz)
        + gather_scratch(sz),
        patches,
        condition,
        w_modulate,
        bias_modulate.astype(F32)[None, :],
        pos_col,
        pos_row,
        w_qkv,
        b_qkv,
        band,
        w_merge,
        merge_output_bias.astype(F32)[None, :],
    )
    up_g, down_g, up_bg, down_bg, d_attn, out, dh, dmod = call(
        functools.partial(mlp_kernel, sz),
        "feed_forward",
        1,
        [
            act_like(D, F),
            act_like(F, D),
            shape(1, F),
            shape(1, D),
            act_like(rows, D),
            act_like(rows, D),
            shape(block, D),
            shape(8, D),
        ],
        [
            pltpu.VMEM((rows, F), F32),
            pltpu.VMEM((rows, F), BF16),
            pltpu.VMEM((rows, D), BF16),
            pltpu.VMEM((rows, F), BF16),
            pltpu.VMEM((rows, D), BF16),
            pltpu.VMEM((rows, D), BF16),
        ]
        + reduce_scratch(sz)
        + reduce_scratch(sz)
        + gather_scratch(sz)
        + gather_scratch(sz),
        mlp,
        up_weight,
        up_projection_bias.astype(F32)[None, :],
        down_weight,
        down_projection_bias.astype(F32)[None, :],
        cot,
        pos_col,
        modv,
        res,
        hidden,
        normed2,
        inv2,
    )
    up_grad, down_grad = lax.psum((up_g, down_g), "dp")
    proj_g, proj_bg, merge_g, merge_bg, band_g, d_kept, dmod_all = call(
        functools.partial(attention_backward_kernel, sz, heads, hd, grid_side),
        "attention_backward",
        2,
        [
            act_like(3, D, local),
            shape(1, 3 * lanes),
            act_like(lanes, D),
            shape(1, D),
            shape(heads, grid_side, span),
            act_like(rows, D),
            shape(mp, 8, D),
        ],
        [
            pltpu.VMEM((rows, 3 * lanes), BF16),
            pltpu.VMEM((rows, D), BF16),
            pltpu.VMEM((heads, L, L), F32),
            pltpu.SemaphoreType.DMA((mp,)),
            pltpu.SemaphoreType.DMA((mp,)),
        ]
        + reduce_scratch(sz)
        + gather_scratch(sz),
        d_attn,
        attn_in,
        qkv,
        probs,
        att,
        w_qkv,
        w_merge,
        pos_col,
        modv,
        normed1,
        inv1,
        dh,
        dmod,
    )
    project_grad, merge_grad = lax.psum(
        (proj_g, merge_g.reshape(heads, HEAD_PAD, D)[:, :hd].reshape(local, D)), "dp"
    )

    slot_of = jnp.arange(samples, dtype=jnp.int32) ^ (me // sz.per)
    own_cols = lax.dynamic_slice_in_dim(
        dmod_all[:, :6].reshape(samples, sz.per, 6 * D).sum(axis=1), me * cols, cols, 1
    )
    cond = condition.astype(F32)
    signal = jax.nn.silu(cond).astype(BF16).astype(F32)
    bias_parts = proj_bg.reshape(3, heads, HEAD_PAD)[:, :, :hd].reshape(3, local)
    smalls = [signal, own_cols, bias_parts, merge_bg, up_bg, down_bg, band_g]
    flat = jnp.concatenate([a.reshape(-1) for a in smalls])
    everyone = lax.all_gather(flat, "dp")
    got, at = [], 0
    for a in smalls:
        got.append(everyone[:, at : at + a.size].reshape((everyone.shape[0],) + a.shape))
        at += a.size
    signal_all = got[0].reshape(-1, D)
    dmod_cols = got[1].reshape(-1, cols)
    modulate_grad = jnp.dot(signal_all.T, dmod_cols, precision=lax.Precision.HIGHEST)
    modulate_bias_grad = jnp.sum(dmod_cols, axis=0)
    proj_bias, merge_bias, up_bias, down_bias, band_sum = [jnp.sum(a, axis=0) for a in got[2:]]
    band_sum = band_sum[:, :, : offsets * grid_side].reshape(heads, grid_side, offsets, grid_side)
    table_grad = jnp.einsum(
        "hxay,bxy->hab", band_sum, pick.astype(F32), precision=lax.Precision.HIGHEST
    )[:, ::-1, :].reshape(heads, offsets * offsets)

    by_sample = lambda s, slot_ref: (slot_ref[s], 0, 0)
    straight = lambda s, slot_ref: (s, 0, 0)
    patch_grad, block_out = pl.pallas_call(
        scatter_kernel,
        out_shape=[shape(samples, L, D), act_like(samples, n, D)],
        grid_spec=pltpu.PrefetchScalarGridSpec(
            num_scalar_prefetch=1,
            grid=(samples,),
            in_specs=[
                pl.BlockSpec((1, 1, n), straight),
                pl.BlockSpec((1, n, D), by_sample),
                pl.BlockSpec((1, n, D), by_sample),
            ],
            out_specs=[pl.BlockSpec((1, L, D), straight), pl.BlockSpec((1, n, D), straight)],
        ),
        name="scatter",
    )(slot_of, pos_row, d_kept.reshape(samples, n, D), out.reshape(samples, n, D))
    if sz.per > 1:
        block_out = jnp.take(block_out, order, axis=1)
    return (
        block_out,
        patch_grad,
        project_grad.astype(F32),
        proj_bias[jnp.array([0, 2])],
        merge_grad.astype(F32),
        merge_bias[0],
        up_grad.astype(F32),
        up_bias[0],
        down_grad.astype(F32),
        down_bias[0],
        modulate_grad,
        modulate_bias_grad,
        table_grad,
    )


def solution(mesh):
    placed = (
        P("dp", None, None),
        P("dp", None),
        P("dp"),
        P("dp", None),
        P("dp", None, None),
        P(None, None, "mp"),
        P(None, "mp"),
        P("mp", None),
        P(),
        P(None, "mp"),
        P("mp"),
        P("mp", None),
        P(),
        P(None, "mp"),
        P("mp"),
        P("mp", None),
    )
    return jax.shard_map(
        body,
        mesh=mesh,
        in_specs=placed,
        out_specs=(
            P("dp", None, None),
            P("dp", None, None),
            P(None, None, "mp"),
            P(None, "mp"),
            P("mp", None),
            P(),
            P(None, "mp"),
            P("mp"),
            P("mp", None),
            P(),
            P(None, "mp"),
            P("mp"),
            P("mp", None),
        ),
        check_vma=False,
    )
```

time: 744 us -> 503 us (0.68)
  Pallas kernels: 0 us -> 237 us
  waiting for transfers between devices: 366 us -> 198 us
  other arithmetic: 157 us -> 9.06 us
  matrix products: 91.1 us -> 5.82 us
  local copies, waits for them, and re-layouts: 74.6 us -> 37.3 us
  blocking collectives: 35.8 us -> 0 us
    pallas_call x0 -> x4, Pallas kernels: none -> 237 us  [the longest x3 226 us: call(): pl.pallas_call(kernel, out_shape=outs, in_specs=[VMEM] * len(args), out_s...]
    psum x4 -> x1, waiting for transfers between devices: 366 us -> 171 us  [body(): lax.psum((proj_g, merge_g.reshape(heads, HEAD_PAD, D)[:, :hd].reshape(loc...]
    dot_general x27 -> x3, matrix products: 89.2 us -> 5.82 us  [the longest x1 5.24 us: body(): jnp.dot(signal_all.T, dmod_cols, precision=lax.Precision.HIGHEST)]
    reduce_sum x11 -> x5, other arithmetic: 60.4 us -> 2.21 us  [the longest x4 1.6 us: body(): jnp.sum(a, axis=0)]
    unnamed x9 -> x0, other arithmetic: 38.7 us -> none
    gather x3 -> x1, local copies, waits for them, and re-layouts: 32.3 us -> 1.13 us  [body(): proj_bias[jnp.array([0, 2])]]
    unnamed x4 -> x3, waiting for transfers between devices: 0.07 us -> 27 us
    psum x1 -> x0, blocking collectives: 25.1 us -> none  [body(): lax.psum(project_bias_grad.astype(jnp.bfloat16), 'dp').astype(jnp.float32)]
  transfers between devices with their start and end apart: 4 -> 2, of which waited for: 4 -> 2; matrix products, arithmetic and copies ran while one was open for 11% -> 3% of each run, Pallas kernels for 0% -> 2%
where the time goes in v1:
time: 503 us; the launch traced here: 502 us
  Pallas kernels  237 us (47%)
  waiting for transfers between devices  198 us (39%)
  local copies, waits for them, and re-layouts  37.3 us (7%)
  between operations  15.1 us (3%)
  other arithmetic  9.06 us (2%)
  matrix products  5.82 us (1%)
    pallas_call x3, Pallas kernels, call(): pl.pallas_call(kernel, out_shape=outs, in_specs=[VMEM] * len(args), out_s...  226 us
    psum x1, waiting for transfers between devices, body(): lax.psum((proj_g, merge_g.reshape(heads, HEAD_PAD, D)[:, :hd].reshape(loc...  171 us
    unnamed x3, waiting for transfers between devices  27 us
    unnamed x50, local copies, waits for them, and re-layouts  15.8 us
    pallas_call x1, Pallas kernels, body(): pl.pallas_call(scatter_kernel, out_shape=[shape(samples, L, D), act_like(...  11 us
  transfers between devices with their start and end apart: 2, of which 2 were waited for; matrix products, arithmetic and copies ran while one was open for 3% of the time, Pallas kernels for 2%

profile of v1, /device:TPU:0, one launch (start us, length us, event | category | flops | bytes accessed | tf_op | source)
XLA Modules:
  0.0 502.4 jit_solution(2215339542915106410)
XLA Ops:
  8.8 2.0 fusion.6
  12.2 1.5 copy.55
  15.2 1.4 pad.27
  17.3 1.2 copy.59.pos_col
  18.5 0.9 pad.31
  20.0 4.1 copy.58.w_mod
  26.9 2.6 copy.60.w_up
  31.0 1.2 copy-done
  32.2 69.9 %attention_forward.1 = (f32[8,6912]{1,0:T(8,128)}, bf16[1536,1152]{1,0:T(8,128)(2,1)}, bf16[1536,768]{1,0:T(8,128)(2,1)}, f32[8,2,192,192]{3,2,1,0:T(8,128)}, bf...) custom-call(bf16[8,256,1152]{2,1,0:T(8,128)(2,1)} %patches.1, ...), custom_call_target="tpu_custom_call" | custom-call | tf_op jit(solution)/shard_map/attention_forward/pallas_call | solution.py:716
  102.1 92.0 %feed_forward.1 = (bf16[1152,576]{1,0:T(8,128)(2,1)}, bf16[576,1152]{1,0:T(8,128)(2,1)}, f32[1,576]{1,0:T(1,128)}, f32[1,1152]{1,0:T(1,128)}, bf16[1536,1152]{1,...) custom-call(bf16[1536,1152]{1,0:T(8,128)(2,1)} %get-tuple-element.42.mlp, ...), custom_call_target="tpu_custom_call" | custom-call | tf_op jit(solution)/shard_map/feed_forward/pallas_call | solution.py:716
  194.1 64.5 %attention_backward.1 = (bf16[3,1152,144]{2,1,0:T(8,128)(2,1)}, f32[1,768]{1,0:T(1,128)}, bf16[256,1152]{1,0:T(8,128)(2,1)}, f32[1,1152]{1,0:T(1,128)}, f32[2,16...) custom-call(bf16[1536,1152]{1,0:T(8,128)(2,1)} %get-tuple-element.48.d_attn, ...), custom_call_target="tpu_custom_call" | custom-call | tf_op jit(solution)/shard_map/attention_backward/pallas_call | solution.py:716
  258.6 1.1 reshape.132
  259.9 0.9 copy.72
  263.7 1.2 dynamic-update-slice
  267.1 11.0 %scatter.1 = (f32[8,256,1152]{2,1,0:T(8,128)}, bf16[8,192,1152]{2,1,0:T(8,128)(2,1)}) custom-call(s32[8]{0:T(128)} %iota_xor_fusion.slot_ref, s32[8,1,192]{2,1,0:T(1,128)} %broadcast_in_dim.42.pos_row, bf16[8,192,1152]{2,1,0:T(8,128)(2,1)} %bitcast.54, bf16[8,192,1152]{2,1,0:T(8,128)(2,1)} %bitcast.53), custom_call_target="tpu_custom_call" | custom-call | tf_op jit(solution)/shard_map/scatter/pallas_call | solution.py:879
  278.1 27.0 %all-reduce.12.cloned.1.call-done = f32[143296]{0:T(1024)} async-done(((f32[143296]{0:T(1024)}), f32[143296]{0:T(1024)}) %all-reduce.12.cloned.1.call-update) | async-done | bytes 573200
  305.1 1.4 reshape.157
  309.1 1.1 gather_fusion
  311.6 5.2 %fusion.7 = f32[1152,864]{0,1:T(8,128)} fusion(f32[32,1152]{1,0:T(8,128)S(1)} %reshape_reshape.10, f32[32,864]{1,0:T(8,128)S(1)} %reshape_reshape.11), kind=kOutput, calls=%fused_computation.31 | convolution fusion | flops 382205952 | bytes 4239360 | tf_op jit(solution)/shard_map/dot_general | solution.py:869
  316.8 170.7 %all-reduce.14.cloned.1.call-done = (bf16[3,1152,144]{2,1,0:T(8,128)(2,1)}, bf16[1152,576]{1,0:T(8,128)(2,1)}, bf16[144,1152]{1,0:T(8,128)(2,1)}, bf16[576,1152]{1,0:T(8,128)(2,1)}) async-done(((bf16[3,1152,144]{2,1,0:T(8,128)(2,1)}, bf16[1152,576]{1,0:T(8,128)(2,1)}, bf16[144,1152]{1,0:T(8,128)(2,1)}, bf16[576,1152]{1,0:T(8,128)(2,1)}), (bf16[3,1152,144]{2,1,0:T(8,128)(2,1)}, bf16[1152,576]{1,0:T(8,128)(2,1)}, ...) | async-done | bytes 3981328 | tf_op jit(solution)/shard_map/psum | solution.py:849
  487.5 3.1 convert_element_type.44
  490.7 2.1 copy.65
  492.8 1.9 copy.64
  494.7 0.9 convert_element_type.42
  (101 shorter events, 18.4 us)
Async XLA Ops:
  7.2 297.9 %all-reduce.12.cloned.1.call-start = ((), (), s32[]{:S(2)}) async-start(), calls=%async_computation | async-start | bytes 1146880
  12.2 4.3 copy-start.18
  15.2 3.4 copy-start.5
  20.0 4.2 copy-start.12
  20.0 4.3 copy-start.10
  20.0 5.8 %copy-start.13 = (bf16[1152]{0:T(1024)(128)(2,1)S(1)}, bf16[1152]{0:T(1024)(128)(2,1)}, u32[]{:S(2)}) copy-start(bf16[1152]{0:T(1024)(128)(2,1)} %param.26) | copy-start | bytes 6916
  20.0 6.4 %copy-start.17 = (bf16[864]{0:T(1024)(128)(2,1)S(1)}, bf16[864]{0:T(1024)(128)(2,1)}, u32[]{:S(2)}) copy-start(bf16[864]{0:T(1024)(128)(2,1)} %param.32) | copy-start | bytes 5188
  24.5 5.1 %copy-start.14 = (bf16[1152]{0:T(1024)(128)(2,1)S(1)}, bf16[1152]{0:T(1024)(128)(2,1)}, u32[]{:S(2)}) copy-start(bf16[1152]{0:T(1024)(128)(2,1)} %param.30) | copy-start | bytes 6916
  24.5 5.7 %copy-start.16 = (bf16[576]{0:T(1024)(128)(2,1)S(1)}, bf16[576]{0:T(1024)(128)(2,1)}, u32[]{:S(2)}) copy-start(bf16[576]{0:T(1024)(128)(2,1)} %param.28) | copy-start | bytes 3460
  24.5 6.2 %copy-start.8 = (bf16[8,1152]{1,0:T(8,128)(2,1)S(1)}, bf16[8,1152]{1,0:T(8,128)(2,1)}, u32[]{:S(2)}) copy-start(bf16[8,1152]{1,0:T(8,128)(2,1)} %condition.1) | copy-start | bytes 55300
  26.9 4.0 copy-start.1
  31.0 1.2 copy-start
  194.1 68.1 %copy-start.11 = (f32[1,1152]{1,0:T(1,128)S(1)}, f32[1,1152]{1,0:T(1,128)}, u32[]{:S(2)}) copy-start(f32[1,1152]{1,0:T(1,128)} %get-tuple-element.66) | copy-start | bytes 13828
  194.1 68.1 %copy-start.15 = (f32[1,576]{1,0:T(1,128)S(1)}, f32[1,576]{1,0:T(1,128)}, u32[]{:S(2)}) copy-start(f32[1,576]{1,0:T(1,128)} %get-tuple-element.65) | copy-start | bytes 6916
  194.1 68.2 %copy-start.19 = (u32[32]{0:T(128)S(1)}, u32[32]{0:T(128)}, u32[]{:S(2)}) copy-start(u32[32]{0:T(128)} %constant.60) | copy-start | bytes 388
  258.6 7.2 %copy-start.7 = (bf16[256,1152]{1,0:T(8,128)(2,1)S(1)}, bf16[256,1152]{1,0:T(8,128)(2,1)}, u32[]{:S(2)}) copy-start(bf16[256,1152]{1,0:T(8,128)(2,1)} %get-tuple-element.68) | copy-start | bytes 1769476
  264.9 0.8 copy-start.2
  265.7 221.8 %all-reduce.14.cloned.1.call-start = ((), (), s32[]{:S(2)}) async-start(), calls=%async_computation.1 | async-start | bytes 9805824 | tf_op jit(solution)/shard_map/psum | solution.py:849
  278.1 29.2 %copy-start.9 = (bf16[31,16,16,1]{0,2,1,3:T(8,128)(2,1)S(1)}, bf16[31,16,16,1]{0,2,1,3:T(8,128)(2,1)}, u32[]{:S(2)}) copy-start(bf16[31,16,16,1]{0,2,1,3:T(8,128)(2,1)} %constant.65) | copy-start | bytes 47620
  487.5 3.1 copy-start.4
  490.7 2.1 copy-start.3
  492.8 1.9 copy-start.6
Sparse Core Ops, SparseCore 0:
  265.9 39.1 all-reduce.11
  308.3 179.1 all-reduce.13

commit v2 on v0

v2 whole, which is shorter than its diff:
```python
import functools
import math
from types import SimpleNamespace

import jax
import jax.numpy as jnp
import numpy as np
from jax import lax
from jax.experimental import pallas as pl
from jax.experimental.pallas import tpu as pltpu
from jax.sharding import PartitionSpec as P

MESH = pl.DeviceIdType.MESH
F32 = jnp.float32
BF16 = jnp.bfloat16
EPSILON = 1e-06
MASKED = -1000000000.0
GELU_C = math.sqrt(2.0 / math.pi)
GELU_A = 0.044715
VMEM = pl.BlockSpec(memory_space=pltpu.VMEM)
HEAD_PAD = 128


def dot(a, b, ca=1, cb=0):
    return lax.dot_general(a, b, (((ca,), (cb,)), ((), ())), preferred_element_type=F32)


def bit_of(value, k):
    return lax.rem(value // (1 << k), 2)


def flip(value, mask):
    out = value
    k = 0
    while (1 << k) <= mask:
        if mask & (1 << k):
            out = out + (1 << k) * (1 - 2 * bit_of(value, k))
        k += 1
    return out


def xor(a, b, bits):
    out = 0
    for k in range(bits):
        out = out + (1 << k) * lax.rem(bit_of(a, k) + bit_of(b, k), 2)
    return out


class Sizes:
    def __init__(self, mp, samples, slots, width):
        self.mp, self.samples, self.slots, self.width = mp, samples, slots, width
        self.bits = mp.bit_length() - 1
        self.rows = samples * slots
        self.block = self.rows // mp
        self.half = self.block // 2
        self.per = self.block and slots // self.block
        rest = [1 << k for k in range(1, self.bits)]
        self.orders = (rest, rest[::-1])
        self.sends = {}
        count = 0
        for h in range(2):
            live = list(range(0, mp, 2))
            for t, bit in enumerate(self.orders[h]):
                moved = [d for d in live if d & bit]
                live = [d for d in live if not d & bit]
                self.sends[h, t] = [(d, bit, count + i) for i, d in enumerate(moved)]
                count += len(moved)
        self.steps = len(rest)
        self.far = count
        self.near = mp // 2
        self.fast = self.steps == 2 and self.per == 1


def my_index():
    return lax.axis_index("dp"), lax.axis_index("mp")


def enter(sz):
    dp, me = my_index()
    barrier = pltpu.get_barrier_semaphore()
    for d in range(1, sz.mp):
        pl.semaphore_signal(barrier, inc=1, device_id=(dp, flip(me, d)), device_id_type=MESH)
    pl.semaphore_wait(barrier, sz.mp - 1)


def rows_of(ref, start, size):
    return ref.at[pl.ds(start, size)]


class Reduce:
    def __init__(self, sz, part, refs):
        self.sz, self.part = sz, part
        self.near_buf, self.far_buf, self.near_send, self.near_recv, self.far_send, self.far_recv = refs
        self.dp, self.me = my_index()

    def near_copy(self, pair):
        b = self.sz.block
        return pltpu.make_async_remote_copy(
            src_ref=rows_of(self.part, (2 * pair + 1) * b, b),
            dst_ref=rows_of(self.near_buf, pair * b, b),
            send_sem=self.near_send.at[pair],
            recv_sem=self.near_recv.at[pair],
            device_id=(self.dp, flip(self.me, 1)),
            device_id_type=MESH,
        )

    def far_copy(self, h, d, bit, i):
        b, hb = self.sz.block, self.sz.half
        return pltpu.make_async_remote_copy(
            src_ref=rows_of(self.part, d * b + h * hb, hb),
            dst_ref=rows_of(self.far_buf, i * hb, hb),
            send_sem=self.far_send.at[i],
            recv_sem=self.far_recv.at[i],
            device_id=(self.dp, flip(self.me, bit)),
            device_id_type=MESH,
        )

    def add(self, start, buf, at, size):
        a = self.part[pl.ds(start, size), :].astype(F32) + buf[pl.ds(at, size), :].astype(F32)
        self.part[pl.ds(start, size), :] = a.astype(BF16)

    def near_add(self, pair):
        b = self.sz.block
        self.near_copy(pair).wait()
        self.add(2 * pair * b, self.near_buf, pair * b, b)

    def send(self, h, d):
        for t in range(self.sz.steps):
            for m in self.sz.sends[h, t]:
                if m[0] == d:
                    self.far_copy(h, *m).start()

    def take(self, h, d, bit, i, add=True):
        b, hb = self.sz.block, self.sz.half
        self.far_copy(h, d, bit, i).wait()
        if add:
            self.add((d - bit) * b + h * hb, self.far_buf, i * hb, hb)

    def after(self, k):
        if k == 0:
            self.send(0, 6)
            self.send(1, 6)
        if k == 1:
            self.send(0, 2)
        if k == 2:
            self.send(1, 4)
            self.take(1, *self.sz.sends[1, 0][1])
            self.send(1, 2)
            self.take(0, *self.sz.sends[0, 0][1])
            self.send(0, 4)

    def close(self):
        sz = self.sz
        if sz.fast:
            for h in range(2):
                for t in range(2):
                    for m in sz.sends[h, t]:
                        if m[0] == m[1]:
                            self.take(h, *m, add=False)
            return

        def one(i, carry):
            self.near_add(sz.near - 1 - i)
            return carry

        lax.fori_loop(0, sz.near, one, 0)
        for t in range(sz.steps):
            for h in range(2):
                for m in sz.sends[h, t]:
                    self.far_copy(h, *m).start()
            for h in range(2):
                for m in sz.sends[h, t]:
                    self.take(h, *m, add=t < sz.steps - 1)

    def own_sum(self):
        sz, hb = self.sz, self.sz.half
        out = []
        for h in range(2):
            total = self.part[h * hb : (h + 1) * hb, :].astype(F32)
            for t in range(0 if sz.fast else sz.steps - 1, sz.steps):
                for d, bit, i in sz.sends[h, t]:
                    if d == bit:
                        total = total + self.far_buf[i * hb : (i + 1) * hb, :].astype(F32)
            out.append(total)
        return jnp.concatenate(out, axis=0)


class Gather:
    def __init__(self, sz, out, sems):
        self.sz, self.out = sz, out
        self.near_send, self.near_recv, self.far_send, self.far_recv = sems
        self.dp, self.me = my_index()
        self.first, self.stages = [], []
        if sz.fast:
            x, y = sz.orders[0]
            self.first = [(1, 0, x, 0), (0, 0, y, 1), (0, 0, x, 2), (1, 0, y, 3)]
            on = {0: (1, x, y, 5), 1: (0, y, x, 4)}
            self.stages = [
                [(self.first[1], [on[1]]), (self.first[0], [on[0]])],
                [(self.first[2], []), (self.first[3], [])],
                [(on[1], []), (on[0], [])],
            ]
        else:
            count, plan = 0, {}
            for h in range(2):
                have = [0]
                for t, bit in enumerate(sz.orders[h][::-1]):
                    plan[h, t] = [(h, d, bit, count + i) for i, d in enumerate(have)]
                    count += len(have)
                    have = have + [d | bit for d in have]
            self.first = plan[0, 0] + plan[1, 0]
            for t in range(sz.steps):
                stage = []
                for h in range(2):
                    later = plan[h, t + 1] if t + 1 < sz.steps else []
                    for k, m in enumerate(plan[h, t]):
                        stage.append((m, later if k == len(plan[h, t]) - 1 else []))
                self.stages.append(stage)

    def near_copy(self, d, h):
        b, hb = self.sz.block, self.sz.half
        return pltpu.make_async_remote_copy(
            src_ref=rows_of(self.out, d * b + h * hb, hb),
            dst_ref=rows_of(self.out, (d + 1) * b + h * hb, hb),
            send_sem=self.near_send.at[d + h],
            recv_sem=self.near_recv.at[d + h],
            device_id=(self.dp, flip(self.me, 1)),
            device_id_type=MESH,
        )

    def far_copy(self, h, d, bit, i):
        b, hb = self.sz.block, self.sz.half
        return pltpu.make_async_remote_copy(
            src_ref=rows_of(self.out, d * b + h * hb, hb),
            dst_ref=rows_of(self.out, (d + bit) * b + h * hb, hb),
            send_sem=self.far_send.at[i],
            recv_sem=self.far_recv.at[i],
            device_id=(self.dp, flip(self.me, bit)),
            device_id_type=MESH,
        )

    def start(self):
        for m in self.first:
            self.far_copy(*m).start()
        for h in range(2):
            self.near_copy(0, h).start()

    def step(self, t):
        for m, later in self.stages[t]:
            self.far_copy(*m).wait()
            for n in later:
                self.far_copy(*n).start()
            h, d, bit, _ = m
            self.near_copy(d + bit, h).start()

    def finish(self, first=0):
        for d in range(first, self.sz.mp, 2):
            for h in range(2):
                self.near_copy(d, h).wait()


def reduce_scratch(sz):
    return [
        pltpu.VMEM((sz.near * sz.block, sz.width), BF16),
        pltpu.VMEM((sz.far * sz.half, sz.width), BF16),
        pltpu.SemaphoreType.DMA((sz.near,)),
        pltpu.SemaphoreType.DMA((sz.near,)),
        pltpu.SemaphoreType.DMA((sz.far,)),
        pltpu.SemaphoreType.DMA((sz.far,)),
    ]


def gather_scratch(sz):
    return [
        pltpu.SemaphoreType.DMA((sz.mp,)),
        pltpu.SemaphoreType.DMA((sz.mp,)),
        pltpu.SemaphoreType.DMA((sz.far,)),
        pltpu.SemaphoreType.DMA((sz.far,)),
    ]


def slot_loop(sz, body, red, extra=None):
    if sz.fast:

        def one(i, carry):
            q = i // 2
            pair = 2 * (1 - lax.rem(q, 2)) + 1 - q // 2
            other = 1 - lax.rem(i, 2)
            body(2 * pair + other)

            @pl.when(other == 1)
            def _():
                red.near_copy(pair).start()

            @pl.when(other == 0)
            def _():
                red.near_add(pair)

            for k in range(3):
                pl.when(i == 2 * k + 1)(functools.partial(red.after, k))
            if extra is not None:
                extra(i)
            return carry

    else:
        pairs = sz.per // 2

        def one(i, carry):
            slot = sz.samples - 1 - i
            body(slot)
            for p in range(pairs):
                red.near_copy(slot * pairs + p).start()
            return carry

    lax.fori_loop(0, sz.samples, one, 0)


def layer_stats(values):
    centre = jnp.mean(values, axis=-1, keepdims=True)
    shifted = values - centre
    spread = jnp.mean(shifted * shifted, axis=-1, keepdims=True)
    inv_std = lax.rsqrt(spread + EPSILON)
    return shifted * inv_std, inv_std


def layer_back(gradient, normed, inv_std):
    mean_grad = jnp.mean(gradient, axis=-1, keepdims=True)
    mean_mix = jnp.mean(gradient * normed, axis=-1, keepdims=True)
    return inv_std * (gradient - mean_grad - normed * mean_mix)


def pick_rows(ids_ref, s, count):
    ids = ids_ref[pl.ds(s, 1), :]
    return (lax.broadcasted_iota(jnp.int32, (count, ids.shape[1]), 0) == ids).astype(F32).astype(BF16)


def live_column(sel):
    ones = jnp.ones((sel.shape[0], 128), BF16)
    return dot(sel, ones, 0, 0)[:, 0:1]


class Call:
    def __init__(self):
        self.args, self.specs, self.outs, self.out_specs, self.scratch_of = {}, [], {}, [], {}

    def arg(self, space=pltpu.VMEM, **values):
        self.args.update(values)
        self.specs += [pl.BlockSpec(memory_space=space)] * len(values)

    def out(self, space=pltpu.VMEM, **results):
        for name, (shape, dtype) in results.items():
            self.outs[name] = jax.ShapeDtypeStruct(shape, dtype)
            self.out_specs.append(pl.BlockSpec(memory_space=space))

    def scratch(self, **buffers):
        self.scratch_of.update(buffers)

    def vmem(self, **buffers):
        for name, (shape, dtype) in buffers.items():
            self.scratch_of[name] = pltpu.VMEM(shape, dtype)

    def run(self, kernel, name, cid, limit):
        flat = []
        for value in self.scratch_of.values():
            flat += value if isinstance(value, list) else [value]

        def inner(*refs):
            r, refs = SimpleNamespace(), list(refs)
            for key in list(self.args) + list(self.outs):
                setattr(r, key, refs.pop(0))
            for key, value in self.scratch_of.items():
                count = len(value) if isinstance(value, list) else 0
                setattr(r, key, [refs.pop(0) for _ in range(count)] if count else refs.pop(0))
            kernel(r)

        got = pl.pallas_call(
            inner,
            out_shape=list(self.outs.values()),
            in_specs=self.specs,
            out_specs=self.out_specs,
            scratch_shapes=flat,
            name=name,
            compiler_params=pltpu.CompilerParams(
                collective_id=cid, has_side_effects=True, vmem_limit_bytes=limit
            ),
        )(*self.args.values())
        return SimpleNamespace(**dict(zip(self.outs, got)))


def attention_forward(sz, heads, hd, grid_side, cols, r):
    dp, me = my_index()
    mine = me // sz.per
    sbits = sz.samples.bit_length() - 1
    D, n, L = sz.width, sz.slots, grid_side * grid_side
    lanes = heads * HEAD_PAD
    red = Reduce(sz, r.part, r.red)
    mod_buf, mod_wide, modv, vec = r.mod_buf, r.mod_wide, r.modv, r.vec
    wide = mod_buf.shape[2]
    sem = r.sem

    load_mod = pltpu.make_async_copy(r.w_mod, r.w_mod_v, sem.at[0])
    load_mod.start()

    def load_patches(i, slot):
        return pltpu.make_async_copy(r.patches.at[xor(mine, slot, sbits)], r.patches_v.at[slot], r.load_sem.at[i])

    def start_load(slot, carry):
        load_patches(slot, slot).start()
        return carry

    lax.fori_loop(0, sz.samples, start_load, 0)
    cond = r.condition[...].astype(F32)
    signal = (cond / (1.0 + jnp.exp(-cond))).astype(BF16)
    mod_buf[me] = jnp.zeros((sz.samples, wide), F32)
    load_mod.wait()
    mod_buf[me, :, 0:cols] = dot(signal, r.w_mod_v[...], 1, 1) + vec[5:6, 0:cols]
    enter(sz)

    def mod_copy(d, slot):
        return pltpu.make_async_remote_copy(
            src_ref=mod_buf.at[slot],
            dst_ref=mod_buf.at[slot],
            send_sem=r.mod_send.at[d],
            recv_sem=r.mod_recv.at[d],
            device_id=(dp, flip(me, d)),
            device_id_type=MESH,
        )

    for d in range(1, sz.mp):
        mod_copy(d, me).start()

    w_qkv, w_merge = r.w_qkv_v, r.w_merge_v
    pad_rows = jnp.zeros((HEAD_PAD - hd, D), F32)
    for h in range(heads):
        for c in range(3):
            piece = r.w_in[c].astype(F32)[h * hd : (h + 1) * hd]
            w_qkv[c * lanes + h * HEAD_PAD : c * lanes + (h + 1) * HEAD_PAD, :] = jnp.concatenate(
                [piece, pad_rows], axis=0
            ).astype(BF16)
        piece = r.w_out[...].astype(F32)[h * hd : (h + 1) * hd]
        w_merge[h * HEAD_PAD : (h + 1) * HEAD_PAD, :] = jnp.concatenate([piece, pad_rows], axis=0).astype(BF16)
    save = [
        pltpu.make_async_copy(w_qkv, r.w_qkv, sem.at[1]),
        pltpu.make_async_copy(w_merge, r.w_merge, sem.at[2]),
    ]
    for copy in save:
        copy.start()

    bias_full = r.bias_full
    span = r.table.shape[1]
    for h in range(heads):
        line = r.table[h : h + 1, :]
        strip = jnp.concatenate([line] + [pltpu.roll(line, span - c, 1) for c in range(1, grid_side)], axis=0)
        for row in range(grid_side):
            rolled = pltpu.roll(strip, span - row * 2 * grid_side, 1) if row else strip
            bias_full[h, row * grid_side : (row + 1) * grid_side, :] = rolled[:, : 2 * L].astype(BF16)

    normed, kept_own = r.normed, r.kept_v

    def norm_one(slot, carry):
        load_patches(slot, slot).wait()
        sel = pick_rows(r.pos, xor(mine, slot, sbits), L)
        kept = dot(sel, r.patches_v[slot], 0, 0)
        value, _ = layer_stats(kept)
        normed[pl.ds(slot * n, n), :] = value

        @pl.when(slot == 0)
        def _():
            kept_own[...] = kept[: sz.block]

        return carry

    lax.fori_loop(0, sz.samples, norm_one, 0)
    save_kept = pltpu.make_async_copy(kept_own, r.kept, sem.at[3])
    save_kept.start()

    for d in range(1, sz.mp):
        mod_copy(d, me).wait_send()
        mod_copy(d, flip(me, d)).wait_recv()
    mod_wide[...] = jnp.zeros_like(mod_wide)
    for m in range(sz.mp):
        base = m * cols // 128 * 128
        phase = m * cols - base
        piece = mod_buf[m]
        if phase:
            piece = pltpu.roll(piece, phase, 1)
        mod_wide[:, base : base + wide] += piece
    modv[...] = mod_wide[:, : 6 * D]

    factor = hd ** (-0.5)
    stores = [(r.attn_in_v, r.attn_in), (r.qkv_v, r.qkv), (r.att_v, r.att)]

    def save_slot(i, slot):
        at = pl.ds(slot * n, n)
        copies = [
            pltpu.make_async_copy(a.at[at], b.at[at], r.save_sem.at[k, slot]) for k, (a, b) in enumerate(stores)
        ]
        copies.append(pltpu.make_async_copy(r.probs_v.at[slot], r.probs.at[slot], r.save_sem.at[3, slot]))
        return copies

    def body(slot):
        s = xor(mine, slot, sbits)
        at = pl.ds(slot * n, n)
        shift = modv[pl.ds(s, 1), 0:D]
        scale = modv[pl.ds(s, 1), D : 2 * D]
        entry = (normed[at, :] * (1.0 + scale) + shift).astype(BF16)
        r.attn_in_v[at, :] = entry
        proj = dot(entry, w_qkv[...], 1, 1)
        qs = (proj[:, :lanes] + vec[0:1, :lanes]).astype(BF16)
        ks = proj[:, lanes : 2 * lanes].astype(BF16)
        vs = (proj[:, 2 * lanes :] + vec[1:2, :lanes]).astype(BF16)
        r.qkv_v[at, 0:lanes] = qs
        r.qkv_v[at, lanes : 2 * lanes] = ks
        r.qkv_v[at, 2 * lanes :] = vs
        sel = pick_rows(r.pos, s, L)
        sel_wide = pick_rows(r.pos_wide, s, 2 * L)
        live = r.pos[pl.ds(s, 1), :] >= 0
        outs = []
        for h in range(heads):
            cut = slice(h * HEAD_PAD, (h + 1) * HEAD_PAD)
            bias = dot(dot(sel, bias_full[h], 0, 0).astype(BF16), sel_wide)
            scores = jnp.where(live, dot(qs[:, cut], ks[:, cut], 1, 1) * factor + bias, MASKED)
            top = jnp.max(scores, axis=-1, keepdims=True)
            e = jnp.exp(scores - top)
            p = e / jnp.sum(e, axis=-1, keepdims=True)
            r.probs_v[slot, h] = p
            outs.append(dot(p.astype(BF16), vs[:, cut]).astype(BF16))
        joined = jnp.concatenate(outs, axis=1) if heads > 1 else outs[0]
        r.att_v[at, :] = joined
        r.part[at, :] = dot(joined, w_merge[...]).astype(BF16)
        for copy in save_slot(0, slot):
            copy.start()

    slot_loop(sz, body, red)
    red.close()
    result = red.own_sum() + vec[2:3, :D]
    r.res_v[...] = result
    hidden = kept_own[...] + modv[pl.ds(mine, 1), 2 * D : 3 * D] * result
    r.hidden_v[...] = hidden
    value, _ = layer_stats(hidden)
    shift = modv[pl.ds(mine, 1), 3 * D : 4 * D]
    scale = modv[pl.ds(mine, 1), 4 * D : 5 * D]
    r.mlp_v[...] = (value * (1.0 + scale) + shift).astype(BF16)
    save_own = [
        pltpu.make_async_copy(r.res_v, r.res, sem.at[4]),
        pltpu.make_async_copy(r.hidden_v, r.hidden, sem.at[5]),
        pltpu.make_async_copy(r.mlp_v, r.mlp, sem.at[6]),
    ]
    for copy in save_own:
        copy.start()

    def wait_slot(slot, carry):
        for copy in save_slot(0, slot):
            copy.wait()
        return carry

    lax.fori_loop(0, sz.samples, wait_slot, 0)
    for copy in save + save_own + [save_kept]:
        copy.wait()


class Line:
    def __init__(self, r, chunk):
        self.r, self.chunk = r, chunk
        self.g, self.outer_buf, self.inner_buf = r.grads, r.z_outer, r.z_inner
        self.count = self.g.shape[1] // chunk
        self.dp, self.me = my_index()
        self.is_inner = (self.dp == 1) | (self.dp == 2)
        self.is_outer = (self.dp == 0) | (self.dp == 3)
        self.step_to = 1 + self.dp // 3
        self.back_to = (self.dp - 1) * 3
        self.other = 3 - self.dp
        self.mine = 2 - self.dp
        self.passed = self.dp - 1

    def rows(self, k):
        return pl.ds(k * self.chunk, self.chunk)

    def copy(self, src, dst, send, recv, to):
        return pltpu.make_async_remote_copy(
            src_ref=src, dst_ref=dst, send_sem=send, recv_sem=recv, device_id=(to, self.me), device_id_type=MESH
        )

    def out_copy(self, j, k):
        return self.copy(
            self.g.at[j, self.rows(k)], self.outer_buf.at[j, self.rows(k)],
            self.r.zs.at[j, k], self.r.zo.at[j, k], self.step_to,
        )

    def in_copy(self, k):
        return self.copy(
            self.g.at[self.passed, self.rows(k)], self.inner_buf.at[self.rows(k)],
            self.r.zf.at[k], self.r.zi.at[k], self.other,
        )

    def total_copy(self, j, k, which, to):
        return self.copy(
            self.outer_buf.at[j, self.rows(k)], self.outer_buf.at[j, self.rows(k)],
            self.r.zt.at[which, k], self.r.zr.at[j, k], to,
        )

    def begin(self, j, k0, k1):
        @pl.when(self.is_outer)
        def _():
            def one(k, carry):
                self.out_copy(j, k).start()
                return carry

            lax.fori_loop(k0, k1, one, 0)

    def add(self, to, j, k, more):
        def one(i, carry):
            at = pl.ds(k * self.chunk + i * 16, 16)
            v = self.g[j, at, :].astype(F32) + self.outer_buf[j, at, :].astype(F32)
            if more:
                v = v + self.inner_buf[at, :].astype(F32)
            to[j, at, :] = v.astype(BF16)
            return carry

        lax.fori_loop(0, self.chunk // 16, one, 0)

    def stage(self, number, j, k):
        if number == 1:

            @pl.when(self.passed == j)
            def _():
                self.out_copy(j, k).wait_recv()
                self.add(self.g, j, k, False)
                self.in_copy(k).start()

        elif number == 2:

            @pl.when(self.mine == j)
            def _():
                self.out_copy(j, k).wait_recv()
                self.in_copy(k).wait_recv()
                self.add(self.outer_buf, j, k, True)
                self.total_copy(j, k, 0, self.other).start()
                self.total_copy(j, k, 1, self.back_to).start()

        else:

            @pl.when(self.passed == j)
            def _():
                self.in_copy(k).wait_send()
                self.total_copy(j, k, 0, self.other).wait_recv()
                self.total_copy(j, k, 2, self.back_to).start()

    def finish(self):
        @pl.when(self.is_inner)
        def _():
            def one(k, carry):
                self.total_copy(self.mine, k, 0, self.other).wait_send()
                self.total_copy(self.mine, k, 1, self.back_to).wait_send()
                self.total_copy(self.passed, k, 2, self.back_to).wait_send()
                return carry

            lax.fori_loop(0, self.count, one, 0)

        @pl.when(self.is_outer)
        def _():
            def one(k, carry):
                for j in range(2):
                    self.out_copy(j, k).wait_send()
                    self.total_copy(j, k, 0, self.step_to).wait_recv()
                return carry

            lax.fori_loop(0, self.count, one, 0)


def block_backward(sz, heads, hd, grid_side, cols, dp_size, chunk, r):
    dp, me = my_index()
    mine = me // sz.per
    sbits = sz.samples.bit_length() - 1
    D, n, L = sz.width, sz.slots, grid_side * grid_side
    lanes = heads * HEAD_PAD
    local = heads * hd
    F = r.w_up_v.shape[0]
    block = sz.block
    vec, modv = r.vec, r.modv
    fwd = Reduce(sz, r.part_f, r.red_f)
    bwd = Reduce(sz, r.part_b, r.red_b)
    last = Reduce(sz, r.part_b, r.red_b[:2] + r.last_sems)
    gat_m = Gather(sz, r.mlp_v, r.gat_m)
    gat_d = Gather(sz, r.d_attn, r.gat_d)
    gat_o = Gather(sz, r.part_f, r.gat_o)
    gat_k = Gather(sz, r.mlp_v, r.gat_k)
    line = Line(r, chunk) if chunk else None
    grads = r.grads
    sem = r.sem

    per_up, per_local = (F // chunk, local // chunk) if chunk else (0, 0)
    marks = [0, per_up, per_up + per_local, per_up + 2 * per_local]
    following = {(number, j): 0 for number in (1, 2, 3) for j in range(2)}

    def tick(*steps):
        if line is None:
            return
        for number, j, count in steps:
            k0 = following[number, j]
            k1 = min(k0 + count, marks[3])
            assert number == 1 or k1 <= following[number - 1, j]
            following[number, j] = k1
            if k1 - k0 == 1:
                line.stage(number, j, k0)
            elif k1 > k0:

                def one(k, carry, number=number, j=j):
                    line.stage(number, j, k)
                    return carry

                lax.fori_loop(k0, k1, one, 0)

    def begin(j, group):
        if line is not None:
            line.begin(j, marks[group], marks[group + 1])

    def ticks_at(i, plan):
        if line is not None:
            for when, steps in plan.items():
                pl.when(i == when)(lambda steps=steps: tick(*steps))

    load_up = pltpu.make_async_copy(r.w_up, r.w_up_v, sem.at[0])
    load_down = pltpu.make_async_copy(r.w_down, r.w_down_v, sem.at[1])
    load_up.start()
    load_down.start()

    load_own = pltpu.make_async_copy(r.mlp, r.mlp_v.at[pl.ds(0, block)], sem.at[12])
    load_own.start()

    def load_cot(slot):
        at = pl.ds(slot * n, n)
        return pltpu.make_async_copy(r.cot.at[xor(mine, slot, sbits)], r.d_mlp.at[at], r.load_sem.at[1, slot])

    def start_cot(slot, carry):
        load_cot(slot).start()
        return carry

    lax.fori_loop(0, sz.samples, start_cot, 0)
    loads = [
        pltpu.make_async_copy(r.cot.at[mine, pl.ds(0, block)], r.cot_own, sem.at[2]),
        pltpu.make_async_copy(r.hidden, r.hidden_v, sem.at[3]),
        pltpu.make_async_copy(r.res, r.res_v, sem.at[4]),
    ]
    late = [
        pltpu.make_async_copy(r.qkv, r.qkv_v, sem.at[6]),
        pltpu.make_async_copy(r.probs, r.probs_v, sem.at[7]),
        pltpu.make_async_copy(r.w_qkv, r.w_qkv_v, sem.at[9]),
        pltpu.make_async_copy(r.w_merge, r.w_merge_v, sem.at[10]),
    ]
    for copy in loads + late:
        copy.start()
    load_attn = pltpu.make_async_copy(r.attn_in, r.d_mlp, sem.at[11])
    load_kept = pltpu.make_async_copy(r.kept, r.res_v, sem.at[5])
    load_att = pltpu.make_async_copy(r.att, r.act.at[:, pl.ds(0, lanes)], sem.at[8])

    barrier = pltpu.get_barrier_semaphore()
    for d in range(1, sz.mp):
        pl.semaphore_signal(barrier, inc=1, device_id=(dp, flip(me, d)), device_id_type=MESH)
    for e in range(1, dp_size):
        pl.semaphore_signal(barrier, inc=1, device_id=(lax.rem(dp + e, dp_size), me), device_id_type=MESH)
    pl.semaphore_wait(barrier, sz.mp + dp_size - 2)
    load_own.wait()
    gat_m.start()
    load_up.wait()
    load_down.wait()
    w_up, w_down, mlp = r.w_up_v, r.w_down_v, r.mlp_v
    act, d_pre, d_mlp, slope = r.act, r.d_pre, r.d_mlp, r.slope

    up_bg, down_bg = r.bias_g.at[dp, 0:1], r.bias_g.at[dp, 1:2]
    merge_bg, proj_bg = r.bias_g.at[dp, 2:3], r.bias_g.at[dp, 3:4]
    r.bias_g[dp] = jnp.zeros(r.bias_g.shape[1:], F32)
    cond = r.condition[...].astype(F32)
    r.signal_g[dp] = (cond / (1.0 + jnp.exp(-cond))).astype(BF16)
    shared = [r.bias_g, r.table_g, r.mod_g, r.signal_g]

    def dp_copy(k, e, slot):
        return pltpu.make_async_remote_copy(
            src_ref=shared[k].at[slot],
            dst_ref=shared[k].at[slot],
            send_sem=r.dp_send.at[k, e],
            recv_sem=r.dp_recv.at[k, e],
            device_id=(lax.rem(dp + e, dp_size), me),
            device_id_type=MESH,
        )

    def share(k):
        for e in range(1, dp_size):
            dp_copy(k, e, dp).start()

    share(3)

    def forward(slot, wide):
        at = pl.ds(slot * n, wide * n)
        v = dot(mlp[at, :], w_up[...], 1, 1) + vec[3:4, :F]
        square = v * v
        t = jnp.tanh(GELU_C * (v + GELU_A * v * square))
        active = (0.5 * v * (1.0 + t)).astype(BF16)
        act[at, :] = active
        slope[at, :] = 0.5 * (1.0 + t) + 0.5 * v * (1.0 - t * t) * (GELU_C * (1.0 + 3.0 * GELU_A * square))
        r.part_f[at, :] = dot(active, w_down[...]).astype(BF16)
        for k in range(wide):
            at = pl.ds((slot + k) * n, n)
            s = xor(mine, slot + k, sbits)
            load_cot(slot + k).wait()
            gate = modv[pl.ds(s, 1), 5 * D : 6 * D]
            live = live_column(pick_rows(r.pos, s, L))
            dm = (gate * (d_mlp[at, :].astype(F32) * live)).astype(BF16)
            d_mlp[at, :] = dm
            down_bg[...] += jnp.sum(dm.astype(F32), axis=0, keepdims=True)

    if sz.fast:
        def two_slots(i, carry):
            @pl.when(i == 1)
            def _():
                gat_m.step(0)
                gat_m.step(1)

            @pl.when(i == 3)
            def _():
                gat_m.step(2)

            for h in range(2):
                gat_m.near_copy(2 * i, h).wait()
            forward(2 * i, 2)
            fwd.near_copy(i).start()

            @pl.when(i > 0)
            def _():
                fwd.near_add(i - 1)

            pl.when(i == 2)(functools.partial(fwd.send, 0, 2))
            pl.when(i == 3)(functools.partial(fwd.send, 1, 4))
            return carry

        lax.fori_loop(0, 4, two_slots, 0)
    else:
        for t in range(len(gat_m.stages)):
            gat_m.step(t)
        gat_m.finish()
        slot_loop(sz, lambda slot: forward(slot, 1), fwd)

    def wide_grad(left, right, half):
        at = 0
        while at < F:
            size = min(256, F - at)
            grads[half, at : at + size, :] = dot(left[:, at : at + size], right[...], 0, 0).astype(BF16)
            at += size

    wide_grad(act, d_mlp, 1)
    begin(1, 0)
    if sz.fast:
        fwd.near_add(3)
        fwd.send(0, 6)
        fwd.send(1, 6)

    def backward(slot):
        at = pl.ds(slot * n, n)
        dpre = (dot(d_mlp[at, :], w_down[...], 1, 1) * slope[at, :]).astype(BF16)
        d_pre[at, :] = dpre
        up_bg[:, :F] += jnp.sum(dpre.astype(F32), axis=0, keepdims=True)
        r.part_b[at, :] = dot(dpre, w_up[...]).astype(BF16)

    plan = {
        1: [(1, 1, 1)],
        2: [(1, 1, 1)],
        3: [(1, 1, 1)],
        4: [(1, 1, 1), (2, 1, 1)],
        5: [(1, 1, 1), (2, 1, 1)],
        6: [(1, 1, 1), (2, 1, 1)],
        7: [(1, 1, 1), (2, 1, 1)],
    }

    slot_loop(sz, backward, bwd, lambda i: ticks_at(i, plan))
    load_attn.start()
    load_att.start()
    wide_grad(d_pre, mlp, 0)
    begin(0, 0)
    tick((1, 1, 1), (2, 1, 1), (3, 1, 2))
    for copy in loads:
        copy.wait()
    normed2, inv2 = layer_stats(r.hidden_v[...])
    r.normed_v[...] = normed2
    if sz.fast:
        fwd.take(1, *sz.sends[1, 0][1])
        fwd.take(0, *sz.sends[0, 0][1])
    bwd.close()
    tick((1, 1, 1), (2, 1, 1), (3, 1, 1))

    mrow = pl.ds(mine, 1)
    live = live_column(pick_rows(r.pos, mine, L)[:, :block])
    d_out = r.cot_own[...].astype(F32) * live
    d_mlp_in = bwd.own_sum()
    g = d_mlp_in * (1.0 + modv[mrow, 4 * D : 5 * D])
    dh = d_out + layer_back(g, r.normed_v[...], inv2)
    r.dh_v[...] = dh
    r.d_attn[:block, :] = (modv[mrow, 2 * D : 3 * D] * dh).astype(BF16)
    gat_d.start()

    early, late_sums = r.early, r.late_sums
    early[me, 0:1, :] = jnp.sum(dh * r.res_v[...], axis=0, keepdims=True)
    load_kept.start()
    early[me, 1:2, :] = jnp.sum(d_mlp_in, axis=0, keepdims=True)
    early[me, 2:3, :] = jnp.sum(d_mlp_in * r.normed_v[...], axis=0, keepdims=True)

    def finish_out():
        fwd.close()
        live = live_column(pick_rows(r.pos, mine, L)[:, :block])
        mlp_out = fwd.own_sum() + vec[4:5, :D]
        early[me, 3:4, :] = jnp.sum(mlp_out * (r.cot_own[...].astype(F32) * live), axis=0, keepdims=True)
        out_own = (r.hidden_v[...] + modv[mrow, 5 * D : 6 * D] * mlp_out) * live
        r.part_f[:block, :] = out_own.astype(BF16)

    def dm_copy(ref, k, d, slot):
        return pltpu.make_async_remote_copy(
            src_ref=ref.at[slot],
            dst_ref=ref.at[slot],
            send_sem=r.dm_send.at[k, d],
            recv_sem=r.dm_recv.at[k, d],
            device_id=(dp, flip(me, d)),
            device_id_type=MESH,
        )

    tick((1, 1, 1))

    def attention_grad(c, half, at):
        if c < 3:
            full = dot(qkv[:, c * lanes : (c + 1) * lanes], d_mlp[...], 0, 0)
        else:
            full = dot(r.act[:, :lanes], r.d_attn[...], 0, 0)
        rows = [full[h * HEAD_PAD : h * HEAD_PAD + hd] for h in range(heads)]
        rows = jnp.concatenate(rows, axis=0) if heads > 1 else rows[0]
        grads[half, at : at + local, :] = rows.astype(BF16)

    for copy in late:
        copy.wait()
    factor = hd ** (-0.5)
    grid_g = r.grid_g
    grid_g[...] = jnp.zeros_like(grid_g)
    qkv, w_qkv, w_merge = r.qkv_v, r.w_qkv_v, r.w_merge_v
    def attention(slot):
        s = xor(mine, slot, sbits)
        at = pl.ds(slot * n, n)
        da = r.d_attn[at, :]
        merge_bg[...] += jnp.sum(da.astype(F32), axis=0, keepdims=True)
        d_att = dot(da, w_merge[...], 1, 1).astype(BF16)
        sel = pick_rows(r.pos, s, L)
        sel_wide = pick_rows(r.pos_wide, s, 2 * L)
        dq, dk, dv = [], [], []
        for h in range(heads):
            q = qkv[at, h * HEAD_PAD : (h + 1) * HEAD_PAD]
            k = qkv[at, lanes + h * HEAD_PAD : lanes + (h + 1) * HEAD_PAD]
            v = qkv[at, 2 * lanes + h * HEAD_PAD : 2 * lanes + (h + 1) * HEAD_PAD]
            d_a = d_att[:, h * HEAD_PAD : (h + 1) * HEAD_PAD]
            p = r.probs_v[slot, h]
            d_p = dot(d_a, v, 1, 1)
            dv.append(dot(p.astype(BF16), d_a, 0, 0).astype(BF16))
            ds = p * (d_p - jnp.sum(p * d_p, axis=-1, keepdims=True))
            dl = ds.astype(BF16)
            dq.append((dot(dl, k) * factor).astype(BF16))
            dk.append((dot(dl, q, 0, 0) * factor).astype(BF16))
            grid_g[h] += dot(dot(sel, dl).astype(BF16), sel_wide, 1, 1)
        joined = jnp.concatenate(dq + dk + dv, axis=1)
        qkv[at, :] = joined
        proj_bg[:, : 3 * lanes] += jnp.sum(joined.astype(F32), axis=0, keepdims=True)
        r.part_b[at, :] = dot(joined, w_qkv[...]).astype(BF16)

    if sz.fast:
        plan_one = {1: [(1, 1, 1), (2, 1, 2), (3, 1, 2)], 2: [(1, 1, 1), (2, 1, 1), (3, 1, 2)]}
        plan_two = {
            3: [(1, 0, 2)],
            4: [(1, 0, 1), (2, 0, 1), (3, 1, 1)],
            5: [(1, 0, 2), (2, 0, 1), (3, 1, 1)],
            6: [(1, 0, 1), (2, 0, 1), (3, 0, 1), (3, 1, 1)],
            7: [(1, 0, 1), (2, 0, 1), (3, 0, 1)],
        }

        def one(i, carry):
            q = i // 2
            pair = q + lax.rem(q, 2) * (q // 2) * -1 + (q // 2) * (1 - lax.rem(q, 2))
            slot = jnp.where(i < 2, i, 2 * pair + 1 - lax.rem(i, 2))

            ticks_at(i, plan_one)

            @pl.when(i == 1)
            def _():
                for h in range(2):
                    gat_d.near_copy(0, h).wait()

            @pl.when(i == 2)
            def _():
                gat_d.step(0)
                tick((2, 1, 1), (3, 1, 1))
                gat_d.step(1)
                fwd.send(1, 2)
                fwd.send(0, 4)
                tick((2, 1, 2), (1, 0, 2), (3, 1, 1))
                for h in range(2):
                    gat_d.near_copy(2, h).wait()

            ticks_at(i, plan_two)

            @pl.when(i == 4)
            def _():
                gat_d.step(2)
                for d in (4, 6):
                    for h in range(2):
                        gat_d.near_copy(d, h).wait()

            attention(slot)

            @pl.when(i == 1)
            def _():
                last.near_copy(0).start()

            @pl.when((i > 1) & (lax.rem(i, 2) == 0))
            def _():
                last.near_copy(pair).start()

            @pl.when(i == 3)
            def _():
                last.near_add(0)
                last.near_add(1)
                last.send(0, 2)

            @pl.when(i == 6)
            def _():
                finish_out()

            @pl.when(i == 5)
            def _():
                last.near_add(3)
                last.send(0, 6)
                last.send(1, 6)

            @pl.when(i == 7)
            def _():
                last.near_add(2)
                last.after(2)

            return carry

        lax.fori_loop(0, 8, one, 0)
        tick((1, 0, 1), (2, 0, 1), (3, 0, 1))
    else:
        for t in range(len(gat_d.stages)):
            gat_d.step(t)
        gat_d.finish()
        finish_out()
        slot_loop(sz, attention, last)

    load_attn.wait()
    load_att.wait()
    attention_grad(3, 1, F)
    begin(1, 1)
    tick((1, 0, 1), (2, 0, 1))
    attention_grad(0, 0, F)
    begin(0, 1)
    attention_grad(2, 1, F + local)
    begin(1, 2)
    attention_grad(1, 0, F + local)
    begin(0, 2)
    tick((1, 0, 1), (2, 0, 1), (3, 0, 2))

    tables = r.table_g
    span = tables.shape[2]
    for h in range(heads):
        strip = jnp.zeros((grid_side, span), F32)
        for row in range(grid_side):
            piece = jnp.concatenate(
                [
                    grid_g[h, row * grid_side : (row + 1) * grid_side, :],
                    jnp.zeros((grid_side, span - 2 * L), F32),
                ],
                axis=1,
            )
            strip = strip + (pltpu.roll(piece, row * 2 * grid_side, 1) if row else piece)
        total_row = strip[0:1]
        for c in range(1, grid_side):
            total_row = total_row + pltpu.roll(strip[c : c + 1], c, 1)
        tables[dp, h : h + 1, :] = total_row

    share(0)
    share(1)
    load_kept.wait()
    normed1, inv1 = layer_stats(r.res_v[...])
    r.normed_v[...] = normed1
    last.close()
    tick((2, 0, 2), (3, 0, 1), (1, 1, 2))
    d_in = last.own_sum()
    g = d_in * (1.0 + modv[mrow, D : 2 * D])
    mlp[:block, :] = (r.dh_v[...] + layer_back(g, r.normed_v[...], inv1)).astype(BF16)
    late_sums[me, 0:1, :] = jnp.sum(d_in, axis=0, keepdims=True)
    late_sums[me, 1:2, :] = jnp.sum(d_in * r.normed_v[...], axis=0, keepdims=True)
    gat_k.start()
    tick((2, 0, 1), (1, 1, 1), (3, 0, 1))

    def out_copy(slot):
        return pltpu.make_async_copy(
            r.part_f.at[pl.ds(slot * n, n)], r.out.at[xor(mine, slot, sbits)], r.load_sem.at[0, slot]
        )

    def start_out(slot, carry):
        out_copy(slot).start()
        return carry

    def patch_copy(slot):
        return pltpu.make_async_copy(
            r.part_b.at[pl.ds(lax.rem(slot, 2) * L, L)], r.patch_g.at[xor(mine, slot, sbits)], r.load_sem.at[1, slot]
        )

    def patch(slot, carry):
        @pl.when(slot >= 2)
        def _():
            patch_copy(slot - 2).wait()

        sel = pick_rows(r.pos, xor(mine, slot, sbits), L)
        r.part_b[pl.ds(lax.rem(slot, 2) * L, L), :] = dot(sel, mlp[pl.ds(slot * n, n), :]).astype(BF16)
        patch_copy(slot).start()
        return carry

    for h in range(2):
        gat_k.near_copy(0, h).wait()
    if sz.fast:
        lax.fori_loop(0, 2, patch, 0)
    gat_k.step(0)
    for d in range(1, sz.mp):
        dm_copy(early, 0, d, me).start()
        dm_copy(late_sums, 1, d, me).start()
    gat_o.start()
    tick((2, 0, 2), (1, 0, 2), (3, 0, 2), (2, 1, 1))
    gat_k.step(1)
    tick((1, 0, 1), (1, 1, 1), (2, 1, 2), (2, 0, 1), (3, 0, 3))
    if sz.fast:
        for d in (2, 4):
            for h in range(2):
                gat_k.near_copy(d, h).wait()
        lax.fori_loop(2, 6, patch, 0)
        gat_k.step(2)
        tick((1, 1, 2), (2, 0, 2), (3, 1, 2))
        for h in range(2):
            gat_k.near_copy(6, h).wait()
        lax.fori_loop(6, 8, patch, 0)
    else:
        for t in range(2, len(gat_k.stages)):
            gat_k.step(t)
        gat_k.finish(2)
        lax.fori_loop(0, sz.samples, patch, 0)
    for d in range(1, sz.mp):
        dm_copy(early, 0, d, me).wait_send()
        dm_copy(early, 0, d, flip(me, d)).wait_recv()
        dm_copy(late_sums, 1, d, me).wait_send()
        dm_copy(late_sums, 1, d, flip(me, d)).wait_recv()
    flat, mod_g = r.flat, r.mod_g
    flat[:, 6 * D :] = jnp.zeros((sz.samples, flat.shape[1] - 6 * D), F32)
    for s in range(sz.samples):
        for c in range(6):
            v = 0
            for p in range(sz.per):
                m = s * sz.per + p
                v = v + (late_sums[m, c : c + 1, :] if c < 2 else early[m, c - 2 : c - 1, :])
            flat[s : s + 1, c * D : (c + 1) * D] = v
    base = pl.multiple_of(me * cols // 128 * 128, 128)
    mod_g[dp] = flat[:, pl.ds(base, mod_g.shape[2])]
    share(2)
    tick((1, 0, 1), (2, 0, 1))
    gat_o.step(0)
    tick((1, 0, 1), (2, 1, 1), (3, 1, 1), (3, 0, 1))
    gat_o.step(1)
    tick((2, 1, 1), (1, 0, 1), (3, 0, 1))
    for t in range(2, len(gat_o.stages)):
        gat_o.step(t)
    gat_o.finish()
    lax.fori_loop(0, sz.samples, start_out, 0)
    tick((2, 1, 1), (3, 0, 1), (2, 0, 1), (3, 1, 1), (2, 0, 1), (3, 1, 1), (2, 0, 1), (3, 1, 1), (3, 0, 3))
    if line is not None:
        assert all(k == marks[3] for k in following.values()), following
    for k in range(4):
        for e in range(1, dp_size):
            dp_copy(k, e, dp).wait_send()
            dp_copy(k, e, lax.rem(dp + dp_size - e, dp_size)).wait_recv()
    for slot in range(sz.samples - 2, sz.samples):
        patch_copy(slot).wait()

    def wait_out(slot, carry):
        out_copy(slot).wait()
        return carry

    lax.fori_loop(0, sz.samples, wait_out, 0)
    if line is not None:
        line.finish()


def body(
    patches,
    condition,
    lengths,
    keep_order,
    cotangent,
    projection_weight,
    query_value_bias,
    merge_weight,
    merge_output_bias,
    up_weight,
    up_projection_bias,
    down_weight,
    down_projection_bias,
    w_modulate,
    bias_modulate,
    bias_table,
):
    samples, L, D = patches.shape
    n = cotangent.shape[1]
    grid_side = math.isqrt(L)
    offsets = 2 * grid_side - 1
    heads = bias_table.shape[0]
    local = projection_weight.shape[2]
    hd = local // heads
    lanes = heads * HEAD_PAD
    F = up_weight.shape[1]
    cols = w_modulate.shape[1]
    mp, dp_size = lax.axis_size("mp"), lax.axis_size("dp")
    me = lax.axis_index("mp")
    sz = Sizes(mp, samples, n, D)
    rows, block = sz.rows, sz.block

    ids = jnp.arange(n, dtype=jnp.int32)
    pos = jnp.where(ids[None, :] < lengths[:, None], keep_order[:, :n], -1)
    cot = cotangent
    if sz.per > 1:
        order = ((ids // block) ^ lax.rem(me, sz.per)) * block + ids % block
        pos = jnp.take(pos, order, axis=1)
        cot = jnp.take(cot, order, axis=1)
    turned = L - 1 - pos
    pos_wide = jnp.where(pos < 0, -1, turned + turned // grid_side * grid_side)

    def wide_row(a):
        return jnp.pad(a.astype(F32), (0, D - a.shape[0]))

    def by_head(a):
        return jnp.pad(a.reshape(heads, hd), ((0, 0), (0, HEAD_PAD - hd))).reshape(lanes)

    vec = jnp.stack(
        [
            wide_row(by_head(query_value_bias[0])),
            wide_row(by_head(query_value_bias[1])),
            wide_row(merge_output_bias),
            wide_row(up_projection_bias),
            wide_row(down_projection_bias),
            wide_row(bias_modulate),
        ]
    )
    table = bias_table.astype(F32).reshape(heads, offsets, offsets)
    table = jnp.pad(table, ((0, 0), (0, 1), (0, 1))).reshape(heads, 4 * L)
    wide = -(-cols // 128) * 128 + 128
    modw = max(m * cols // 128 * 128 + wide for m in range(mp))
    dma = pltpu.SemaphoreType.DMA

    one = Call()
    one.arg(
        condition=condition,
        vec=vec,
        pos=pos,
        pos_wide=pos_wide,
        w_in=jnp.swapaxes(projection_weight, 1, 2),
        w_out=merge_weight,
        table=table,
    )
    one.arg(pl.ANY, patches=patches, w_mod=w_modulate.T)
    one.out(modv=((samples, 6 * D), F32))
    one.out(
        pl.ANY,
        attn_in=((rows, D), BF16),
        qkv=((rows, 3 * lanes), BF16),
        probs=((samples, heads, n, n), F32),
        att=((rows, lanes), BF16),
        kept=((block, D), F32),
        res=((block, D), F32),
        hidden=((block, D), F32),
        mlp=((block, D), BF16),
        w_qkv=((3 * lanes, D), BF16),
        w_merge=((lanes, D), BF16),
    )
    one.vmem(
        attn_in_v=((rows, D), BF16),
        qkv_v=((rows, 3 * lanes), BF16),
        probs_v=((samples, heads, n, n), F32),
        att_v=((rows, lanes), BF16),
        kept_v=((block, D), F32),
        res_v=((block, D), F32),
        hidden_v=((block, D), F32),
        mlp_v=((block, D), BF16),
        w_qkv_v=((3 * lanes, D), BF16),
        w_merge_v=((lanes, D), BF16),
        w_mod_v=((cols, D), BF16),
        patches_v=((samples, L, D), BF16),
        mod_buf=((mp, samples, wide), F32),
        mod_wide=((samples, modw), F32),
        normed=((rows, D), F32),
        bias_full=((heads, L, 2 * L), BF16),
        part=((rows, D), BF16),
    )
    one.scratch(
        mod_send=dma((mp,)),
        mod_recv=dma((mp,)),
        sem=dma((7,)),
        load_sem=dma((samples,)),
        save_sem=dma((4, samples)),
        red=reduce_scratch(sz),
    )
    first = one.run(
        functools.partial(attention_forward, sz, heads, hd, grid_side, cols), "attention_forward", 0, 62 << 20
    )

    chunk = 48 if dp_size == 4 and F % 48 == 0 and local % 48 == 0 else 0
    two = Call()
    two.arg(condition=condition, vec=vec, pos=pos, pos_wide=pos_wide, modv=first.modv)
    two.arg(
        pl.ANY,
        cot=cot,
        w_up=up_weight.T,
        w_down=down_weight,
        mlp=first.mlp,
        hidden=first.hidden,
        res=first.res,
        kept=first.kept,
        qkv=first.qkv,
        probs=first.probs,
        att=first.att,
        w_qkv=first.w_qkv,
        w_merge=first.w_merge,
        attn_in=first.attn_in,
    )
    both = ((2, F + 2 * local, D), BF16)
    if chunk:
        count = (F + 2 * local) // chunk
        two.out(z_outer=both)
        two.vmem(grads=both, z_inner=((F + 2 * local, D), BF16))
        two.scratch(
            zs=dma((2, count)),
            zo=dma((2, count)),
            zf=dma((count,)),
            zi=dma((count,)),
            zt=dma((3, count)),
            zr=dma((2, count)),
        )
    else:
        two.out(grads=both)
    two.out(
        bias_g=((dp_size, 4, D), F32),
        table_g=((dp_size, heads, 4 * L), F32),
        signal_g=((dp_size, samples, D), BF16),
        mod_g=((dp_size, samples, wide), F32),
    )
    two.out(pl.ANY, out=((samples, n, D), BF16), patch_g=((samples, L, D), BF16))
    two.vmem(
        w_up_v=((F, D), BF16),
        w_down_v=((F, D), BF16),
        mlp_v=((rows, D), BF16),
        d_mlp=((rows, D), BF16),
        slope=((rows, F), F32),
        act=((rows, F), BF16),
        d_pre=((rows, F), BF16),
        part_f=((rows, D), BF16),
        part_b=((rows, D), BF16),
        d_attn=((rows, D), BF16),
        cot_own=((block, D), BF16),
        hidden_v=((block, D), F32),
        res_v=((block, D), F32),
        normed_v=((block, D), F32),
        dh_v=((block, D), F32),
        qkv_v=((rows, 3 * lanes), BF16),
        probs_v=((samples, heads, n, n), F32),
        w_qkv_v=((3 * lanes, D), BF16),
        w_merge_v=((lanes, D), BF16),
        grid_g=((heads, L, 2 * L), F32),
        early=((mp, 4, D), F32),
        late_sums=((mp, 2, D), F32),
        flat=((samples, modw), F32),
    )
    two.scratch(
        sem=dma((13,)),
        load_sem=dma((3, samples)),
        dm_send=dma((2, mp)),
        dm_recv=dma((2, mp)),
        dp_send=dma((4, dp_size)),
        dp_recv=dma((4, dp_size)),
        red_f=reduce_scratch(sz),
        red_b=reduce_scratch(sz),
        last_sems=reduce_scratch(sz)[2:],
        gat_m=gather_scratch(sz),
        gat_d=gather_scratch(sz),
        gat_o=gather_scratch(sz),
        gat_k=gather_scratch(sz),
    )
    got = two.run(
        functools.partial(block_backward, sz, heads, hd, grid_side, cols, dp_size, chunk), "block_backward", 1, 64 << 20
    )

    grads = got.z_outer if chunk else lax.psum(got.grads, "dp")
    up_grad = grads[0, :F].astype(F32).T
    down_grad = grads[1, :F].astype(F32)
    projected = jnp.concatenate([grads[0, F:], grads[1, F + local :]]).reshape(3, local, D)
    project_grad = jnp.swapaxes(projected.astype(F32), 1, 2)
    merge_grad = grads[1, F : F + local].astype(F32)

    signal_all = got.signal_g.reshape(dp_size * samples, D)
    dmod_cols = got.mod_g.reshape(dp_size * samples, wide)
    dmod_cols = lax.dynamic_slice_in_dim(dmod_cols, lax.rem(me * cols, 128), cols, 1)
    upper = lax.reduce_precision(dmod_cols, 8, 7)
    parts = jnp.concatenate([upper, dmod_cols - upper]).astype(BF16)
    modulate_grad = lax.dot_general(
        parts,
        jnp.concatenate([signal_all, signal_all]),
        (((0,), (0,)), ((), ())),
        preferred_element_type=F32,
    ).T
    modulate_bias_grad = jnp.sum(dmod_cols, axis=0)
    biases = jnp.sum(got.bias_g, axis=0)
    proj_bias = biases[3, : 3 * lanes].reshape(3, heads, HEAD_PAD)[:, :, :hd].reshape(3, local)
    proj_bias = jnp.stack([proj_bias[0], proj_bias[2]])
    table_grad = jnp.sum(got.table_g, axis=0).reshape(heads, 2 * grid_side, 2 * grid_side)
    table_grad = table_grad[:, :offsets, :offsets].reshape(heads, offsets * offsets)
    block_out = got.out
    if sz.per > 1:
        block_out = jnp.take(block_out, order, axis=1)
    return (
        block_out,
        got.patch_g.astype(F32),
        project_grad,
        proj_bias,
        merge_grad,
        biases[2],
        up_grad,
        biases[0, :F],
        down_grad,
        biases[1],
        modulate_grad,
        modulate_bias_grad,
        table_grad,
    )


def solution(mesh):
    placed = (
        P("dp", None, None),
        P("dp", None),
        P("dp"),
        P("dp", None),
        P("dp", None, None),
        P(None, None, "mp"),
        P(None, "mp"),
        P("mp", None),
        P(),
        P(None, "mp"),
        P("mp"),
        P("mp", None),
        P(),
        P(None, "mp"),
        P("mp"),
        P("mp", None),
    )
    return jax.shard_map(
        body,
        mesh=mesh,
        in_specs=placed,
        out_specs=(
            P("dp", None, None),
            P("dp", None, None),
            P(None, None, "mp"),
            P(None, "mp"),
            P("mp", None),
            P(),
            P(None, "mp"),
            P("mp"),
            P("mp", None),
            P(),
            P(None, "mp"),
            P("mp"),
            P("mp", None),
        ),
        check_vma=False,
    )
```

time: 744 us -> 236 us (0.32)
  waiting for transfers between devices: 366 us -> 0 us
  Pallas kernels: 0 us -> 198 us
  other arithmetic: 157 us -> 19.6 us
  matrix products: 91.1 us -> 3.63 us
  local copies, waits for them, and re-layouts: 74.6 us -> 12.7 us
  blocking collectives: 35.8 us -> 0 us
  between operations: 14.7 us -> 0.74 us
    psum x4 -> x0, waiting for transfers between devices: 366 us -> none  [the longest x1 140 us: body(): lax.psum(project_grad.astype(jnp.bfloat16), 'dp').astype(jnp.float32)]
    pallas_call x0 -> x2, Pallas kernels: none -> 198 us  [run(): pl.pallas_call(inner, out_shape=list(self.outs.values()), in_specs=self.s...]
    dot_general x27 -> x1, matrix products: 89.2 us -> 3.63 us  [body(): lax.dot_general(parts, jnp.concatenate([signal_all, signal_all]), (((0,),...]
    reduce_sum x11 -> x3, other arithmetic: 60.4 us -> 2.4 us  [the longest x1 1.6 us: body(): modulate_bias_grad = jnp.sum(dmod_cols, axis=0)]
    unnamed x9 -> x0, other arithmetic: 38.7 us -> none
    gather x3 -> x0, local copies, waits for them, and re-layouts: 32.3 us -> none  [body(): jnp.take_along_axis(patches, positions[:, :, None], axis=1)]
    psum x1 -> x0, blocking collectives: 25.1 us -> none  [body(): lax.psum(project_bias_grad.astype(jnp.bfloat16), 'dp').astype(jnp.float32)]
    add x2 -> x0, other arithmetic: 17 us -> none  [the longest x1 17 us: body(): d_hidden_one + layer_back(d_attn_in * (1.0 + scale_one), normed_one, inv_...]
  transfers between devices with their start and end apart: 4 -> 0, of which waited for: 4 -> 0; matrix products, arithmetic and copies ran while one was open for 11% -> 0% of each run, Pallas kernels for 0% -> 0%
where the time goes in v2:
time: 236 us; the launch traced here: 235 us
  Pallas kernels  198 us (84%)
  other arithmetic  19.6 us (8%)
  local copies, waits for them, and re-layouts  12.7 us (5%)
  matrix products  3.63 us (2%)
    pallas_call x2, Pallas kernels, run(): pl.pallas_call(inner, out_shape=list(self.outs.values()), in_specs=self.s...  198 us
    convert_element_type x1, other arithmetic, body(): got.patch_g.astype(F32)  6.72 us

profile of v2, /device:TPU:0, one launch (start us, length us, event | category | flops | bytes accessed | tf_op | source)
XLA Modules:
  0.0 235.1 jit_solution(1458482128093966910)
XLA Ops:
  0.6 0.8 slice_reduce_fusion.3
  1.6 0.7 stack.34
  2.3 0.7 pad.35
  3.0 0.7 stack.36
  3.7 0.7 pad.36
  4.5 0.6 stack.39.refs_1_
  5.1 1.4 fusion.11
  6.5 0.8 reshape.66
  7.3 0.7 reshape.74.refs_6_
  8.0 38.9 %attention_forward.1 = (f32[8,6912]{1,0:T(8,128)}, bf16[1536,1152]{1,0:T(8,128)(2,1)}, bf16[1536,768]{1,0:T(8,128)(2,1)}, f32[8,2,192,192]{3,2,1,0:T(8,128)}, bf...) custom-call(bf16[8,1152]{1,0:T(8,128)(2,1)} %refs_0_.3, ...), custom_call_target="tpu_custom_call" | custom-call | tf_op jit(solution)/shard_map/attention_forward/pallas_call | solution.py:376
  46.8 159.5 %block_backward.1 = (bf16[2,864,1152]{2,1,0:T(8,128)(2,1)}, f32[4,4,1152]{2,1,0:T(4,128)}, f32[4,2,1024]{2,1,0:T(2,128)}, bf16[4,8,1152]{2,1,0:T(8,128)(2,1)}, f...) custom-call(bf16[8,1152]{1,0:T(8,128)(2,1)} %refs_0_.3, ...), custom_call_target="tpu_custom_call" | custom-call | tf_op jit(solution)/shard_map/block_backward/pallas_call | solution.py:376
  206.4 6.7 %convert_element_type.51 = f32[8,256,1152]{2,1,0:T(8,128)} convert(bf16[8,256,1152]{2,1,0:T(8,128)(2,1)} %get-tuple-element.43) | non-fusion elementwise | flops 2359296 | bytes 14155776 | tf_op jit(solution)/shard_map/convert_element_type | solution.py:1429
  213.1 2.0 bitcast_convert_fusion.1
  215.1 1.1 slice_bitcast_fusion
  216.3 1.4 convert_bitcast_fusion.1
  218.6 0.6 slice_reduce_fusion
  219.2 4.4 %bitcast_convert_fusion = (f32[576,1152]{1,0:T(8,128)}, f32[1152,576]{0,1:T(8,128)}) fusion(bf16[2,864,1152]{2,1,0:T(8,128)(2,1)} %get-tuple-element.44), kind=kLoop, calls=%fused_computation.2 | loop fusion | flops 1327104 | bytes 7962624 | tf_op jit(solution)/shard_map/convert_element_type | solution.py:1402
  223.6 1.5 slice_reduce_fusion.2
  225.1 1.6 dynamic-slice_reduce_fusion
  226.7 3.6 %fusion = f32[1152,864]{0,1:T(8,128)} fusion(bf16[32,1152]{1,0:T(8,128)(2,1)} %bitcast.36, bf16[32,864]{1,0:T(8,128)(2,1)S(1)} %get-tuple-element.60, bf16[32,864]{1,0:T(8,128)(2,1)S(1)} %get-tuple-element.61), kind=kOutput, calls=%fused_computation.9 | convolution fusion | flops 127918080 | bytes 4165632 | tf_op jit(solution)/shard_map/dot_general | solution.py:1412
  230.3 0.8 reduce_sum.29
  231.1 0.7 reshape.71
  231.8 1.5 reshape.72
  233.3 1.8 copy.30
  (25 shorter events, 1.2 us)
Async XLA Ops:
  216.2 1.5 copy-start.1
  217.8 1.4 copy-start.2
  223.6 9.6 %copy-start = (bf16[8,192,1152]{2,1,0:T(8,128)(2,1)S(1)}, bf16[8,192,1152]{2,1,0:T(8,128)(2,1)}, u32[]{:S(2)}) copy-start(bf16[8,192,1152]{2,1,0:T(8,128)(2,1)} %get-tuple-element.77) | copy-start | bytes 10616836

commit v3 on v2

--- a/solution.py
+++ b/solution.py
@@ -380,9 +380,9 @@
             out_specs=self.out_specs,
             scratch_shapes=flat,
             name=name,
-            compiler_params=pltpu.CompilerParams(
-                collective_id=cid, has_side_effects=True, vmem_limit_bytes=limit
-            ),
+            compiler_params=pltpu.CompilerParams(vmem_limit_bytes=limit)
+            if cid is None
+            else pltpu.CompilerParams(collective_id=cid, has_side_effects=True, vmem_limit_bytes=limit),
         )(*self.args.values())
         return SimpleNamespace(**dict(zip(self.outs, got)))
 
@@ -599,11 +599,12 @@
             self.r.zt.at[which, k], self.r.zr.at[j, k], to,
         )
 
-    def begin(self, j, k0, k1):
+    def begin(self, halves, k0, k1):
         @pl.when(self.is_outer)
         def _():
             def one(k, carry):
-                self.out_copy(j, k).start()
+                for j in halves:
+                    self.out_copy(j, k).start()
                 return carry
 
             lax.fori_loop(k0, k1, one, 0)
@@ -689,8 +690,8 @@
     grads = r.grads
     sem = r.sem
 
-    per_up, per_local = (F // chunk, local // chunk) if chunk else (0, 0)
-    marks = [0, per_up, per_up + per_local, per_up + 2 * per_local]
+    per_half, per_local = (F // 2 // chunk, local // chunk) if chunk else (0, 0)
+    marks = [0, per_half, 2 * per_half, 2 * per_half + per_local, 2 * per_half + 2 * per_local]
     following = {(number, j): 0 for number in (1, 2, 3) for j in range(2)}
 
     def tick(*steps):
@@ -698,7 +699,7 @@
             return
         for number, j, count in steps:
             k0 = following[number, j]
-            k1 = min(k0 + count, marks[3])
+            k1 = min(k0 + count, marks[4])
             assert number == 1 or k1 <= following[number - 1, j]
             following[number, j] = k1
             if k1 - k0 == 1:
@@ -711,9 +712,9 @@
 
                 lax.fori_loop(k0, k1, one, 0)
 
-    def begin(j, group):
+    def begin(group, *halves):
         if line is not None:
-            line.begin(j, marks[group], marks[group + 1])
+            line.begin(halves or (0, 1), marks[group], marks[group + 1])
 
     def ticks_at(i, plan):
         if line is not None:
@@ -799,20 +800,23 @@
         act[at, :] = active
         slope[at, :] = 0.5 * (1.0 + t) + 0.5 * v * (1.0 - t * t) * (GELU_C * (1.0 + 3.0 * GELU_A * square))
         r.part_f[at, :] = dot(active, w_down[...]).astype(BF16)
-        for k in range(wide):
-            at = pl.ds((slot + k) * n, n)
-            s = xor(mine, slot + k, sbits)
-            load_cot(slot + k).wait()
-            gate = modv[pl.ds(s, 1), 5 * D : 6 * D]
-            live = live_column(pick_rows(r.pos, s, L))
-            dm = (gate * (d_mlp[at, :].astype(F32) * live)).astype(BF16)
-            d_mlp[at, :] = dm
-            down_bg[...] += jnp.sum(dm.astype(F32), axis=0, keepdims=True)
+
+    def output_grad(slot, carry):
+        at = pl.ds(slot * n, n)
+        s = xor(mine, slot, sbits)
+        load_cot(slot).wait()
+        gate = modv[pl.ds(s, 1), 5 * D : 6 * D]
+        live = live_column(pick_rows(r.pos, s, L))
+        dm = (gate * (d_mlp[at, :].astype(F32) * live)).astype(BF16)
+        d_mlp[at, :] = dm
+        down_bg[...] += jnp.sum(dm.astype(F32), axis=0, keepdims=True)
+        return carry
 
     if sz.fast:
         def two_slots(i, carry):
             @pl.when(i == 1)
             def _():
+                lax.fori_loop(0, sz.samples, output_grad, 0)
                 gat_m.step(0)
                 gat_m.step(1)
 
@@ -838,21 +842,24 @@
         for t in range(len(gat_m.stages)):
             gat_m.step(t)
         gat_m.finish()
+        lax.fori_loop(0, sz.samples, output_grad, 0)
         slot_loop(sz, lambda slot: forward(slot, 1), fwd)
 
-    def wide_grad(left, right, half):
+    def wide_grad(left, right, base):
         at = 0
         while at < F:
             size = min(256, F - at)
-            grads[half, at : at + size, :] = dot(left[:, at : at + size], right[...], 0, 0).astype(BF16)
+            value = dot(left[:, at : at + size], right[...], 0, 0).astype(BF16)
+            cut = min(max(F // 2 - at, 0), size)
+            if cut:
+                grads[0, base + at : base + at + cut, :] = value[:cut]
+            if cut < size:
+                start = base + at + cut - F // 2
+                grads[1, start : start + size - cut, :] = value[cut:]
             at += size
 
-    wide_grad(act, d_mlp, 1)
-    begin(1, 0)
-    if sz.fast:
-        fwd.near_add(3)
-        fwd.send(0, 6)
-        fwd.send(1, 6)
+    wide_grad(act, d_mlp, 0)
+    begin(0)
 
     def backward(slot):
         at = pl.ds(slot * n, n)
@@ -862,30 +869,32 @@
         r.part_b[at, :] = dot(dpre, w_up[...]).astype(BF16)
 
     plan = {
-        1: [(1, 1, 1)],
-        2: [(1, 1, 1)],
-        3: [(1, 1, 1)],
-        4: [(1, 1, 1), (2, 1, 1)],
-        5: [(1, 1, 1), (2, 1, 1)],
-        6: [(1, 1, 1), (2, 1, 1)],
-        7: [(1, 1, 1), (2, 1, 1)],
+        4: [(1, 0, 1), (1, 1, 1)],
+        6: [(1, 1, 1), (2, 0, 1), (2, 1, 1)],
+        7: [(1, 0, 1)],
     }
 
-    slot_loop(sz, backward, bwd, lambda i: ticks_at(i, plan))
+    def bwd_extra(i):
+        ticks_at(i, plan)
+
+        @pl.when(i == 5)
+        def _():
+            fwd.near_add(3)
+            fwd.send(0, 6)
+            fwd.send(1, 6)
+
+    slot_loop(sz, backward, bwd, bwd_extra)
     load_attn.start()
     load_att.start()
-    wide_grad(d_pre, mlp, 0)
-    begin(0, 0)
-    tick((1, 1, 1), (2, 1, 1), (3, 1, 2))
+    wide_grad(d_pre, mlp, F // 2)
+    begin(1)
+    tick((1, 1, 1), (2, 1, 1))
     for copy in loads:
         copy.wait()
     normed2, inv2 = layer_stats(r.hidden_v[...])
     r.normed_v[...] = normed2
-    if sz.fast:
-        fwd.take(1, *sz.sends[1, 0][1])
-        fwd.take(0, *sz.sends[0, 0][1])
     bwd.close()
-    tick((1, 1, 1), (2, 1, 1), (3, 1, 1))
+    tick((1, 0, 1), (1, 1, 1), (2, 0, 1), (2, 1, 1), (3, 0, 1), (3, 1, 2))
 
     mrow = pl.ds(mine, 1)
     live = live_column(pick_rows(r.pos, mine, L)[:, :block])
@@ -896,6 +905,7 @@
     r.dh_v[...] = dh
     r.d_attn[:block, :] = (modv[mrow, 2 * D : 3 * D] * dh).astype(BF16)
     gat_d.start()
+    tick((1, 0, 1))
 
     early, late_sums = r.early, r.late_sums
     early[me, 0:1, :] = jnp.sum(dh * r.res_v[...], axis=0, keepdims=True)
@@ -920,8 +930,6 @@
             device_id=(dp, flip(me, d)),
             device_id_type=MESH,
         )
-
-    tick((1, 1, 1))
 
     def attention_grad(c, half, at):
         if c < 3:
@@ -966,13 +974,13 @@
         r.part_b[at, :] = dot(joined, w_qkv[...]).astype(BF16)
 
     if sz.fast:
-        plan_one = {1: [(1, 1, 1), (2, 1, 2), (3, 1, 2)], 2: [(1, 1, 1), (2, 1, 1), (3, 1, 2)]}
+        plan_one = {1: [(2, 0, 1), (2, 1, 1)], 2: [(1, 0, 1), (1, 1, 1), (3, 0, 1), (3, 1, 1)]}
         plan_two = {
-            3: [(1, 0, 2)],
-            4: [(1, 0, 1), (2, 0, 1), (3, 1, 1)],
-            5: [(1, 0, 2), (2, 0, 1), (3, 1, 1)],
+            3: [(1, 0, 1), (1, 1, 1), (2, 0, 2), (2, 1, 1), (3, 0, 1)],
+            4: [(1, 0, 1), (1, 1, 1), (3, 1, 1)],
+            5: [(1, 1, 1), (2, 0, 1), (2, 1, 1), (3, 0, 1)],
             6: [(1, 0, 1), (2, 0, 1), (3, 0, 1), (3, 1, 1)],
-            7: [(1, 0, 1), (2, 0, 1), (3, 0, 1)],
+            7: [(1, 0, 1), (1, 1, 1), (2, 1, 1), (3, 1, 1)],
         }
 
         def one(i, carry):
@@ -990,11 +998,13 @@
             @pl.when(i == 2)
             def _():
                 gat_d.step(0)
-                tick((2, 1, 1), (3, 1, 1))
+                tick((2, 0, 1), (3, 0, 1))
                 gat_d.step(1)
+                fwd.take(1, *sz.sends[1, 0][1])
+                fwd.take(0, *sz.sends[0, 0][1])
                 fwd.send(1, 2)
                 fwd.send(0, 4)
-                tick((2, 1, 2), (1, 0, 2), (3, 1, 1))
+                tick((1, 0, 1), (1, 1, 1), (2, 1, 1), (3, 1, 1))
                 for h in range(2):
                     gat_d.near_copy(2, h).wait()
 
@@ -1041,7 +1051,7 @@
             return carry
 
         lax.fori_loop(0, 8, one, 0)
-        tick((1, 0, 1), (2, 0, 1), (3, 0, 1))
+        tick((1, 1, 1), (2, 0, 1), (2, 1, 1), (3, 0, 1))
     else:
         for t in range(len(gat_d.stages)):
             gat_d.step(t)
@@ -1052,15 +1062,15 @@
     load_attn.wait()
     load_att.wait()
     attention_grad(3, 1, F)
-    begin(1, 1)
+    begin(2, 1)
     tick((1, 0, 1), (2, 0, 1))
     attention_grad(0, 0, F)
-    begin(0, 1)
+    begin(2, 0)
     attention_grad(2, 1, F + local)
-    begin(1, 2)
+    begin(3, 1)
     attention_grad(1, 0, F + local)
-    begin(0, 2)
-    tick((1, 0, 1), (2, 0, 1), (3, 0, 2))
+    begin(3, 0)
+    tick((1, 1, 1), (2, 1, 1), (3, 0, 1), (3, 1, 1))
 
     tables = r.table_g
     span = tables.shape[2]
@@ -1086,14 +1096,14 @@
     normed1, inv1 = layer_stats(r.res_v[...])
     r.normed_v[...] = normed1
     last.close()
-    tick((2, 0, 2), (3, 0, 1), (1, 1, 2))
+    tick((1, 0, 1), (1, 1, 1), (2, 0, 1), (2, 1, 1), (3, 1, 1))
     d_in = last.own_sum()
     g = d_in * (1.0 + modv[mrow, D : 2 * D])
     mlp[:block, :] = (r.dh_v[...] + layer_back(g, r.normed_v[...], inv1)).astype(BF16)
     late_sums[me, 0:1, :] = jnp.sum(d_in, axis=0, keepdims=True)
     late_sums[me, 1:2, :] = jnp.sum(d_in * r.normed_v[...], axis=0, keepdims=True)
     gat_k.start()
-    tick((2, 0, 1), (1, 1, 1), (3, 0, 1))
+    tick((1, 1, 2), (3, 0, 1), (3, 1, 1))
 
     def out_copy(slot):
         return pltpu.make_async_copy(
@@ -1128,16 +1138,16 @@
         dm_copy(early, 0, d, me).start()
         dm_copy(late_sums, 1, d, me).start()
     gat_o.start()
-    tick((2, 0, 2), (1, 0, 2), (3, 0, 2), (2, 1, 1))
+    tick((2, 0, 1), (2, 1, 2), (3, 0, 1), (3, 1, 1))
     gat_k.step(1)
-    tick((1, 0, 1), (1, 1, 1), (2, 1, 2), (2, 0, 1), (3, 0, 3))
+    tick((1, 0, 2), (1, 1, 1), (3, 0, 1), (3, 1, 1))
     if sz.fast:
         for d in (2, 4):
             for h in range(2):
                 gat_k.near_copy(d, h).wait()
         lax.fori_loop(2, 6, patch, 0)
         gat_k.step(2)
-        tick((1, 1, 2), (2, 0, 2), (3, 1, 2))
+        tick((1, 0, 1), (1, 1, 1), (2, 0, 1), (2, 1, 2), (3, 1, 1))
         for h in range(2):
             gat_k.near_copy(6, h).wait()
         lax.fori_loop(6, 8, patch, 0)
@@ -1163,18 +1173,22 @@
     base = pl.multiple_of(me * cols // 128 * 128, 128)
     mod_g[dp] = flat[:, pl.ds(base, mod_g.shape[2])]
     share(2)
-    tick((1, 0, 1), (2, 0, 1))
+    tick((1, 1, 1), (2, 0, 1), (2, 1, 1), (3, 0, 1))
+    tick((2, 0, 1), (2, 1, 1))
     gat_o.step(0)
-    tick((1, 0, 1), (2, 1, 1), (3, 1, 1), (3, 0, 1))
+    tick((1, 0, 1), (3, 1, 1), (3, 0, 1), (1, 0, 1))
+    tick((3, 1, 1), (2, 1, 1))
     gat_o.step(1)
-    tick((2, 1, 1), (1, 0, 1), (3, 0, 1))
+    tick((1, 0, 1), (3, 1, 1), (3, 0, 1), (3, 1, 1))
+    tick((3, 0, 1), (2, 0, 1))
     for t in range(2, len(gat_o.stages)):
         gat_o.step(t)
     gat_o.finish()
     lax.fori_loop(0, sz.samples, start_out, 0)
-    tick((2, 1, 1), (3, 0, 1), (2, 0, 1), (3, 1, 1), (2, 0, 1), (3, 1, 1), (2, 0, 1), (3, 1, 1), (3, 0, 3))
+    tick((2, 0, 1), (3, 0, 1), (3, 1, 1), (3, 0, 1))
+    tick((2, 0, 1), (3, 0, 1))
     if line is not None:
-        assert all(k == marks[3] for k in following.values()), following
+        assert all(k == marks[4] for k in following.values()), following
     for k in range(4):
         for e in range(1, dp_size):
             dp_copy(k, e, dp).wait_send()
@@ -1189,6 +1203,85 @@
     lax.fori_loop(0, sz.samples, wait_out, 0)
     if line is not None:
         line.finish()
+
+
+def write_results(cols, r):
+    total = r.total
+    F, local = r.up.shape[0], r.merge.shape[0]
+    D = total.shape[2]
+    depth = r.narrow.shape[0]
+    samples = r.out.shape[0]
+
+    def out_in(s):
+        return pltpu.make_async_copy(r.out.at[s], r.out_v.at[s], r.out_sem.at[0, s])
+
+    def out_back(s):
+        return pltpu.make_async_copy(r.out_v.at[s], r.block_out.at[s], r.out_sem.at[1, s])
+
+    jobs = []
+    for s in range(samples):
+        jobs.append((r.patch_g.at[s], r.patch.at[s], r.patch.shape[1]))
+    rows_most = r.narrow.shape[1]
+
+    def add(half, start, to, at, count):
+        while count:
+            size = min(rows_most, count)
+            jobs.append((total.at[half, pl.ds(start, size)], to.at[pl.ds(at, size)], size))
+            start, at, count = start + size, at + size, count - size
+
+    for half in range(2):
+        add(half, 0, r.down, half * (F // 2), F // 2)
+        add(half, F // 2, r.up, half * (F // 2), F // 2)
+    add(0, F, r.project, 0, 2 * local)
+    add(1, F + local, r.project, 2 * local, local)
+    add(1, F, r.merge, 0, local)
+
+    def load(k):
+        src, _, size = jobs[k]
+        return pltpu.make_async_copy(src, r.narrow.at[k % depth, pl.ds(0, size)], r.load_sem.at[k % depth])
+
+    def save(k):
+        _, dst, size = jobs[k]
+        return pltpu.make_async_copy(r.wide.at[k % depth, pl.ds(0, size)], dst, r.save_sem.at[k % depth])
+
+    for k in range(depth):
+        load(k).start()
+    for s in range(samples):
+        out_in(s).start()
+
+    members, _, width = r.mod_g.shape
+    shift = lax.rem(lax.axis_index("mp") * cols, 128)
+    dmod = jnp.concatenate([r.mod_g[m] for m in range(members)], axis=0)
+    dmod = pltpu.roll(dmod, lax.rem(width - shift, width), 1)
+    upper = dmod.astype(BF16)
+    parts = jnp.concatenate([upper, (dmod - upper.astype(F32)).astype(BF16)], axis=0)
+    signal = jnp.concatenate([r.signal_g[m].astype(F32) for m in range(members)], axis=0).astype(BF16)
+    r.mod_v[...] = dot(parts, jnp.concatenate([signal, signal], axis=0), 0, 0)[:cols]
+    modulate = pltpu.make_async_copy(r.mod_v, r.modulate, r.sem.at[0])
+    modulate.start()
+    r.mod_bias[...] = jnp.sum(dmod, axis=0, keepdims=True)
+    bias, table = r.bias_g[0], r.table_g[0]
+    for m in range(1, members):
+        bias, table = bias + r.bias_g[m], table + r.table_g[m]
+    r.bias[...] = bias
+    r.table[...] = table
+
+    for k, (_, _, size) in enumerate(jobs):
+        load(k).wait()
+        if k >= depth:
+            save(k - depth).wait()
+        r.wide[k % depth, :size] = r.narrow[k % depth, :size].astype(F32)
+        save(k).start()
+        if k + depth < len(jobs):
+            load(k + depth).start()
+        if k < samples:
+            out_in(k).wait()
+            out_back(k).start()
+    for k in range(max(0, len(jobs) - depth), len(jobs)):
+        save(k).wait()
+    for s in range(samples):
+        out_back(s).wait()
+    modulate.wait()
 
 
 def body(
@@ -1312,7 +1405,7 @@
         functools.partial(attention_forward, sz, heads, hd, grid_side, cols), "attention_forward", 0, 62 << 20
     )
 
-    chunk = 48 if dp_size == 4 and F % 48 == 0 and local % 48 == 0 else 0
+    chunk = 48 if dp_size == 4 and F % 96 == 0 and local % 48 == 0 else 0
     two = Call()
     two.arg(condition=condition, vec=vec, pos=pos, pos_wide=pos_wide, modv=first.modv)
     two.arg(
@@ -1397,46 +1490,46 @@
         functools.partial(block_backward, sz, heads, hd, grid_side, cols, dp_size, chunk), "block_backward", 1, 64 << 20
     )
 
-    grads = got.z_outer if chunk else lax.psum(got.grads, "dp")
-    up_grad = grads[0, :F].astype(F32).T
-    down_grad = grads[1, :F].astype(F32)
-    projected = jnp.concatenate([grads[0, F:], grads[1, F + local :]]).reshape(3, local, D)
-    project_grad = jnp.swapaxes(projected.astype(F32), 1, 2)
-    merge_grad = grads[1, F : F + local].astype(F32)
-
-    signal_all = got.signal_g.reshape(dp_size * samples, D)
-    dmod_cols = got.mod_g.reshape(dp_size * samples, wide)
-    dmod_cols = lax.dynamic_slice_in_dim(dmod_cols, lax.rem(me * cols, 128), cols, 1)
-    upper = lax.reduce_precision(dmod_cols, 8, 7)
-    parts = jnp.concatenate([upper, dmod_cols - upper]).astype(BF16)
-    modulate_grad = lax.dot_general(
-        parts,
-        jnp.concatenate([signal_all, signal_all]),
-        (((0,), (0,)), ((), ())),
-        preferred_element_type=F32,
-    ).T
-    modulate_bias_grad = jnp.sum(dmod_cols, axis=0)
-    biases = jnp.sum(got.bias_g, axis=0)
-    proj_bias = biases[3, : 3 * lanes].reshape(3, heads, HEAD_PAD)[:, :, :hd].reshape(3, local)
-    proj_bias = jnp.stack([proj_bias[0], proj_bias[2]])
-    table_grad = jnp.sum(got.table_g, axis=0).reshape(heads, 2 * grid_side, 2 * grid_side)
-    table_grad = table_grad[:, :offsets, :offsets].reshape(heads, offsets * offsets)
-    block_out = got.out
+    total = got.z_outer if chunk else lax.psum(got.grads, "dp")
+    three = Call()
+    three.arg(mod_g=got.mod_g, signal_g=got.signal_g, bias_g=got.bias_g, table_g=got.table_g)
+    three.arg(pl.ANY, total=total, out=got.out, patch_g=got.patch_g)
+    three.out(mod_bias=((1, wide), F32), bias=((4, D), F32), table=((heads, 4 * L), F32))
+    three.out(
+        pl.ANY,
+        block_out=((samples, n, D), BF16),
+        patch=((samples, L, D), F32),
+        up=((F, D), F32),
+        down=((F, D), F32),
+        project=((3 * local, D), F32),
+        merge=((local, D), F32),
+        modulate=((cols, D), F32),
+    )
+    depth = 4
+    three.vmem(narrow=((depth, 288, D), BF16), wide=((depth, 288, D), F32), mod_v=((cols, D), F32), out_v=((samples, n, D), BF16))
+    three.scratch(sem=dma((1,)), out_sem=dma((2, samples)), load_sem=dma((depth,)), save_sem=dma((depth,)))
+    end = three.run(functools.partial(write_results, cols), "write_results", None, 63 << 20)
+
+    block_out = end.block_out
     if sz.per > 1:
         block_out = jnp.take(block_out, order, axis=1)
+    proj_bias = end.bias[3, : 3 * lanes].reshape(3, heads, HEAD_PAD)[:, :, :hd].reshape(3, local)
+    proj_bias = jnp.stack([proj_bias[0], proj_bias[2]])
+    table_grad = end.table.reshape(heads, 2 * grid_side, 2 * grid_side)
+    table_grad = table_grad[:, :offsets, :offsets].reshape(heads, offsets * offsets)
     return (
         block_out,
-        got.patch_g.astype(F32),
-        project_grad,
+        end.patch,
+        jnp.swapaxes(end.project.reshape(3, local, D), 1, 2),
         proj_bias,
-        merge_grad,
-        biases[2],
-        up_grad,
-        biases[0, :F],
-        down_grad,
-        biases[1],
-        modulate_grad,
-        modulate_bias_grad,
+        end.merge,
+        end.bias[2],
+        end.up.T,
+        end.bias[0, :F],
+        end.down,
+        end.bias[1],
+        end.modulate.T,
+        end.mod_bias[0, :cols],
         table_grad,
     )
 

time: 236 us -> 219 us (0.928)
  other arithmetic: 19.6 us -> 2.59 us
  Pallas kernels: 198 us -> 203 us
  matrix products: 3.63 us -> 0 us
    convert_element_type x3 -> x0, other arithmetic: 13.1 us -> none  [the longest x1 6.72 us: body(): got.patch_g.astype(F32)]
    pallas_call x2 -> x3, Pallas kernels: 198 us -> 203 us  [run(): pl.pallas_call(inner, out_shape=list(self.outs.values()), in_specs=self.s...]
    dot_general x1 -> x0, matrix products: 3.63 us -> none  [body(): lax.dot_general(parts, jnp.concatenate([signal_all, signal_all]), (((0,),...]
    slice x3 -> x4, local copies, waits for them, and re-layouts: 2.09 us -> 4.74 us  [the longest x1 1.43 us: body(): end.bias[1]]
    reduce_sum x3 -> x0, other arithmetic: 2.4 us -> none  [the longest x1 1.6 us: body(): modulate_bias_grad = jnp.sum(dmod_cols, axis=0)]
where the time goes in v3:
time: 219 us; the launch traced here: 218 us
  Pallas kernels  203 us (93%)
  local copies, waits for them, and re-layouts  11.7 us (5%)
  other arithmetic  2.59 us (1%)
    pallas_call x3, Pallas kernels, run(): pl.pallas_call(inner, out_shape=list(self.outs.values()), in_specs=self.s...  203 us

profile of v3, /device:TPU:0, one launch (start us, length us, event | category | flops | bytes accessed | tf_op | source)
XLA Modules:
  0.0 218.4 jit_solution(15442649347848108033)
XLA Ops:
  0.6 0.8 slice_reduce_fusion.4
  1.4 0.1 reshape_squeeze.10
  1.5 0.1 reshape_squeeze.9
  1.7 0.7 pad.35
  2.4 0.7 pad.36
  3.0 0.7 stack.34
  3.7 0.7 stack.36
  4.4 0.1 stack.38
  4.5 0.8 reshape.54
  5.3 0.7 reshape.61.refs_6_
  6.0 1.4 fusion.3
  7.4 0.6 stack.39.refs_1_
  8.0 38.9 %attention_forward.1 = (f32[8,6912]{1,0:T(8,128)}, bf16[1536,1152]{1,0:T(8,128)(2,1)}, bf16[1536,768]{1,0:T(8,128)(2,1)}, f32[8,2,192,192]{3,2,1,0:T(8,128)}, bf...) custom-call(bf16[8,1152]{1,0:T(8,128)(2,1)} %refs_0_.3, ...), custom_call_target="tpu_custom_call" | custom-call | tf_op jit(solution)/shard_map/attention_forward/pallas_call | solution.py:376
  46.9 150.5 %block_backward.1 = (bf16[2,864,1152]{2,1,0:T(8,128)(2,1)}, f32[4,4,1152]{2,1,0:T(4,128)}, f32[4,2,1024]{2,1,0:T(2,128)}, bf16[4,8,1152]{2,1,0:T(8,128)(2,1)}, f...) custom-call(bf16[8,1152]{1,0:T(8,128)(2,1)} %refs_0_.3, ...), custom_call_target="tpu_custom_call" | custom-call | tf_op jit(solution)/shard_map/block_backward/pallas_call | solution.py:376
  197.5 13.9 %write_results.1 = (f32[1,1024]{1,0:T(1,128)}, f32[4,1152]{1,0:T(4,128)}, f32[2,1024]{1,0:T(2,128)}, bf16[8,192,1152]{2,1,0:T(8,128)(2,1)}, f32[8,256,1152]{2,1,...) custom-call(f32[4,8,1024]{2,1,0:T(8,128)} %get-tuple-element.52.refs, ...), custom_call_target="tpu_custom_call" | custom-call | tf_op jit(solution)/shard_map/write_results/pallas_call | solution.py:376
  211.4 0.7 slice.45
  212.1 0.1 slice.47
  212.2 0.1 slice.49
  212.3 0.6 pad_maximum_fusion
  212.9 1.3 slice_reduce_fusion.2
  214.2 1.3 slice_reduce_fusion.3
  215.5 1.4 slice_reduce_fusion
  216.9 0.8 reshape.58
  217.7 0.7 reshape.59
  (10 shorter events, 0.1 us)

commit v4 on v3

--- a/solution.py
+++ b/solution.py
@@ -4,7 +4,6 @@
 
 import jax
 import jax.numpy as jnp
-import numpy as np
 from jax import lax
 from jax.experimental import pallas as pl
 from jax.experimental.pallas import tpu as pltpu
@@ -334,6 +333,21 @@
     return (lax.broadcasted_iota(jnp.int32, (count, ids.shape[1]), 0) == ids).astype(F32).astype(BF16)
 
 
+def spread(row, pieces, size, step):
+    width = row.shape[1]
+    lane = lax.broadcasted_iota(jnp.int32, row.shape, 1)
+    total = jnp.zeros_like(row)
+    for p in range(pieces):
+        start = p * (size + step) if step > 0 else p * size
+        moved = pltpu.roll(row, (p * step) % width, 1) if p else row
+        total = jnp.where((lane >= start) & (lane < start + size), moved, total)
+    return total
+
+
+def spread_heads(row, heads, hd):
+    return spread(row, heads, hd, HEAD_PAD - hd)
+
+
 def live_column(sel):
     ones = jnp.ones((sel.shape[0], 128), BF16)
     return dot(sel, ones, 0, 0)[:, 0:1]
@@ -394,7 +408,7 @@
     D, n, L = sz.width, sz.slots, grid_side * grid_side
     lanes = heads * HEAD_PAD
     red = Reduce(sz, r.part, r.red)
-    mod_buf, mod_wide, modv, vec = r.mod_buf, r.mod_wide, r.modv, r.vec
+    mod_buf, mod_wide, modv = r.mod_buf, r.mod_wide, r.modv
     wide = mod_buf.shape[2]
     sem = r.sem
 
@@ -409,11 +423,24 @@
         return carry
 
     lax.fori_loop(0, sz.samples, start_load, 0)
+    slots = lax.broadcasted_iota(jnp.int32, (1, n), 1)
+    for s in range(sz.samples):
+        pos = jnp.where(slots < r.lengths[s], r.keep[s : s + 1, 0:n], -1)
+        r.pos[s : s + 1, :] = pos
+        turned = L - 1 - pos
+        r.pos_wide[s : s + 1, :] = jnp.where(pos < 0, -1, turned + turned // grid_side * grid_side)
+    r.qv_wide[...] = jnp.zeros_like(r.qv_wide)
+    r.qv_wide[:, 0 : heads * hd] = r.b_qv[...].astype(F32)
+    r.qv_wide[...] = spread_heads(r.qv_wide[...], heads, hd)
+    r.table_v[...] = jnp.zeros_like(r.table_v)
+    offsets = 2 * grid_side - 1
+    r.table_v[:, 0 : offsets * offsets] = r.b_table[...].astype(F32)
+    r.table_v[...] = spread(r.table_v[...], offsets, offsets, 1)
     cond = r.condition[...].astype(F32)
     signal = (cond / (1.0 + jnp.exp(-cond))).astype(BF16)
     mod_buf[me] = jnp.zeros((sz.samples, wide), F32)
     load_mod.wait()
-    mod_buf[me, :, 0:cols] = dot(signal, r.w_mod_v[...], 1, 1) + vec[5:6, 0:cols]
+    mod_buf[me, :, 0:cols] = dot(signal, r.w_mod_v[...], 1, 1) + r.b_mod[...].astype(F32).reshape(1, cols)
     enter(sz)
 
     def mod_copy(d, slot):
@@ -447,9 +474,9 @@
         copy.start()
 
     bias_full = r.bias_full
-    span = r.table.shape[1]
+    span = r.table_v.shape[1]
     for h in range(heads):
-        line = r.table[h : h + 1, :]
+        line = r.table_v[h : h + 1, :]
         strip = jnp.concatenate([line] + [pltpu.roll(line, span - c, 1) for c in range(1, grid_side)], axis=0)
         for row in range(grid_side):
             rolled = pltpu.roll(strip, span - row * 2 * grid_side, 1) if row else strip
@@ -506,9 +533,9 @@
         entry = (normed[at, :] * (1.0 + scale) + shift).astype(BF16)
         r.attn_in_v[at, :] = entry
         proj = dot(entry, w_qkv[...], 1, 1)
-        qs = (proj[:, :lanes] + vec[0:1, :lanes]).astype(BF16)
+        qs = (proj[:, :lanes] + r.qv_wide[0:1, :]).astype(BF16)
         ks = proj[:, lanes : 2 * lanes].astype(BF16)
-        vs = (proj[:, 2 * lanes :] + vec[1:2, :lanes]).astype(BF16)
+        vs = (proj[:, 2 * lanes :] + r.qv_wide[1:2, :]).astype(BF16)
         r.qkv_v[at, 0:lanes] = qs
         r.qkv_v[at, lanes : 2 * lanes] = ks
         r.qkv_v[at, 2 * lanes :] = vs
@@ -533,7 +560,7 @@
 
     slot_loop(sz, body, red)
     red.close()
-    result = red.own_sum() + vec[2:3, :D]
+    result = red.own_sum() + r.b_merge[...].astype(F32).reshape(1, D)
     r.res_v[...] = result
     hidden = kept_own[...] + modv[pl.ds(mine, 1), 2 * D : 3 * D] * result
     r.hidden_v[...] = hidden
@@ -678,7 +705,7 @@
     local = heads * hd
     F = r.w_up_v.shape[0]
     block = sz.block
-    vec, modv = r.vec, r.modv
+    modv = r.modv
     fwd = Reduce(sz, r.part_f, r.red_f)
     bwd = Reduce(sz, r.part_b, r.red_b)
     last = Reduce(sz, r.part_b, r.red_b[:2] + r.last_sems)
@@ -763,6 +790,8 @@
     pl.semaphore_wait(barrier, sz.mp + dp_size - 2)
     load_own.wait()
     gat_m.start()
+    r.bias_v[0:1, 0:F] = r.b_up[...].astype(F32).reshape(1, F)
+    r.bias_v[1:2, :] = r.b_down[...].astype(F32).reshape(1, D)
     load_up.wait()
     load_down.wait()
     w_up, w_down, mlp = r.w_up_v, r.w_down_v, r.mlp_v
@@ -793,7 +822,7 @@
 
     def forward(slot, wide):
         at = pl.ds(slot * n, wide * n)
-        v = dot(mlp[at, :], w_up[...], 1, 1) + vec[3:4, :F]
+        v = dot(mlp[at, :], w_up[...], 1, 1) + r.bias_v[0:1, 0:F]
         square = v * v
         t = jnp.tanh(GELU_C * (v + GELU_A * v * square))
         active = (0.5 * v * (1.0 + t)).astype(BF16)
@@ -916,7 +945,7 @@
     def finish_out():
         fwd.close()
         live = live_column(pick_rows(r.pos, mine, L)[:, :block])
-        mlp_out = fwd.own_sum() + vec[4:5, :D]
+        mlp_out = fwd.own_sum() + r.bias_v[1:2, :]
         early[me, 3:4, :] = jnp.sum(mlp_out * (r.cot_own[...].astype(F32) * live), axis=0, keepdims=True)
         out_own = (r.hidden_v[...] + modv[mrow, 5 * D : 6 * D] * mlp_out) * live
         r.part_f[:block, :] = out_own.astype(BF16)
@@ -1205,7 +1234,7 @@
         line.finish()
 
 
-def write_results(cols, r):
+def write_results(heads, hd, grid_side, cols, r):
     total = r.total
     F, local = r.up.shape[0], r.merge.shape[0]
     D = total.shape[2]
@@ -1259,12 +1288,19 @@
     r.mod_v[...] = dot(parts, jnp.concatenate([signal, signal], axis=0), 0, 0)[:cols]
     modulate = pltpu.make_async_copy(r.mod_v, r.modulate, r.sem.at[0])
     modulate.start()
-    r.mod_bias[...] = jnp.sum(dmod, axis=0, keepdims=True)
+    r.mod_bias[...] = jnp.sum(dmod, axis=0, keepdims=True)[:, :cols].reshape(cols)
     bias, table = r.bias_g[0], r.table_g[0]
     for m in range(1, members):
         bias, table = bias + r.bias_g[m], table + r.table_g[m]
-    r.bias[...] = bias
-    r.table[...] = table
+    r.up_bias[...] = bias[0:1, :F].reshape(F)
+    r.down_bias[...] = bias[1:2].reshape(D)
+    r.merge_bias[...] = bias[2:3].reshape(D)
+    lanes = heads * HEAD_PAD
+    for k, c in enumerate((0, 2)):
+        row = spread(bias[3:4, c * lanes : (c + 1) * lanes], heads, hd, hd - HEAD_PAD)
+        r.proj_bias[k : k + 1, :] = row[:, : heads * hd]
+    offsets = 2 * grid_side - 1
+    r.table[...] = spread(table, offsets, offsets, -1)[:, : offsets * offsets]
 
     for k, (_, _, size) in enumerate(jobs):
         load(k).wait()
@@ -1317,34 +1353,13 @@
     sz = Sizes(mp, samples, n, D)
     rows, block = sz.rows, sz.block
 
-    ids = jnp.arange(n, dtype=jnp.int32)
-    pos = jnp.where(ids[None, :] < lengths[:, None], keep_order[:, :n], -1)
-    cot = cotangent
+    keep, counts, cot = keep_order, lengths, cotangent
     if sz.per > 1:
+        ids = jnp.arange(n, dtype=jnp.int32)
         order = ((ids // block) ^ lax.rem(me, sz.per)) * block + ids % block
-        pos = jnp.take(pos, order, axis=1)
+        keep = jnp.take(jnp.where(ids[None, :] < lengths[:, None], keep_order[:, :n], -1), order, axis=1)
+        counts = jnp.full_like(lengths, n)
         cot = jnp.take(cot, order, axis=1)
-    turned = L - 1 - pos
-    pos_wide = jnp.where(pos < 0, -1, turned + turned // grid_side * grid_side)
-
-    def wide_row(a):
-        return jnp.pad(a.astype(F32), (0, D - a.shape[0]))
-
-    def by_head(a):
-        return jnp.pad(a.reshape(heads, hd), ((0, 0), (0, HEAD_PAD - hd))).reshape(lanes)
-
-    vec = jnp.stack(
-        [
-            wide_row(by_head(query_value_bias[0])),
-            wide_row(by_head(query_value_bias[1])),
-            wide_row(merge_output_bias),
-            wide_row(up_projection_bias),
-            wide_row(down_projection_bias),
-            wide_row(bias_modulate),
-        ]
-    )
-    table = bias_table.astype(F32).reshape(heads, offsets, offsets)
-    table = jnp.pad(table, ((0, 0), (0, 1), (0, 1))).reshape(heads, 4 * L)
     wide = -(-cols // 128) * 128 + 128
     modw = max(m * cols // 128 * 128 + wide for m in range(mp))
     dma = pltpu.SemaphoreType.DMA
@@ -1352,15 +1367,17 @@
     one = Call()
     one.arg(
         condition=condition,
-        vec=vec,
-        pos=pos,
-        pos_wide=pos_wide,
+        keep=keep,
+        b_qv=query_value_bias,
+        b_merge=merge_output_bias,
+        b_mod=bias_modulate,
+        b_table=bias_table,
         w_in=jnp.swapaxes(projection_weight, 1, 2),
         w_out=merge_weight,
-        table=table,
     )
+    one.arg(pltpu.SMEM, lengths=counts)
     one.arg(pl.ANY, patches=patches, w_mod=w_modulate.T)
-    one.out(modv=((samples, 6 * D), F32))
+    one.out(modv=((samples, 6 * D), F32), pos=((samples, n), jnp.int32), pos_wide=((samples, n), jnp.int32))
     one.out(
         pl.ANY,
         attn_in=((rows, D), BF16),
@@ -1389,6 +1406,8 @@
         patches_v=((samples, L, D), BF16),
         mod_buf=((mp, samples, wide), F32),
         mod_wide=((samples, modw), F32),
+        qv_wide=((2, lanes), F32),
+        table_v=((heads, 4 * L), F32),
         normed=((rows, D), F32),
         bias_full=((heads, L, 2 * L), BF16),
         part=((rows, D), BF16),
@@ -1407,7 +1426,14 @@
 
     chunk = 48 if dp_size == 4 and F % 96 == 0 and local % 48 == 0 else 0
     two = Call()
-    two.arg(condition=condition, vec=vec, pos=pos, pos_wide=pos_wide, modv=first.modv)
+    two.arg(
+        condition=condition,
+        b_up=up_projection_bias,
+        b_down=down_projection_bias,
+        pos=first.pos,
+        pos_wide=first.pos_wide,
+        modv=first.modv,
+    )
     two.arg(
         pl.ANY,
         cot=cot,
@@ -1470,6 +1496,7 @@
         early=((mp, 4, D), F32),
         late_sums=((mp, 2, D), F32),
         flat=((samples, modw), F32),
+        bias_v=((2, D), F32),
     )
     two.scratch(
         sem=dma((13,)),
@@ -1494,7 +1521,14 @@
     three = Call()
     three.arg(mod_g=got.mod_g, signal_g=got.signal_g, bias_g=got.bias_g, table_g=got.table_g)
     three.arg(pl.ANY, total=total, out=got.out, patch_g=got.patch_g)
-    three.out(mod_bias=((1, wide), F32), bias=((4, D), F32), table=((heads, 4 * L), F32))
+    three.out(
+        mod_bias=((cols,), F32),
+        up_bias=((F,), F32),
+        down_bias=((D,), F32),
+        merge_bias=((D,), F32),
+        proj_bias=((2, local), F32),
+        table=((heads, offsets * offsets), F32),
+    )
     three.out(
         pl.ANY,
         block_out=((samples, n, D), BF16),
@@ -1508,29 +1542,25 @@
     depth = 4
     three.vmem(narrow=((depth, 288, D), BF16), wide=((depth, 288, D), F32), mod_v=((cols, D), F32), out_v=((samples, n, D), BF16))
     three.scratch(sem=dma((1,)), out_sem=dma((2, samples)), load_sem=dma((depth,)), save_sem=dma((depth,)))
-    end = three.run(functools.partial(write_results, cols), "write_results", None, 63 << 20)
+    end = three.run(functools.partial(write_results, heads, hd, grid_side, cols), "write_results", None, 63 << 20)
 
     block_out = end.block_out
     if sz.per > 1:
         block_out = jnp.take(block_out, order, axis=1)
-    proj_bias = end.bias[3, : 3 * lanes].reshape(3, heads, HEAD_PAD)[:, :, :hd].reshape(3, local)
-    proj_bias = jnp.stack([proj_bias[0], proj_bias[2]])
-    table_grad = end.table.reshape(heads, 2 * grid_side, 2 * grid_side)
-    table_grad = table_grad[:, :offsets, :offsets].reshape(heads, offsets * offsets)
     return (
         block_out,
         end.patch,
         jnp.swapaxes(end.project.reshape(3, local, D), 1, 2),
-        proj_bias,
+        end.proj_bias,
         end.merge,
-        end.bias[2],
+        end.merge_bias,
         end.up.T,
-        end.bias[0, :F],
+        end.up_bias,
         end.down,
-        end.bias[1],
+        end.down_bias,
         end.modulate.T,
-        end.mod_bias[0, :cols],
-        table_grad,
+        end.mod_bias,
+        end.table,
     )
 
 

time: 219 us -> 205 us (0.936)
  local copies, waits for them, and re-layouts: 11.7 us -> 0 us
  other arithmetic: 2.59 us -> 0 us
    slice x8 -> x0, local copies, waits for them, and re-layouts: 5.68 us -> none  [the longest x1 1.43 us: body(): end.bias[1]]
    reshape x4 -> x0, local copies, waits for them, and re-layouts: 2.97 us -> none  [the longest x1 0.8 us: body(): table = bias_table.astype(F32).reshape(heads, offsets, offsets)]
where the time goes in v4:
time: 205 us
  Pallas kernels  204 us (100%)
    pallas_call x3, Pallas kernels, run(): pl.pallas_call(inner, out_shape=list(self.outs.values()), in_specs=self.s...  204 us

profile of v4, /device:TPU:0, one launch (start us, length us, event | category | flops | bytes accessed | tf_op | source)
XLA Modules:
  0.0 204.9 jit_solution(17333196260017216394)
XLA Ops:
  0.6 38.9 %attention_forward.1 = (f32[8,6912]{1,0:T(8,128)}, s32[8,192]{1,0:T(8,128)}, s32[8,192]{1,0:T(8,128)}, bf16[1536,1152]{1,0:T(8,128)(2,1)}, bf16[1536,768]{1,0:T(...) custom-call(bf16[8,1152]{1,0:T(8,128)(2,1)} %refs_0_.3, ...), custom_call_target="tpu_custom_call" | custom-call | tf_op jit(solution)/shard_map/attention_forward/pallas_call | solution.py:390
  39.6 150.6 %block_backward.1 = (bf16[2,864,1152]{2,1,0:T(8,128)(2,1)}, f32[4,4,1152]{2,1,0:T(4,128)}, f32[4,2,1024]{2,1,0:T(2,128)}, bf16[4,8,1152]{2,1,0:T(8,128)(2,1)}, f...) custom-call(bf16[8,1152]{1,0:T(8,128)(2,1)} %refs_0_.3, ...), custom_call_target="tpu_custom_call" | custom-call | tf_op jit(solution)/shard_map/block_backward/pallas_call | solution.py:390
  190.2 14.6 %write_results.1 = (f32[864]{0:T(1024)}, f32[576]{0:T(1024)}, f32[1152]{0:T(1024)}, f32[1152]{0:T(1024)}, f32[2,144]{1,0:T(2,128)}, /*index=5*/f32[2,961]{1,0:T(...) custom-call(f32[4,8,1024]{2,1,0:T(8,128)} %get-tuple-element.59.refs, ...), custom_call_target="tpu_custom_call" | custom-call | tf_op jit(solution)/shard_map/write_results/pallas_call | solution.py:390

commit v5 on v4

--- a/solution.py
+++ b/solution.py
@@ -72,14 +72,6 @@
 
 def my_index():
     return lax.axis_index("dp"), lax.axis_index("mp")
-
-
-def enter(sz):
-    dp, me = my_index()
-    barrier = pltpu.get_barrier_semaphore()
-    for d in range(1, sz.mp):
-        pl.semaphore_signal(barrier, inc=1, device_id=(dp, flip(me, d)), device_id_type=MESH)
-    pl.semaphore_wait(barrier, sz.mp - 1)
 
 
 def rows_of(ref, start, size):
@@ -353,6 +345,10 @@
     return dot(sel, ones, 0, 0)[:, 0:1]
 
 
+def stripe_of(rows):
+    return 96 if rows % 192 == 0 else rows // 2
+
+
 class Call:
     def __init__(self):
         self.args, self.specs, self.outs, self.out_specs, self.scratch_of = {}, [], {}, [], {}
@@ -412,8 +408,10 @@
     wide = mod_buf.shape[2]
     sem = r.sem
 
+    barrier = pltpu.get_barrier_semaphore()
+    for d in range(1, sz.mp):
+        pl.semaphore_signal(barrier, inc=1, device_id=(dp, flip(me, d)), device_id_type=MESH)
     load_mod = pltpu.make_async_copy(r.w_mod, r.w_mod_v, sem.at[0])
-    load_mod.start()
 
     def load_patches(i, slot):
         return pltpu.make_async_copy(r.patches.at[xor(mine, slot, sbits)], r.patches_v.at[slot], r.load_sem.at[i])
@@ -422,6 +420,7 @@
         load_patches(slot, slot).start()
         return carry
 
+    load_mod.start()
     lax.fori_loop(0, sz.samples, start_load, 0)
     slots = lax.broadcasted_iota(jnp.int32, (1, n), 1)
     for s in range(sz.samples):
@@ -436,26 +435,6 @@
     offsets = 2 * grid_side - 1
     r.table_v[:, 0 : offsets * offsets] = r.b_table[...].astype(F32)
     r.table_v[...] = spread(r.table_v[...], offsets, offsets, 1)
-    cond = r.condition[...].astype(F32)
-    signal = (cond / (1.0 + jnp.exp(-cond))).astype(BF16)
-    mod_buf[me] = jnp.zeros((sz.samples, wide), F32)
-    load_mod.wait()
-    mod_buf[me, :, 0:cols] = dot(signal, r.w_mod_v[...], 1, 1) + r.b_mod[...].astype(F32).reshape(1, cols)
-    enter(sz)
-
-    def mod_copy(d, slot):
-        return pltpu.make_async_remote_copy(
-            src_ref=mod_buf.at[slot],
-            dst_ref=mod_buf.at[slot],
-            send_sem=r.mod_send.at[d],
-            recv_sem=r.mod_recv.at[d],
-            device_id=(dp, flip(me, d)),
-            device_id_type=MESH,
-        )
-
-    for d in range(1, sz.mp):
-        mod_copy(d, me).start()
-
     w_qkv, w_merge = r.w_qkv_v, r.w_merge_v
     pad_rows = jnp.zeros((HEAD_PAD - hd, D), F32)
     for h in range(heads):
@@ -481,6 +460,26 @@
         for row in range(grid_side):
             rolled = pltpu.roll(strip, span - row * 2 * grid_side, 1) if row else strip
             bias_full[h, row * grid_side : (row + 1) * grid_side, :] = rolled[:, : 2 * L].astype(BF16)
+
+    cond = r.condition[...].astype(F32)
+    signal = (cond / (1.0 + jnp.exp(-cond))).astype(BF16)
+    mod_buf[me] = jnp.zeros((sz.samples, wide), F32)
+    load_mod.wait()
+    mod_buf[me, :, 0:cols] = dot(signal, r.w_mod_v[...], 1, 1) + r.b_mod[...].astype(F32).reshape(1, cols)
+    pl.semaphore_wait(barrier, sz.mp - 1)
+
+    def mod_copy(d, slot):
+        return pltpu.make_async_remote_copy(
+            src_ref=mod_buf.at[slot],
+            dst_ref=mod_buf.at[slot],
+            send_sem=r.mod_send.at[d],
+            recv_sem=r.mod_recv.at[d],
+            device_id=(dp, flip(me, d)),
+            device_id_type=MESH,
+        )
+
+    for d in range(1, sz.mp):
+        mod_copy(d, me).start()
 
     normed, kept_own = r.normed, r.kept_v
 
@@ -717,6 +716,7 @@
     grads = r.grads
     sem = r.sem
 
+    stripe = stripe_of(F)
     per_half, per_local = (F // 2 // chunk, local // chunk) if chunk else (0, 0)
     marks = [0, per_half, 2 * per_half, 2 * per_half + per_local, 2 * per_half + 2 * per_local]
     following = {(number, j): 0 for number in (1, 2, 3) for j in range(2)}
@@ -824,10 +824,10 @@
         at = pl.ds(slot * n, wide * n)
         v = dot(mlp[at, :], w_up[...], 1, 1) + r.bias_v[0:1, 0:F]
         square = v * v
-        t = jnp.tanh(GELU_C * (v + GELU_A * v * square))
-        active = (0.5 * v * (1.0 + t)).astype(BF16)
+        h = 0.5 * jnp.tanh(v * (GELU_C * GELU_A * square + GELU_C)) + 0.5
+        active = (v * h).astype(BF16)
         act[at, :] = active
-        slope[at, :] = 0.5 * (1.0 + t) + 0.5 * v * (1.0 - t * t) * (GELU_C * (1.0 + 3.0 * GELU_A * square))
+        slope[at, :] = h * (1.0 + (1.0 - h) * (v * (6.0 * GELU_C * GELU_A * square + 2.0 * GELU_C)))
         r.part_f[at, :] = dot(active, w_down[...]).astype(BF16)
 
     def output_grad(slot, carry):
@@ -874,21 +874,26 @@
         lax.fori_loop(0, sz.samples, output_grad, 0)
         slot_loop(sz, lambda slot: forward(slot, 1), fwd)
 
-    def wide_grad(left, right, base):
-        at = 0
+    def wide_grad(left, right, base, group):
+        at, sent = 0, 0
         while at < F:
             size = min(256, F - at)
             value = dot(left[:, at : at + size], right[...], 0, 0).astype(BF16)
-            cut = min(max(F // 2 - at, 0), size)
-            if cut:
-                grads[0, base + at : base + at + cut, :] = value[:cut]
-            if cut < size:
-                start = base + at + cut - F // 2
-                grads[1, start : start + size - cut, :] = value[cut:]
+            row = at
+            while row < at + size:
+                turn = row // stripe
+                count = min((turn + 1) * stripe, at + size) - row
+                to = base + turn // 2 * stripe + row % stripe
+                grads[turn % 2, to : to + count, :] = value[row - at : row - at + count]
+                row += count
             at += size
-
-    wide_grad(act, d_mlp, 0)
-    begin(0)
+            if line is not None:
+                ready = at // (2 * stripe) * (stripe // chunk)
+                if ready > sent:
+                    line.begin((0, 1), marks[group] + sent, marks[group] + ready)
+                    sent = ready
+
+    wide_grad(act, d_mlp, 0, 0)
 
     def backward(slot):
         at = pl.ds(slot * n, n)
@@ -898,9 +903,9 @@
         r.part_b[at, :] = dot(dpre, w_up[...]).astype(BF16)
 
     plan = {
-        4: [(1, 0, 1), (1, 1, 1)],
-        6: [(1, 1, 1), (2, 0, 1), (2, 1, 1)],
-        7: [(1, 0, 1)],
+        2: [(1, 1, 1)],
+        3: [(1, 0, 1)],
+        5: [(1, 0, 1), (1, 1, 1), (2, 0, 1), (2, 1, 1)],
     }
 
     def bwd_extra(i):
@@ -915,15 +920,14 @@
     slot_loop(sz, backward, bwd, bwd_extra)
     load_attn.start()
     load_att.start()
-    wide_grad(d_pre, mlp, F // 2)
-    begin(1)
-    tick((1, 1, 1), (2, 1, 1))
+    wide_grad(d_pre, mlp, F // 2, 1)
+    tick((1, 0, 1), (1, 1, 1), (2, 0, 1), (2, 1, 1))
     for copy in loads:
         copy.wait()
     normed2, inv2 = layer_stats(r.hidden_v[...])
     r.normed_v[...] = normed2
     bwd.close()
-    tick((1, 0, 1), (1, 1, 1), (2, 0, 1), (2, 1, 1), (3, 0, 1), (3, 1, 2))
+    tick((1, 0, 1), (1, 1, 1), (2, 0, 1), (2, 1, 1), (3, 0, 1), (3, 1, 1))
 
     mrow = pl.ds(mine, 1)
     live = live_column(pick_rows(r.pos, mine, L)[:, :block])
@@ -934,7 +938,6 @@
     r.dh_v[...] = dh
     r.d_attn[:block, :] = (modv[mrow, 2 * D : 3 * D] * dh).astype(BF16)
     gat_d.start()
-    tick((1, 0, 1))
 
     early, late_sums = r.early, r.late_sums
     early[me, 0:1, :] = jnp.sum(dh * r.res_v[...], axis=0, keepdims=True)
@@ -1003,13 +1006,13 @@
         r.part_b[at, :] = dot(joined, w_qkv[...]).astype(BF16)
 
     if sz.fast:
-        plan_one = {1: [(2, 0, 1), (2, 1, 1)], 2: [(1, 0, 1), (1, 1, 1), (3, 0, 1), (3, 1, 1)]}
+        plan_one = {1: [(1, 0, 1), (1, 1, 1), (2, 0, 1), (2, 1, 1), (3, 0, 1), (3, 1, 1)], 2: [(3, 0, 1), (3, 1, 1)]}
         plan_two = {
-            3: [(1, 0, 1), (1, 1, 1), (2, 0, 2), (2, 1, 1), (3, 0, 1)],
-            4: [(1, 0, 1), (1, 1, 1), (3, 1, 1)],
-            5: [(1, 1, 1), (2, 0, 1), (2, 1, 1), (3, 0, 1)],
-            6: [(1, 0, 1), (2, 0, 1), (3, 0, 1), (3, 1, 1)],
-            7: [(1, 0, 1), (1, 1, 1), (2, 1, 1), (3, 1, 1)],
+            3: [(1, 1, 1), (2, 0, 1), (2, 1, 1), (3, 0, 1), (3, 1, 1)],
+            4: [(1, 0, 1), (2, 0, 1), (2, 1, 1)],
+            5: [(1, 0, 1), (1, 1, 1), (2, 1, 1), (3, 0, 1), (3, 1, 1)],
+            6: [(1, 1, 1), (2, 0, 1), (3, 0, 1), (3, 1, 1)],
+            7: [(1, 0, 1), (2, 0, 1), (2, 1, 1)],
         }
 
         def one(i, carry):
@@ -1027,13 +1030,13 @@
             @pl.when(i == 2)
             def _():
                 gat_d.step(0)
-                tick((2, 0, 1), (3, 0, 1))
+                tick((1, 0, 1), (1, 1, 1), (2, 0, 1), (2, 1, 1))
                 gat_d.step(1)
                 fwd.take(1, *sz.sends[1, 0][1])
                 fwd.take(0, *sz.sends[0, 0][1])
                 fwd.send(1, 2)
                 fwd.send(0, 4)
-                tick((1, 0, 1), (1, 1, 1), (2, 1, 1), (3, 1, 1))
+                tick((1, 0, 1), (1, 1, 1), (3, 0, 1), (3, 1, 1))
                 for h in range(2):
                     gat_d.near_copy(2, h).wait()
 
@@ -1080,7 +1083,7 @@
             return carry
 
         lax.fori_loop(0, 8, one, 0)
-        tick((1, 1, 1), (2, 0, 1), (2, 1, 1), (3, 0, 1))
+        tick((1, 0, 1), (1, 1, 1), (2, 1, 1), (3, 0, 1), (3, 1, 1))
     else:
         for t in range(len(gat_d.stages)):
             gat_d.step(t)
@@ -1092,14 +1095,14 @@
     load_att.wait()
     attention_grad(3, 1, F)
     begin(2, 1)
-    tick((1, 0, 1), (2, 0, 1))
+    tick((2, 0, 1))
     attention_grad(0, 0, F)
     begin(2, 0)
     attention_grad(2, 1, F + local)
     begin(3, 1)
     attention_grad(1, 0, F + local)
     begin(3, 0)
-    tick((1, 1, 1), (2, 1, 1), (3, 0, 1), (3, 1, 1))
+    tick((1, 0, 1), (1, 1, 1), (2, 1, 1), (3, 0, 1), (3, 1, 1))
 
     tables = r.table_g
     span = tables.shape[2]
@@ -1125,14 +1128,14 @@
     normed1, inv1 = layer_stats(r.res_v[...])
     r.normed_v[...] = normed1
     last.close()
-    tick((1, 0, 1), (1, 1, 1), (2, 0, 1), (2, 1, 1), (3, 1, 1))
+    tick((1, 1, 2), (2, 0, 1), (3, 0, 1), (3, 1, 1))
     d_in = last.own_sum()
     g = d_in * (1.0 + modv[mrow, D : 2 * D])
     mlp[:block, :] = (r.dh_v[...] + layer_back(g, r.normed_v[...], inv1)).astype(BF16)
     late_sums[me, 0:1, :] = jnp.sum(d_in, axis=0, keepdims=True)
     late_sums[me, 1:2, :] = jnp.sum(d_in * r.normed_v[...], axis=0, keepdims=True)
     gat_k.start()
-    tick((1, 1, 2), (3, 0, 1), (3, 1, 1))
+    tick((1, 1, 1), (2, 0, 1), (2, 1, 1))
 
     def out_copy(slot):
         return pltpu.make_async_copy(
@@ -1167,16 +1170,16 @@
         dm_copy(early, 0, d, me).start()
         dm_copy(late_sums, 1, d, me).start()
     gat_o.start()
-    tick((2, 0, 1), (2, 1, 2), (3, 0, 1), (3, 1, 1))
+    tick((1, 0, 1), (2, 1, 1), (3, 0, 1), (3, 1, 2))
     gat_k.step(1)
-    tick((1, 0, 2), (1, 1, 1), (3, 0, 1), (3, 1, 1))
+    tick((1, 0, 2), (1, 1, 1), (2, 0, 1), (2, 1, 2))
     if sz.fast:
         for d in (2, 4):
             for h in range(2):
                 gat_k.near_copy(d, h).wait()
         lax.fori_loop(2, 6, patch, 0)
         gat_k.step(2)
-        tick((1, 0, 1), (1, 1, 1), (2, 0, 1), (2, 1, 2), (3, 1, 1))
+        tick((1, 1, 2), (2, 0, 1), (2, 1, 1), (3, 0, 1), (3, 1, 1))
         for h in range(2):
             gat_k.near_copy(6, h).wait()
         lax.fori_loop(6, 8, patch, 0)
@@ -1202,20 +1205,19 @@
     base = pl.multiple_of(me * cols // 128 * 128, 128)
     mod_g[dp] = flat[:, pl.ds(base, mod_g.shape[2])]
     share(2)
-    tick((1, 1, 1), (2, 0, 1), (2, 1, 1), (3, 0, 1))
-    tick((2, 0, 1), (2, 1, 1))
+    tick((3, 0, 1), (3, 1, 1))
+    tick((1, 0, 1), (2, 1, 1), (2, 0, 1))
     gat_o.step(0)
-    tick((1, 0, 1), (3, 1, 1), (3, 0, 1), (1, 0, 1))
-    tick((3, 1, 1), (2, 1, 1))
+    tick((1, 0, 1), (3, 0, 1), (3, 1, 1), (1, 0, 1))
+    tick((2, 1, 1), (3, 1, 1))
     gat_o.step(1)
-    tick((1, 0, 1), (3, 1, 1), (3, 0, 1), (3, 1, 1))
-    tick((3, 0, 1), (2, 0, 1))
+    tick((3, 0, 1), (2, 0, 1), (3, 1, 1), (3, 0, 1))
+    tick((2, 0, 1))
     for t in range(2, len(gat_o.stages)):
         gat_o.step(t)
     gat_o.finish()
     lax.fori_loop(0, sz.samples, start_out, 0)
     tick((2, 0, 1), (3, 0, 1), (3, 1, 1), (3, 0, 1))
-    tick((2, 0, 1), (3, 0, 1))
     if line is not None:
         assert all(k == marks[4] for k in following.values()), following
     for k in range(4):
@@ -1258,9 +1260,10 @@
             jobs.append((total.at[half, pl.ds(start, size)], to.at[pl.ds(at, size)], size))
             start, at, count = start + size, at + size, count - size
 
-    for half in range(2):
-        add(half, 0, r.down, half * (F // 2), F // 2)
-        add(half, F // 2, r.up, half * (F // 2), F // 2)
+    stripe = stripe_of(F)
+    for turn in range(F // stripe):
+        add(turn % 2, turn // 2 * stripe, r.down, turn * stripe, stripe)
+        add(turn % 2, F // 2 + turn // 2 * stripe, r.up, turn * stripe, stripe)
     add(0, F, r.project, 0, 2 * local)
     add(1, F + local, r.project, 2 * local, local)
     add(1, F, r.merge, 0, local)
@@ -1278,29 +1281,31 @@
     for s in range(samples):
         out_in(s).start()
 
-    members, _, width = r.mod_g.shape
-    shift = lax.rem(lax.axis_index("mp") * cols, 128)
-    dmod = jnp.concatenate([r.mod_g[m] for m in range(members)], axis=0)
-    dmod = pltpu.roll(dmod, lax.rem(width - shift, width), 1)
-    upper = dmod.astype(BF16)
-    parts = jnp.concatenate([upper, (dmod - upper.astype(F32)).astype(BF16)], axis=0)
-    signal = jnp.concatenate([r.signal_g[m].astype(F32) for m in range(members)], axis=0).astype(BF16)
-    r.mod_v[...] = dot(parts, jnp.concatenate([signal, signal], axis=0), 0, 0)[:cols]
-    modulate = pltpu.make_async_copy(r.mod_v, r.modulate, r.sem.at[0])
-    modulate.start()
-    r.mod_bias[...] = jnp.sum(dmod, axis=0, keepdims=True)[:, :cols].reshape(cols)
-    bias, table = r.bias_g[0], r.table_g[0]
-    for m in range(1, members):
-        bias, table = bias + r.bias_g[m], table + r.table_g[m]
-    r.up_bias[...] = bias[0:1, :F].reshape(F)
-    r.down_bias[...] = bias[1:2].reshape(D)
-    r.merge_bias[...] = bias[2:3].reshape(D)
-    lanes = heads * HEAD_PAD
-    for k, c in enumerate((0, 2)):
-        row = spread(bias[3:4, c * lanes : (c + 1) * lanes], heads, hd, hd - HEAD_PAD)
-        r.proj_bias[k : k + 1, :] = row[:, : heads * hd]
-    offsets = 2 * grid_side - 1
-    r.table[...] = spread(table, offsets, offsets, -1)[:, : offsets * offsets]
+    def small_results():
+        members, _, width = r.mod_g.shape
+        shift = lax.rem(lax.axis_index("mp") * cols, 128)
+        dmod = jnp.concatenate([r.mod_g[m] for m in range(members)], axis=0)
+        dmod = pltpu.roll(dmod, lax.rem(width - shift, width), 1)
+        upper = dmod.astype(BF16)
+        parts = jnp.concatenate([upper, (dmod - upper.astype(F32)).astype(BF16)], axis=0)
+        signal = jnp.concatenate([r.signal_g[m].astype(F32) for m in range(members)], axis=0).astype(BF16)
+        r.mod_v[...] = dot(parts, jnp.concatenate([signal, signal], axis=0), 0, 0)[:cols]
+        modulate = pltpu.make_async_copy(r.mod_v, r.modulate, r.sem.at[0])
+        modulate.start()
+        r.mod_bias[...] = jnp.sum(dmod, axis=0, keepdims=True)[:, :cols].reshape(cols)
+        bias, table = r.bias_g[0], r.table_g[0]
+        for m in range(1, members):
+            bias, table = bias + r.bias_g[m], table + r.table_g[m]
+        r.up_bias[...] = bias[0:1, :F].reshape(F)
+        r.down_bias[...] = bias[1:2].reshape(D)
+        r.merge_bias[...] = bias[2:3].reshape(D)
+        lanes = heads * HEAD_PAD
+        for k, c in enumerate((0, 2)):
+            row = spread(bias[3:4, c * lanes : (c + 1) * lanes], heads, hd, hd - HEAD_PAD)
+            r.proj_bias[k : k + 1, :] = row[:, : heads * hd]
+        offsets = 2 * grid_side - 1
+        r.table[...] = spread(table, offsets, offsets, -1)[:, : offsets * offsets]
+        return modulate
 
     for k, (_, _, size) in enumerate(jobs):
         load(k).wait()
@@ -1313,6 +1318,8 @@
         if k < samples:
             out_in(k).wait()
             out_back(k).start()
+        if k == depth:
+            modulate = small_results()
     for k in range(max(0, len(jobs) - depth), len(jobs)):
         save(k).wait()
     for s in range(samples):
@@ -1539,7 +1546,7 @@
         merge=((local, D), F32),
         modulate=((cols, D), F32),
     )
-    depth = 4
+    depth = 8
     three.vmem(narrow=((depth, 288, D), BF16), wide=((depth, 288, D), F32), mod_v=((cols, D), F32), out_v=((samples, n, D), BF16))
     three.scratch(sem=dma((1,)), out_sem=dma((2, samples)), load_sem=dma((depth,)), save_sem=dma((depth,)))
     end = three.run(functools.partial(write_results, heads, hd, grid_side, cols), "write_results", None, 63 << 20)

time: 205 us -> 199 us (0.971)
  Pallas kernels: 204 us -> 198 us
    pallas_call x3, Pallas kernels: 204 us -> 198 us  [run(): pl.pallas_call(inner, out_shape=list(self.outs.values()), in_specs=self.s...]
where the time goes in v5:
time: 199 us
  Pallas kernels  198 us (99%)
    pallas_call x3, Pallas kernels, run(): pl.pallas_call(inner, out_shape=list(self.outs.values()), in_specs=self.s...  198 us

profile of v5, /device:TPU:0, one launch (start us, length us, event | category | flops | bytes accessed | tf_op | source)
XLA Modules:
  0.0 198.9 jit_solution(781861261893963538)
XLA Ops:
  0.6 36.7 %attention_forward.1 = (f32[8,6912]{1,0:T(8,128)}, s32[8,192]{1,0:T(8,128)}, s32[8,192]{1,0:T(8,128)}, bf16[1536,1152]{1,0:T(8,128)(2,1)}, bf16[1536,768]{1,0:T(...) custom-call(bf16[8,1152]{1,0:T(8,128)(2,1)} %refs_0_.3, ...), custom_call_target="tpu_custom_call" | custom-call | tf_op jit(solution)/shard_map/attention_forward/pallas_call | solution.py:386
  37.4 147.2 %block_backward.1 = (bf16[2,864,1152]{2,1,0:T(8,128)(2,1)}, f32[4,4,1152]{2,1,0:T(4,128)}, f32[4,2,1024]{2,1,0:T(2,128)}, bf16[4,8,1152]{2,1,0:T(8,128)(2,1)}, f...) custom-call(bf16[8,1152]{1,0:T(8,128)(2,1)} %refs_0_.3, ...), custom_call_target="tpu_custom_call" | custom-call | tf_op jit(solution)/shard_map/block_backward/pallas_call | solution.py:386
  184.5 14.1 %write_results.1 = (f32[864]{0:T(1024)}, f32[576]{0:T(1024)}, f32[1152]{0:T(1024)}, f32[1152]{0:T(1024)}, f32[2,144]{1,0:T(2,128)}, /*index=5*/f32[2,961]{1,0:T(...) custom-call(f32[4,8,1024]{2,1,0:T(8,128)} %get-tuple-element.59.refs, ...), custom_call_target="tpu_custom_call" | custom-call | tf_op jit(solution)/shard_map/write_results/pallas_call | solution.py:386

commit v6 on v5

--- a/solution.py
+++ b/solution.py
@@ -1205,19 +1205,17 @@
     base = pl.multiple_of(me * cols // 128 * 128, 128)
     mod_g[dp] = flat[:, pl.ds(base, mod_g.shape[2])]
     share(2)
-    tick((3, 0, 1), (3, 1, 1))
-    tick((1, 0, 1), (2, 1, 1), (2, 0, 1))
+    tick((1, 0, 2), (2, 0, 1), (3, 0, 1), (3, 1, 1), (1, 0, 1))
     gat_o.step(0)
-    tick((1, 0, 1), (3, 0, 1), (3, 1, 1), (1, 0, 1))
-    tick((2, 1, 1), (3, 1, 1))
+    tick((2, 0, 1), (2, 1, 1), (2, 0, 1), (3, 1, 1), (3, 0, 1))
+    tick((2, 0, 1), (2, 1, 1), (3, 1, 1), (3, 0, 1))
     gat_o.step(1)
-    tick((3, 0, 1), (2, 0, 1), (3, 1, 1), (3, 0, 1))
-    tick((2, 0, 1))
+    tick((3, 0, 1), (3, 1, 1), (3, 0, 1))
     for t in range(2, len(gat_o.stages)):
         gat_o.step(t)
     gat_o.finish()
     lax.fori_loop(0, sz.samples, start_out, 0)
-    tick((2, 0, 1), (3, 0, 1), (3, 1, 1), (3, 0, 1))
+    tick((3, 1, 1), (3, 0, 1))
     if line is not None:
         assert all(k == marks[4] for k in following.values()), following
     for k in range(4):

time: 199 us -> 197 us (0.990)
  Pallas kernels: 198 us -> 195 us
    pallas_call x3, Pallas kernels: 198 us -> 195 us  [run(): pl.pallas_call(inner, out_shape=list(self.outs.values()), in_specs=self.s...]
where the time goes in v6:
time: 197 us; the launch traced here: 196 us
  Pallas kernels  195 us (99%)
    pallas_call x3, Pallas kernels, run(): pl.pallas_call(inner, out_shape=list(self.outs.values()), in_specs=self.s...  195 us

profile of v6, /device:TPU:0, one launch (start us, length us, event | category | flops | bytes accessed | tf_op | source)
XLA Modules:
  0.0 196.3 jit_solution(15812994806670870038)
XLA Ops:
  0.6 36.7 %attention_forward.1 = (f32[8,6912]{1,0:T(8,128)}, s32[8,192]{1,0:T(8,128)}, s32[8,192]{1,0:T(8,128)}, bf16[1536,1152]{1,0:T(8,128)(2,1)}, bf16[1536,768]{1,0:T(...) custom-call(bf16[8,1152]{1,0:T(8,128)(2,1)} %refs_0_.3, ...), custom_call_target="tpu_custom_call" | custom-call | tf_op jit(solution)/shard_map/attention_forward/pallas_call | solution.py:386
  37.4 144.6 %block_backward.1 = (bf16[2,864,1152]{2,1,0:T(8,128)(2,1)}, f32[4,4,1152]{2,1,0:T(4,128)}, f32[4,2,1024]{2,1,0:T(2,128)}, bf16[4,8,1152]{2,1,0:T(8,128)(2,1)}, f...) custom-call(bf16[8,1152]{1,0:T(8,128)(2,1)} %refs_0_.3, ...), custom_call_target="tpu_custom_call" | custom-call | tf_op jit(solution)/shard_map/block_backward/pallas_call | solution.py:386
  182.0 14.1 %write_results.1 = (f32[864]{0:T(1024)}, f32[576]{0:T(1024)}, f32[1152]{0:T(1024)}, f32[1152]{0:T(1024)}, f32[2,144]{1,0:T(2,128)}, /*index=5*/f32[2,961]{1,0:T(...) custom-call(f32[4,8,1024]{2,1,0:T(8,128)} %get-tuple-element.59.refs, ...), custom_call_target="tpu_custom_call" | custom-call | tf_op jit(solution)/shard_map/write_results/pallas_call | solution.py:386

commit v7 on v6

--- a/solution.py
+++ b/solution.py
@@ -1177,9 +1177,12 @@
         for d in (2, 4):
             for h in range(2):
                 gat_k.near_copy(d, h).wait()
-        lax.fori_loop(2, 6, patch, 0)
+        lax.fori_loop(2, 4, patch, 0)
+        tick((1, 1, 1), (2, 0, 1))
+        lax.fori_loop(4, 6, patch, 0)
+        tick((1, 1, 1))
         gat_k.step(2)
-        tick((1, 1, 2), (2, 0, 1), (2, 1, 1), (3, 0, 1), (3, 1, 1))
+        tick((2, 1, 1), (3, 0, 1), (3, 1, 1))
         for h in range(2):
             gat_k.near_copy(6, h).wait()
         lax.fori_loop(6, 8, patch, 0)

time: 197 us -> 197 us (level)
  no operation moved by 1% of the time
where the time goes in v7:
time: 197 us; the launch traced here: 196 us
  Pallas kernels  195 us (99%)
    pallas_call x3, Pallas kernels, run(): pl.pallas_call(inner, out_shape=list(self.outs.values()), in_specs=self.s...  195 us

profile of v7, /device:TPU:0, one launch (start us, length us, event | category | flops | bytes accessed | tf_op | source)
XLA Modules:
  0.0 196.3 jit_solution(40565989543772873)
XLA Ops:
  0.6 36.7 %attention_forward.1 = (f32[8,6912]{1,0:T(8,128)}, s32[8,192]{1,0:T(8,128)}, s32[8,192]{1,0:T(8,128)}, bf16[1536,1152]{1,0:T(8,128)(2,1)}, bf16[1536,768]{1,0:T(...) custom-call(bf16[8,1152]{1,0:T(8,128)(2,1)} %refs_0_.3, ...), custom_call_target="tpu_custom_call" | custom-call | tf_op jit(solution)/shard_map/attention_forward/pallas_call | solution.py:386
  37.4 144.6 %block_backward.1 = (bf16[2,864,1152]{2,1,0:T(8,128)(2,1)}, f32[4,4,1152]{2,1,0:T(4,128)}, f32[4,2,1024]{2,1,0:T(2,128)}, bf16[4,8,1152]{2,1,0:T(8,128)(2,1)}, f...) custom-call(bf16[8,1152]{1,0:T(8,128)(2,1)} %refs_0_.3, ...), custom_call_target="tpu_custom_call" | custom-call | tf_op jit(solution)/shard_map/block_backward/pallas_call | solution.py:386
  182.0 14.1 %write_results.1 = (f32[864]{0:T(1024)}, f32[576]{0:T(1024)}, f32[1152]{0:T(1024)}, f32[1152]{0:T(1024)}, f32[2,144]{1,0:T(2,128)}, /*index=5*/f32[2,961]{1,0:T(...) custom-call(f32[4,8,1024]{2,1,0:T(8,128)} %get-tuple-element.59.refs, ...), custom_call_target="tpu_custom_call" | custom-call | tf_op jit(solution)/shard_map/write_results/pallas_call | solution.py:386
